TPU v7x, 32 devices: a whole 2x2x4 slice. The times are simulated.
32 devices in a mesh: section: 2 (over core), ctx: 4 (over y, x), wt: 4 (over z).
Axes of the slice: x: 2, y: 2, z: 4, core: 2. Of those that a mesh axis runs over, the one named last changes fastest.
Arguments:
- layer_input: bfloat16 [2, 1024, 2048], P(None, 'ctx'), may hold values from -6 to 6
- cotangent: bfloat16 [2, 1024, 2048], P(None, 'ctx'), may hold values from -6 to 6
- seq_lengths: int32 [2], replicated, may hold values from 256 to 1024, as said below
- adapter_ids: int32 [2], replicated, may hold values from 0 to 7
- mixer_gain: bfloat16 [2, 2048], P('section'), may hold values from 0.5 to 1.5
- feed_gain: bfloat16 [2, 2048], P('section'), may hold values from 0.5 to 1.5
- decay_rate: float32 [2, 48], P('section', 'wt'), may hold values from 0.05859375 to 20
- step_bias: float32 [2, 48], P('section', 'wt'), may hold values from -5.5 to -3.5
- skip_gain: float32 [2, 48], P('section', 'wt'), may hold values from 0.5 to 1.5
- query_weight: bfloat16 [2, 2048, 1024], P('section', None, 'wt'), may hold values from -0.125 to 0.125
- mamba_weight: bfloat16 [2, 2048, 2, 3072], P('section', None, None, 'wt'), may hold values from -0.125 to 0.125
- shared_weight: bfloat16 [2, 2048, 1072], P('section'), may hold values from -0.125 to 0.125
- attnout_weight: bfloat16 [2, 1024, 2048], P('section', 'wt'), may hold values from -3 to 3
- mambaout_weight: bfloat16 [2, 3072, 2048], P('section', 'wt'), may hold values from -0.109375 to 0.109375
- gateup_weight: bfloat16 [2, 2048, 2, 4096], P('section', None, None, 'wt'), may hold values from -0.125 to 0.125
- down_weight: bfloat16 [2, 4096, 2048], P('section', 'wt'), may hold values from -0.09375 to 0.09375
- mixin_down: bfloat16 [2, 8, 16, 2048], P('section'), may hold values from -0.125 to 0.125
- query_up: bfloat16 [2, 8, 16, 1024], P('section', None, None, 'wt'), may hold values from -0.59765625 to 0.59765625
- mamba_up: bfloat16 [2, 8, 16, 2, 3072], P('section', None, None, None, 'wt'), may hold values from -0.59765625 to 0.59765625
- shared_up: bfloat16 [2, 8, 16, 1072], P('section'), may hold values from -0.59765625 to 0.59765625
- attnout_down: bfloat16 [2, 8, 16, 1024], P('section', None, None, 'wt'), may hold values from -1.1953125 to 1.1953125
- mambaout_down: bfloat16 [2, 8, 16, 3072], P('section', None, None, 'wt'), may hold values from -0.109375 to 0.109375
- mixout_up: bfloat16 [2, 8, 16, 2048], P('section'), may hold values from -0.59765625 to 0.59765625
- feedin_down: bfloat16 [2, 8, 16, 2048], P('section'), may hold values from -0.125 to 0.125
- feedin_up: bfloat16 [2, 8, 16, 2, 4096], P('section', None, None, None, 'wt'), may hold values from -0.59765625 to 0.59765625
- feedout_down: bfloat16 [2, 8, 16, 4096], P('section', None, None, 'wt'), may hold values from -0.09375 to 0.09375
- feedout_up: bfloat16 [2, 8, 16, 2048], P('section'), may hold values from -0.59765625 to 0.59765625
Outputs:
- section_out: bfloat16 [2, 2, 1024, 2048], P('section', None, 'ctx')
- section_grad: bfloat16 [2, 2, 1024, 2048], P('section', None, 'ctx')
- grad_mixin_down: float32 [2, 8, 16, 2048], P('section')
- grad_query_up: float32 [2, 8, 16, 1024], P('section', None, None, 'wt')
- grad_mamba_up: float32 [2, 8, 16, 2, 3072], P('section', None, None, None, 'wt')
- grad_shared_up: float32 [2, 8, 16, 1072], P('section')
- grad_attnout_down: float32 [2, 8, 16, 1024], P('section', None, None, 'wt')
- grad_mambaout_down: float32 [2, 8, 16, 3072], P('section', None, None, 'wt')
- grad_mixout_up: float32 [2, 8, 16, 2048], P('section')
- grad_feedin_down: float32 [2, 8, 16, 2048], P('section')
- grad_feedin_up: float32 [2, 8, 16, 2, 4096], P('section', None, None, None, 'wt')
- grad_feedout_down: float32 [2, 8, 16, 4096], P('section', None, None, 'wt')
- grad_feedout_up: float32 [2, 8, 16, 2048], P('section')
Inputs may be any that keep to these rules, and one draw needn't show every extreme that they name: Micro-batch m holds one sequence at positions 0 to seq_lengths[m] - 1 of its 1024 positions; the rest is padding. In every draw some micro-batch fills its whole slot.
All inputs are finite; a program needn't handle non-finite values.
Results may differ from a plain program's by a relative error of at most 0.035.
Values may be sent and summed in bfloat16 or wider, within the bound.
No kernel may reach another device: no remote copies, remote signals or barrier semaphores. Data moves between devices by JAX's collectives and lax.ppermute only.
A program may use at most 320 MiB of HBM per device.

v0:
```python
import jax
import jax.numpy as jnp
from jax import lax
from jax.sharding import PartitionSpec as P

D = 2048
QHEADS = 8
KVHEADS = 2
HEAD = 128
MHEADS = 48
MHEAD = 64
NSTATE = 256
RANK = 16
SCAN_BLOCK = 64
KEY_BLOCK = 256


epsilon = 1e-05
rope_base = 10000.0
masked_score = -1e30


def shifted(value, axis, steps):
    count = lax.axis_size(axis)
    first, last = (max(0, -steps), min(count, count - steps))
    return lax.ppermute(value, axis, [(source, source + steps) for source in range(first, last)])


def low_dot(first_operand, second_operand):
    return jnp.dot(first_operand, second_operand, preferred_element_type=jnp.float32)


def high_dot(first_operand, second_operand):
    return jnp.dot(
        first_operand,
        second_operand,
        precision=lax.Precision.HIGHEST,
        preferred_element_type=jnp.float32,
    )


def against(first_operand, second_operand):
    return lax.dot_general(
        first_operand, second_operand, (((1,), (1,)), ((), ())), preferred_element_type=jnp.float32
    )


def high_against(first_operand, second_operand):
    return lax.dot_general(
        first_operand,
        second_operand,
        (((1,), (1,)), ((), ())),
        precision=lax.Precision.HIGHEST,
        preferred_element_type=jnp.float32,
    )


def plain_outer(first_operand, second_operand):
    return lax.dot_general(
        first_operand, second_operand, (((0,), (0,)), ((), ())), preferred_element_type=jnp.float32
    )


def high_outer(first_operand, second_operand):
    return lax.dot_general(
        first_operand,
        second_operand,
        (((0,), (0,)), ((), ())),
        precision=lax.Precision.HIGHEST,
        preferred_element_type=jnp.float32,
    )


def rms_scale(vector):
    return lax.rsqrt(jnp.mean(vector * vector, axis=-1, keepdims=True) + epsilon)


def norm_back(vector, grad_normed, gain_vec):
    scale_now = rms_scale(vector)
    weighted = grad_normed * gain_vec
    return weighted * scale_now - vector * scale_now**3 * jnp.mean(
        weighted * vector, axis=-1, keepdims=True
    )


def rotate(head_values, positions, direction):
    half_width = head_values.shape[-1] // 2
    frequencies = rope_base ** (-jnp.arange(half_width, dtype=jnp.float32) / half_width)
    angles = positions.astype(jnp.float32)[:, None] * frequencies[None, :]
    cosine = jnp.cos(angles)[:, None, :]
    sine_part = direction * jnp.sin(angles)[:, None, :]
    first_half = head_values[..., :half_width]
    second_half = head_values[..., half_width:]
    return jnp.concatenate(
        [
            first_half * cosine - second_half * sine_part,
            second_half * cosine + first_half * sine_part,
        ],
        axis=-1,
    )


def scan_states(ssm_inputs, input_map, output_map, step_sizes, logdecay, state_start):
    block_count = ssm_inputs.shape[0] // SCAN_BLOCK
    pieces = (
        ssm_inputs.reshape(block_count, SCAN_BLOCK, ssm_inputs.shape[1], ssm_inputs.shape[2]),
        input_map.reshape(block_count, SCAN_BLOCK, -1),
        output_map.reshape(block_count, SCAN_BLOCK, -1),
        step_sizes.reshape(block_count, SCAN_BLOCK, -1),
        logdecay.reshape(block_count, SCAN_BLOCK, -1),
    )
    causal = jnp.arange(SCAN_BLOCK)[:, None] >= jnp.arange(SCAN_BLOCK)[None, :]

    def scan_block_step(state_now, block_parts):
        block_inputs, block_in_map, block_out_map, block_steps, block_decay = block_parts
        cumulative = jnp.cumsum(block_decay, axis=0)
        gram_matrix = high_dot(block_out_map, block_in_map.T)
        differences = cumulative[:, None, :] - cumulative[None, :, :]
        decay_mask = jnp.where(causal[:, :, None], jnp.exp(jnp.minimum(differences, 0.0)), 0.0)
        weights = gram_matrix[:, :, None] * decay_mask * block_steps[None, :, :]
        within = jnp.einsum("ijh,jhp->ihp", weights, block_inputs, precision=lax.Precision.HIGHEST)
        carried = jnp.exp(cumulative)[:, :, None] * jnp.einsum(
            "in,hnp->ihp", block_out_map, state_now, precision=lax.Precision.HIGHEST
        )
        tail_weight = jnp.exp(cumulative[-1][None, :] - cumulative) * block_steps
        new_state = jnp.exp(cumulative[-1])[:, None, None] * state_now + jnp.einsum(
            "jh,jn,jhp->hnp",
            tail_weight,
            block_in_map,
            block_inputs,
            precision=lax.Precision.HIGHEST,
        )
        return (new_state, within + carried)

    final_state, outputs = lax.scan(jax.checkpoint(scan_block_step), state_start, pieces)
    return (outputs.reshape(ssm_inputs.shape), final_state)


def start_state_grad(grad_joined, output_map, logdecay):
    block_count = grad_joined.shape[0] // SCAN_BLOCK
    pieces = (
        grad_joined.reshape(block_count, SCAN_BLOCK, grad_joined.shape[1], grad_joined.shape[2]),
        output_map.reshape(block_count, SCAN_BLOCK, -1),
        logdecay.reshape(block_count, SCAN_BLOCK, -1),
    )

    def start_block_step(carry, block_parts):
        offset, summed = carry
        block_grad, block_out_map, block_decay = block_parts
        cumulative = offset[None, :] + jnp.cumsum(block_decay, axis=0)
        summed = summed + jnp.einsum(
            "ih,in,ihp->hnp",
            jnp.exp(cumulative),
            block_out_map,
            block_grad,
            precision=lax.Precision.HIGHEST,
        )
        return ((cumulative[-1], summed), None)

    start = (
        jnp.zeros((grad_joined.shape[1],), jnp.float32),
        jnp.zeros((grad_joined.shape[1], output_map.shape[1], grad_joined.shape[2]), jnp.float32),
    )
    (unused, summed), nothing = lax.scan(start_block_step, start, pieces)
    return summed


def chain_states(total_decay, state_values, reverse):
    direction = -1 if reverse else 1

    def relay_step(turn_index, state_carry):
        return shifted(
            (jnp.exp(total_decay)[:, None, None] * state_carry + state_values).astype(jnp.bfloat16),
            "ctx",
            direction,
        ).astype(jnp.float32)

    return lax.fori_loop(0, lax.axis_size("ctx") - 1, relay_step, jnp.zeros_like(state_values))


def mamba_apply(
    step_raw,
    ssm_inputs,
    gate_raw,
    input_map,
    output_map,
    state_start,
    step_bias,
    decay_rate,
    skip_gain,
    live_mask,
):
    step_sizes = jax.nn.softplus(step_raw + step_bias) * live_mask[:, None]
    logdecay = -decay_rate * step_sizes
    scanned, final_state = scan_states(
        ssm_inputs, input_map, output_map, step_sizes, logdecay, state_start
    )
    joined = (scanned + skip_gain[None, :, None] * ssm_inputs).reshape(ssm_inputs.shape[0], -1)
    return (joined * jax.nn.silu(gate_raw), final_state)


def mixer_front(layer_entry, fixed_params, selected_adapter):
    layer_float = layer_entry.astype(jnp.float32)
    normed = (layer_float * rms_scale(layer_float) * fixed_params[0]).astype(jnp.bfloat16)
    small_in = against(normed, selected_adapter[0])
    query_proj = low_dot(normed, fixed_params[5]) + high_dot(
        small_in, selected_adapter[1].astype(jnp.float32)
    )
    mamba_proj = low_dot(normed, fixed_params[6].reshape(D, -1)) + high_dot(
        small_in, selected_adapter[2].reshape(RANK, -1).astype(jnp.float32)
    )
    shared = low_dot(normed, fixed_params[7]) + high_dot(
        small_in, selected_adapter[3].astype(jnp.float32)
    )
    return (layer_float, normed, small_in, query_proj, mamba_proj, shared)


def attention_inputs(query_proj, shared, positions, wt_index):
    span_len = query_proj.shape[0]
    local_heads = query_proj.shape[1] // HEAD
    key_head = wt_index * local_heads // (QHEADS // KVHEADS)
    queries = rotate(query_proj.reshape(span_len, local_heads, HEAD), positions, 1.0).astype(
        jnp.bfloat16
    )
    key_part = lax.dynamic_slice_in_dim(shared, key_head * HEAD, HEAD, 1)
    value_part = lax.dynamic_slice_in_dim(shared, (KVHEADS + key_head) * HEAD, HEAD, 1)
    key_rotated = rotate(key_part[:, None, :], positions, 1.0)[:, 0]
    key_value = jnp.concatenate([key_rotated, value_part], axis=1).astype(jnp.bfloat16)
    return (queries.reshape(span_len * local_heads, HEAD), key_value, key_head)


def split_ssm(mamba_proj, shared, wt_index):
    span_len = mamba_proj.shape[0]
    half_width = mamba_proj.shape[1] // 2
    local_mheads = half_width // MHEAD
    offset = 2 * KVHEADS * HEAD
    gate_raw = mamba_proj[:, :half_width]
    ssm_inputs = mamba_proj[:, half_width:].reshape(span_len, local_mheads, MHEAD)
    input_map = shared[:, offset : offset + NSTATE]
    output_map = shared[:, offset + NSTATE : offset + 2 * NSTATE]
    step_raw = lax.dynamic_slice_in_dim(
        shared, offset + 2 * NSTATE + wt_index * local_mheads, local_mheads, 1
    )
    return (gate_raw, ssm_inputs, input_map, output_map, step_raw)


def visible_blocks(span_len, ctx_index, length):
    last_query = (ctx_index + 1) * span_len
    return jnp.minimum(
        (last_query + KEY_BLOCK - 1) // KEY_BLOCK, (length + KEY_BLOCK - 1) // KEY_BLOCK
    )


def block_scores(query_rows, key_all, block_start, query_pos, length):
    key_block = lax.dynamic_slice_in_dim(key_all, block_start, KEY_BLOCK, 0)
    keys_part = key_block[:, :HEAD]
    values_part = key_block[:, HEAD:]
    scores = HEAD ** (-0.5) * against(query_rows, keys_part)
    key_pos = block_start + jnp.arange(KEY_BLOCK, dtype=jnp.int32)
    allowed = (key_pos[None, :] <= query_pos[:, None]) & (key_pos[None, :] < length)
    return (scores, allowed, keys_part, values_part)


def attend_forward(query_rows, key_all, query_pos, length, blocks):
    row_count = query_rows.shape[0]

    def measure(block_index, running_total):
        running_max, running_sum = running_total
        scores, allowed, keys_part, values_part = block_scores(
            query_rows, key_all, block_index * KEY_BLOCK, query_pos, length
        )
        updated_max = jnp.maximum(
            running_max, jnp.max(jnp.where(allowed, scores, masked_score), axis=1)
        )
        fresh = jnp.sum(jnp.where(allowed, jnp.exp(scores - updated_max[:, None]), 0.0), axis=1)
        return (updated_max, running_sum * jnp.exp(running_max - updated_max) + fresh)

    start_max = jnp.full((row_count,), masked_score, jnp.float32)
    running_max, running_sum = lax.fori_loop(
        0, blocks, measure, (start_max, jnp.zeros((row_count,), jnp.float32))
    )
    logsum = running_max + jnp.log(running_sum)

    def collect(block_index, summed):
        scores, allowed, keys_part, values_part = block_scores(
            query_rows, key_all, block_index * KEY_BLOCK, query_pos, length
        )
        probabilities = jnp.where(allowed, jnp.exp(scores - logsum[:, None]), 0.0)
        return summed + low_dot(probabilities.astype(jnp.bfloat16), values_part)

    attended = lax.fori_loop(0, blocks, collect, jnp.zeros((row_count, HEAD), jnp.float32))
    return (attended, logsum)


def attend_backward(
    query_rows, key_all, query_pos, length, blocks, logsum, attended, grad_rows_low
):
    row_delta = jnp.sum(grad_rows_low.astype(jnp.float32) * attended, axis=1)

    def sweep(block_index, running_total):
        grad_query, grad_keyval = running_total
        block_start = block_index * KEY_BLOCK
        scores, allowed, keys_part, values_part = block_scores(
            query_rows, key_all, block_start, query_pos, length
        )
        probabilities = jnp.where(allowed, jnp.exp(scores - logsum[:, None]), 0.0)
        grad_prob = against(grad_rows_low, values_part)
        grad_score = (probabilities * (grad_prob - row_delta[:, None])).astype(jnp.bfloat16)
        grad_query = grad_query + HEAD ** (-0.5) * low_dot(grad_score, keys_part)
        grad_key = HEAD ** (-0.5) * plain_outer(grad_score, query_rows)
        grad_value = plain_outer(probabilities.astype(jnp.bfloat16), grad_rows_low)
        grad_keyval = lax.dynamic_update_slice_in_dim(
            grad_keyval, jnp.concatenate([grad_key, grad_value], axis=1), block_start, 0
        )
        return (grad_query, grad_keyval)

    start_query = jnp.zeros((query_rows.shape[0], HEAD), jnp.float32)
    start_keyval = jnp.zeros((key_all.shape[0], 2 * HEAD), jnp.float32)
    return lax.fori_loop(0, blocks, sweep, (start_query, start_keyval))


def feed_front(hidden, fixed_params, selected_adapter):
    feed_normed = (hidden * rms_scale(hidden) * fixed_params[1]).astype(jnp.bfloat16)
    small_feed = against(feed_normed, selected_adapter[7])
    gateup = low_dot(feed_normed, fixed_params[10].reshape(D, -1)) + high_dot(
        small_feed, selected_adapter[8].reshape(RANK, -1).astype(jnp.float32)
    )
    half_width = gateup.shape[1] // 2
    gate_value = gateup[:, :half_width]
    up_value = gateup[:, half_width:]
    inner_low = (jax.nn.silu(gate_value) * up_value).astype(jnp.bfloat16)
    small_out = against(inner_low, selected_adapter[9])
    return (feed_normed, small_feed, gate_value, up_value, inner_low, small_out)


def layer_forward(layer_entry, fixed_params, selected_adapter, adapter_placement):
    positions, live_mask, length, wt_index, ctx_index = adapter_placement
    span_len = layer_entry.shape[0]
    layer_float, normed, small_in, query_proj, mamba_proj, shared = mixer_front(
        layer_entry, fixed_params, selected_adapter
    )
    query_rows, key_value, key_head = attention_inputs(query_proj, shared, positions, wt_index)
    key_all = lax.all_gather(key_value, "ctx", axis=0, tiled=True)
    local_heads = query_rows.shape[0] // span_len
    query_pos = jnp.repeat(positions, local_heads)
    blocks = visible_blocks(span_len, ctx_index, length)
    attended, logsum = attend_forward(query_rows, key_all, query_pos, length, blocks)
    gate_raw, ssm_inputs, input_map, output_map, step_raw = split_ssm(mamba_proj, shared, wt_index)
    step_sizes = jax.nn.softplus(step_raw + fixed_params[3]) * live_mask[:, None]
    logdecay = -fixed_params[2] * step_sizes
    zero_state = jnp.zeros((ssm_inputs.shape[1], NSTATE, MHEAD), jnp.float32)
    scanned_local, state_local = scan_states(
        ssm_inputs, input_map, output_map, step_sizes, logdecay, zero_state
    )
    state_in = chain_states(jnp.sum(logdecay, axis=0), state_local, False)
    running_decay = jnp.cumsum(logdecay, axis=0)
    carried = jnp.exp(running_decay)[:, :, None] * jnp.einsum(
        "tn,hnp->thp", output_map, state_in, precision=lax.Precision.HIGHEST
    )
    joined = (scanned_local + carried + fixed_params[4][None, :, None] * ssm_inputs).reshape(
        span_len, -1
    )
    gated_out = joined * jax.nn.silu(gate_raw)
    attended_low = attended.reshape(span_len, -1).astype(jnp.bfloat16)
    gated_low = gated_out.astype(jnp.bfloat16)
    small_mid = against(attended_low, selected_adapter[4]) + against(gated_low, selected_adapter[5])
    part_sum = (
        low_dot(attended_low, fixed_params[8])
        + low_dot(gated_low, fixed_params[9])
        + high_dot(small_mid, selected_adapter[6].astype(jnp.float32))
    )
    mixed_out = lax.psum(part_sum.astype(jnp.bfloat16), "wt").astype(jnp.float32)
    hidden = layer_float + live_mask[:, None] * mixed_out
    feed_normed, small_feed, gate_value, up_value, inner_low, small_out = feed_front(
        hidden, fixed_params, selected_adapter
    )
    feed_part = low_dot(inner_low, fixed_params[11]) + high_dot(
        small_out, selected_adapter[10].astype(jnp.float32)
    )
    feed_out = lax.psum(feed_part.astype(jnp.bfloat16), "wt").astype(jnp.float32)
    return (hidden + feed_out, (key_all, state_in, hidden, attended, logsum))


def hybrid_layer_backward(
    layer_entry, grad_layer_output, fixed_params, selected_adapter, adapter_placement, saved_state
):
    positions, live_mask, length, wt_index, ctx_index = adapter_placement
    key_all, state_in, hidden, attended, logsum = saved_state
    span_len = layer_entry.shape[0]
    feed_normed, small_feed, gate_value, up_value, inner_low, small_out = feed_front(
        hidden, fixed_params, selected_adapter
    )
    grad_feed_low = grad_layer_output.astype(jnp.bfloat16)
    grad_feed = grad_feed_low.astype(jnp.float32)
    grad_small_out = high_against(grad_feed, selected_adapter[10].astype(jnp.float32))
    grad_feedout_up = high_outer(small_out, grad_feed)
    grad_feedout_down = high_outer(grad_small_out, inner_low.astype(jnp.float32))
    grad_inner = against(grad_feed_low, fixed_params[11]) + high_dot(
        grad_small_out, selected_adapter[9].astype(jnp.float32)
    )
    sigmoid_gate = jax.nn.sigmoid(gate_value)
    grad_gate = grad_inner * up_value * sigmoid_gate * (1.0 + gate_value * (1.0 - sigmoid_gate))
    grad_up = grad_inner * gate_value * sigmoid_gate
    grad_gateup_low = jnp.concatenate([grad_gate, grad_up], axis=1).astype(jnp.bfloat16)
    grad_gateup = grad_gateup_low.astype(jnp.float32)
    grad_small_feed = high_against(
        grad_gateup, selected_adapter[8].reshape(RANK, -1).astype(jnp.float32)
    )
    grad_feedin_up = high_outer(small_feed, grad_gateup).reshape(RANK, 2, -1)
    grad_feedin_down = high_outer(grad_small_feed, feed_normed.astype(jnp.float32))
    feed_norm_part = against(grad_gateup_low, fixed_params[10].reshape(D, -1)) + high_dot(
        grad_small_feed, selected_adapter[7].astype(jnp.float32)
    )
    grad_feed_normed = lax.psum(feed_norm_part.astype(jnp.bfloat16), "wt").astype(jnp.float32)
    grad_hidden = grad_layer_output + norm_back(hidden, grad_feed_normed, fixed_params[1])
    layer_float, normed, small_in, query_proj, mamba_proj, shared = mixer_front(
        layer_entry, fixed_params, selected_adapter
    )
    query_rows, key_value, key_head = attention_inputs(query_proj, shared, positions, wt_index)
    local_heads = query_rows.shape[0] // span_len
    query_pos = jnp.repeat(positions, local_heads)
    blocks = visible_blocks(span_len, ctx_index, length)
    gate_raw, ssm_inputs, input_map, output_map, step_raw = split_ssm(mamba_proj, shared, wt_index)
    local_mheads = ssm_inputs.shape[1]

    def ssm_function(raw_steps, ssm_values, gate_values, map_in, map_out, state_start):
        return mamba_apply(
            raw_steps,
            ssm_values,
            gate_values,
            map_in,
            map_out,
            state_start,
            fixed_params[3],
            fixed_params[2],
            fixed_params[4],
            live_mask,
        )

    (gated_out, final_state), pullback = jax.vjp(
        ssm_function, step_raw, ssm_inputs, gate_raw, input_map, output_map, state_in
    )
    grad_mixed_low = (grad_hidden * live_mask[:, None]).astype(jnp.bfloat16)
    grad_mixed = grad_mixed_low.astype(jnp.float32)
    attended_low = attended.reshape(span_len, -1).astype(jnp.bfloat16)
    gated_low = gated_out.astype(jnp.bfloat16)
    grad_small_mid = high_against(grad_mixed, selected_adapter[6].astype(jnp.float32))
    small_mid = against(attended_low, selected_adapter[4]) + against(gated_low, selected_adapter[5])
    grad_mixout_up = high_outer(small_mid, grad_mixed)
    grad_attnout_down = high_outer(grad_small_mid, attended_low.astype(jnp.float32))
    grad_mambaout_down = high_outer(grad_small_mid, gated_low.astype(jnp.float32))
    grad_attended_low = (
        against(grad_mixed_low, fixed_params[8])
        + high_dot(grad_small_mid, selected_adapter[4].astype(jnp.float32))
    ).astype(jnp.bfloat16)
    grad_gated = against(grad_mixed_low, fixed_params[9]) + high_dot(
        grad_small_mid, selected_adapter[5].astype(jnp.float32)
    )
    grad_query_rows, grad_keyval = attend_backward(
        query_rows,
        key_all,
        query_pos,
        length,
        blocks,
        logsum,
        attended,
        grad_attended_low.reshape(-1, HEAD),
    )
    own_grads = lax.psum_scatter(
        grad_keyval.astype(jnp.bfloat16), "ctx", scatter_dimension=0, tiled=True
    ).astype(jnp.float32)
    step_sizes = jax.nn.softplus(step_raw + fixed_params[3]) * live_mask[:, None]
    logdecay = -fixed_params[2] * step_sizes
    grad_joined = (grad_gated * jax.nn.silu(gate_raw)).reshape(span_len, local_mheads, MHEAD)
    grad_state_local = start_state_grad(grad_joined, output_map, logdecay)
    grad_state_out = chain_states(jnp.sum(logdecay, axis=0), grad_state_local, True)
    grad_step, grad_inputs, grad_gates, grad_map_in, grad_map_out, unused = pullback(
        (grad_gated, grad_state_out)
    )
    grad_queries = rotate(
        grad_query_rows.reshape(span_len, local_heads, HEAD), positions, -1.0
    ).reshape(span_len, -1)
    grad_keys = rotate(own_grads[:, None, :HEAD], positions, -1.0)[:, 0]
    keyval_grad = jnp.zeros((span_len, 2 * KVHEADS * HEAD), jnp.float32)
    keyval_grad = lax.dynamic_update_slice_in_dim(keyval_grad, grad_keys, key_head * HEAD, 1)
    keyval_grad = lax.dynamic_update_slice_in_dim(
        keyval_grad, own_grads[:, HEAD:], (KVHEADS + key_head) * HEAD, 1
    )
    step_grad = lax.dynamic_update_slice_in_dim(
        jnp.zeros((span_len, MHEADS), jnp.float32), grad_step, wt_index * local_mheads, 1
    )
    grad_shared = jnp.concatenate([keyval_grad, grad_map_in, grad_map_out, step_grad], axis=1)
    shared_total = lax.psum(grad_shared.astype(jnp.bfloat16), "wt").astype(jnp.float32)
    share_width = shared_total.shape[1] // lax.axis_size("wt")
    share_low = lax.dynamic_slice_in_dim(
        shared_total, wt_index * share_width, share_width, 1
    ).astype(jnp.bfloat16)
    share_round = share_low.astype(jnp.float32)
    weight_share = lax.dynamic_slice_in_dim(fixed_params[7], wt_index * share_width, share_width, 1)
    up_share = lax.dynamic_slice_in_dim(
        selected_adapter[3], wt_index * share_width, share_width, 1
    ).astype(jnp.float32)
    grad_query_low = grad_queries.astype(jnp.bfloat16)
    grad_query_round = grad_query_low.astype(jnp.float32)
    grad_mamba_low = jnp.concatenate(
        [grad_gates, grad_inputs.reshape(span_len, -1)], axis=1
    ).astype(jnp.bfloat16)
    grad_mamba_round = grad_mamba_low.astype(jnp.float32)
    grad_small_in = (
        high_against(grad_query_round, selected_adapter[1].astype(jnp.float32))
        + high_against(grad_mamba_round, selected_adapter[2].reshape(RANK, -1).astype(jnp.float32))
        + high_against(share_round, up_share)
    )
    grad_query_up = high_outer(small_in, grad_query_round)
    grad_mamba_up = high_outer(small_in, grad_mamba_round).reshape(RANK, 2, -1)
    grad_shared_up = lax.dynamic_update_slice_in_dim(
        jnp.zeros((RANK, shared.shape[1]), jnp.float32),
        high_outer(small_in, share_round),
        wt_index * share_width,
        1,
    )
    mixer_norm_part = (
        against(grad_query_low, fixed_params[5])
        + against(grad_mamba_low, fixed_params[6].reshape(D, -1))
        + against(share_low, weight_share)
        + high_dot(grad_small_in, selected_adapter[0].astype(jnp.float32))
    )
    grad_mixin_down = high_outer(grad_small_in, normed.astype(jnp.float32))
    grad_normed = lax.psum(mixer_norm_part.astype(jnp.bfloat16), "wt").astype(jnp.float32)
    grad_layer_input = grad_hidden + norm_back(layer_float, grad_normed, fixed_params[0])
    return (
        grad_layer_input,
        (
            grad_mixin_down,
            grad_query_up,
            grad_mamba_up,
            grad_shared_up,
            grad_attnout_down,
            grad_mambaout_down,
            grad_mixout_up,
            grad_feedin_down,
            grad_feedin_up,
            grad_feedout_down,
            grad_feedout_up,
        ),
    )


def store_slot(buffer, new_value, chosen, active):
    previous = lax.dynamic_index_in_dim(buffer, chosen, 0, keepdims=False)
    return lax.dynamic_update_index_in_dim(
        buffer, jnp.where(active, new_value, previous), chosen, 0
    )


def pick_adapter(adapters, adapter):
    return tuple((lax.dynamic_index_in_dim(item, adapter, 0, keepdims=False) for item in adapters))


def shards(
    layer_input,
    cotangent,
    seq_lengths,
    adapter_ids,
    mixer_gain,
    feed_gain,
    decay_rate,
    step_bias,
    skip_gain,
    query_weight,
    mamba_weight,
    shared_weight,
    attnout_weight,
    mambaout_weight,
    gateup_weight,
    down_weight,
    mixin_down,
    query_up,
    mamba_up,
    shared_up,
    attnout_down,
    mambaout_down,
    mixout_up,
    feedin_down,
    feedin_up,
    feedout_down,
    feedout_up,
):
    fixed_params = tuple(
        (
            item[0]
            for item in (
                mixer_gain,
                feed_gain,
                decay_rate,
                step_bias,
                skip_gain,
                query_weight,
                mamba_weight,
                shared_weight,
                attnout_weight,
                mambaout_weight,
                gateup_weight,
                down_weight,
            )
        )
    )
    adapters = tuple(
        (
            item[0]
            for item in (
                mixin_down,
                query_up,
                mamba_up,
                shared_up,
                attnout_down,
                mambaout_down,
                mixout_up,
                feedin_down,
                feedin_up,
                feedout_down,
                feedout_up,
            )
        )
    )
    section_index = lax.axis_index("section")
    ctx_index = lax.axis_index("ctx")
    wt_index = lax.axis_index("wt")
    micro_count = layer_input.shape[0]
    span_len = layer_input.shape[1]
    local_heads = fixed_params[5].shape[1] // HEAD
    local_mheads = fixed_params[2].shape[0]
    slot_len = span_len * lax.axis_size("ctx")
    positions = ctx_index * span_len + jnp.arange(span_len, dtype=jnp.int32)
    key_buffer = jnp.zeros((micro_count, slot_len, 2 * HEAD), jnp.bfloat16)
    state_buffer = jnp.zeros((micro_count, local_mheads, NSTATE, MHEAD), jnp.float32)
    hidden_buffer = jnp.zeros((micro_count, span_len, D), jnp.float32)
    attended_buffer = jnp.zeros((micro_count, span_len * local_heads, HEAD), jnp.float32)
    logsum_buffer = jnp.zeros((micro_count, span_len * local_heads), jnp.float32)
    input_buffer = jnp.zeros((micro_count, span_len, D), jnp.bfloat16)
    output_buffer = jnp.zeros((micro_count, span_len, D), jnp.bfloat16)
    received = jnp.zeros((span_len, D), jnp.bfloat16)
    for round_index in range(micro_count + 1):
        micro_index = round_index - section_index
        chosen = jnp.clip(micro_index, 0, micro_count - 1)
        active = (micro_index >= 0) & (micro_index < micro_count)
        layer_entry = jnp.where(
            section_index == 0, layer_input[min(round_index, micro_count - 1)], received
        )
        length = seq_lengths[chosen]
        selected_adapter = pick_adapter(adapters, adapter_ids[chosen])
        adapter_placement = (
            positions,
            (positions < length).astype(jnp.float32),
            length,
            wt_index,
            ctx_index,
        )
        result, saved_state = layer_forward(
            layer_entry, fixed_params, selected_adapter, adapter_placement
        )
        result_low = result.astype(jnp.bfloat16)
        output_buffer = store_slot(output_buffer, result_low, chosen, active)
        input_buffer = store_slot(input_buffer, layer_entry, chosen, active)
        key_buffer = store_slot(key_buffer, saved_state[0], chosen, active)
        state_buffer = store_slot(state_buffer, saved_state[1], chosen, active)
        hidden_buffer = store_slot(hidden_buffer, saved_state[2], chosen, active)
        attended_buffer = store_slot(attended_buffer, saved_state[3], chosen, active)
        logsum_buffer = store_slot(logsum_buffer, saved_state[4], chosen, active)
        if round_index < micro_count:
            received = shifted(result_low, "section", 1)
    partial_sums = tuple((jnp.zeros(item.shape, jnp.float32) for item in adapters))
    gradient_buffer = jnp.zeros((micro_count, span_len, D), jnp.bfloat16)
    returned = jnp.zeros((span_len, D), jnp.bfloat16)
    for round_index in range(micro_count + 1):
        micro_index = round_index - (1 - section_index)
        chosen = jnp.clip(micro_index, 0, micro_count - 1)
        active = (micro_index >= 0) & (micro_index < micro_count)
        grad_layer_output = jnp.where(
            section_index == 1, cotangent[min(round_index, micro_count - 1)], returned
        ).astype(jnp.float32)
        length = seq_lengths[chosen]
        adapter = adapter_ids[chosen]
        selected_adapter = pick_adapter(adapters, adapter)
        adapter_placement = (
            positions,
            (positions < length).astype(jnp.float32),
            length,
            wt_index,
            ctx_index,
        )
        saved_state = tuple(
            (
                lax.dynamic_index_in_dim(buffer, chosen, 0, keepdims=False)
                for buffer in (
                    key_buffer,
                    state_buffer,
                    hidden_buffer,
                    attended_buffer,
                    logsum_buffer,
                )
            )
        )
        layer_entry = lax.dynamic_index_in_dim(input_buffer, chosen, 0, keepdims=False)
        grad_layer_input, term_values = hybrid_layer_backward(
            layer_entry,
            grad_layer_output,
            fixed_params,
            selected_adapter,
            adapter_placement,
            saved_state,
        )
        partial_sums = tuple(
            (
                running_total.at[adapter].add(jnp.where(active, term_value, 0.0))
                for running_total, term_value in zip(partial_sums, term_values)
            )
        )
        grad_low = grad_layer_input.astype(jnp.bfloat16)
        gradient_buffer = store_slot(gradient_buffer, grad_low, chosen, active)
        if round_index < micro_count:
            returned = shifted(grad_low, "section", -1)
    shared_set = lax.psum(
        (partial_sums[0], partial_sums[3], partial_sums[6], partial_sums[7], partial_sums[10]),
        ("ctx", "wt"),
    )
    local_set = (
        lax.psum(partial_sums[1].astype(jnp.bfloat16), "ctx").astype(jnp.float32),
        lax.psum(partial_sums[2].astype(jnp.bfloat16), "ctx").astype(jnp.float32),
        lax.psum(partial_sums[4].astype(jnp.bfloat16), "ctx").astype(jnp.float32),
        lax.psum(partial_sums[5].astype(jnp.bfloat16), "ctx").astype(jnp.float32),
        lax.psum(partial_sums[8].astype(jnp.bfloat16), "ctx").astype(jnp.float32),
        lax.psum(partial_sums[9].astype(jnp.bfloat16), "ctx").astype(jnp.float32),
    )
    return (
        output_buffer[None],
        gradient_buffer[None],
        shared_set[0][None],
        local_set[0][None],
        local_set[1][None],
        shared_set[1][None],
        local_set[2][None],
        local_set[3][None],
        shared_set[2][None],
        shared_set[3][None],
        local_set[4][None],
        local_set[5][None],
        shared_set[4][None],
    )


def solution(mesh):
    in_specs = (
        P(None, "ctx", None),
        P(None, "ctx", None),
        P(),
        P(),
        P("section", None),
        P("section", None),
        P("section", "wt"),
        P("section", "wt"),
        P("section", "wt"),
        P("section", None, "wt"),
        P("section", None, None, "wt"),
        P("section", None, None),
        P("section", "wt", None),
        P("section", "wt", None),
        P("section", None, None, "wt"),
        P("section", "wt", None),
        P("section", None, None, None),
        P("section", None, None, "wt"),
        P("section", None, None, None, "wt"),
        P("section", None, None, None),
        P("section", None, None, "wt"),
        P("section", None, None, "wt"),
        P("section", None, None, None),
        P("section", None, None, None),
        P("section", None, None, None, "wt"),
        P("section", None, None, "wt"),
        P("section", None, None, None),
    )
    out_specs = (
        P("section", None, "ctx", None),
        P("section", None, "ctx", None),
        P("section", None, None, None),
        P("section", None, None, "wt"),
        P("section", None, None, None, "wt"),
        P("section", None, None, None),
        P("section", None, None, "wt"),
        P("section", None, None, "wt"),
        P("section", None, None, None),
        P("section", None, None, None),
        P("section", None, None, None, "wt"),
        P("section", None, None, "wt"),
        P("section", None, None, None),
    )
    return jax.shard_map(shards, mesh=mesh, in_specs=in_specs, out_specs=out_specs, check_vma=False)
```

profile of v0, /device:TPU:0, one launch (start us, length us, event | category | flops | bytes accessed | tf_op | source)
XLA Modules:
  0.0 3488.8 jit_solution(16278684055541321418)
XLA Ops:
  61.0 96.6 %while.438 = (s32[]{:T(128)}, f32[12,256,64]{1,2,0:T(8,128)}, f32[4,64,12,64]{1,0,3,2:T(4,128)}, f32[4,64,12]{2,1,0:T(8,128)}, f32[4,64,12]{2,1,0:T(8,128)}, /*i...) while((s32[]{:T(128)}, f32[12,256,64]{1,2,0:T(8,128)}, ...), condition=%wide.region_9.10_spmd.clone, body=%wide.region_7.9_spmd.clone.sunk | while | flops 353555200 | bytes 4747716 | solution.py:135
  158.3 46.6 %while.439 = (s32[]{:T(128)}, f32[12,256,64]{1,2,0:T(8,128)}, f32[12,1,1]{0,2,1:T(1,128)S(1)}, f32[12,256,64]{1,2,0:T(8,128)}, s32[]{:T(128)}, /*index=5*/s32[]{:T(128)}) while((s32[]{:T(128)}, f32[12,256,64]{1,2,0:T(8,128)}, f32[12,1,1]{0,2,1:T(1,128)S(1)}, f32[12,256,64]{1,2,0:T(8,128)}, s32[]{:T(128)}, ...), condition=%wide.region_14.15_spmd.clone, body=%wide.region_13.14_spmd.clone.sunk | while | flops 983043 | bytes 4718759 | solution.py:178
  223.6 16.5 all_gather.9
  292.5 42.6 %all-reduce.26.cloned.1.call-done = bf16[256,2048]{1,0:T(8,128)(2,1)} async-done(((bf16[256,2048]{1,0:T(8,128)(2,1)}), bf16[256,2048]{1,0:T(8,128)(2,1)}) %all-reduce.26.cloned.1.call-update) | async-done | bytes 1048592 | tf_op jit(solution)/shard_map/psum | solution.py:372
  378.5 26.6 all-reduce.28.cloned.1.call-done
  452.6 99.0 %while.440 = (s32[]{:T(128)}, f32[12,256,64]{1,2,0:T(8,128)}, f32[4,64,12,64]{1,0,3,2:T(4,128)}, f32[4,64,12]{2,1,0:T(8,128)}, f32[4,64,12]{2,1,0:T(8,128)}, /*i...) while((s32[]{:T(128)}, f32[12,256,64]{1,2,0:T(8,128)}, ...), condition=%wide.region_27.28_spmd.clone, body=%wide.region_25.27_spmd.clone.sunk | while | flops 353555200 | bytes 4727236 | solution.py:135
  552.9 43.7 %while.441 = (s32[]{:T(128)}, f32[12,256,64]{1,2,0:T(8,128)}, f32[12,1,1]{0,2,1:T(1,128)}, f32[12,256,64]{1,2,0:T(8,128)}, s32[]{:T(128)}, /*index=5*/s32[]{:T(128)}) while((s32[]{:T(128)}, f32[12,256,64]{1,2,0:T(8,128)}, f32[12,1,1]{0,2,1:T(1,128)}, f32[12,256,64]{1,2,0:T(8,128)}, s32[]{:T(128)}, /*index=5*/s32[]{:T(128)}) %tuple.1042), condition=%wide.region_32.33_spmd.clone, body=%wide.region_31.32_spmd.clone.sunk | while | flops 983043 | bytes 4718759 | solution.py:178
  616.8 16.5 all_gather.10
  659.2 54.5 %all-reduce.30.cloned.1.call-done = bf16[256,2048]{1,0:T(8,128)(2,1)} async-done(((bf16[256,2048]{1,0:T(8,128)(2,1)}), bf16[256,2048]{1,0:T(8,128)(2,1)}) %all-reduce.30.cloned.1.call-update) | async-done | bytes 1048592 | tf_op jit(solution)/shard_map/psum | solution.py:372
  742.2 40.2 %all-reduce.32.cloned.1.call-done = bf16[256,2048]{1,0:T(8,128)(2,1)} async-done(((bf16[256,2048]{1,0:T(8,128)(2,1)}), bf16[256,2048]{1,0:T(8,128)(2,1)}) %all-reduce.32.cloned.1.call-update) | async-done | bytes 1048592 | tf_op jit(solution)/shard_map/psum | solution.py:380
  884.0 97.0 %while.442 = (s32[]{:T(128)}, f32[12,256,64]{1,2,0:T(8,128)}, f32[4,64,12,64]{1,0,3,2:T(4,128)}, f32[4,64,12]{2,1,0:T(8,128)}, f32[4,64,12]{2,1,0:T(8,128)}, /*i...) while((s32[]{:T(128)}, f32[12,256,64]{1,2,0:T(8,128)}, ...), condition=%wide.region_45.46_spmd.clone, body=%wide.region_43.45_spmd.clone.sunk | while | flops 353555200 | bytes 4747716 | solution.py:135
  981.6 43.7 %while.443 = (s32[]{:T(128)}, f32[12,256,64]{1,2,0:T(8,128)}, f32[12,1,1]{0,2,1:T(1,128)S(1)}, f32[12,256,64]{1,2,0:T(8,128)}, s32[]{:T(128)}, /*index=5*/s32[]{:T(128)}) while((s32[]{:T(128)}, f32[12,256,64]{1,2,0:T(8,128)}, f32[12,1,1]{0,2,1:T(1,128)S(1)}, f32[12,256,64]{1,2,0:T(8,128)}, s32[]{:T(128)}, ...), condition=%wide.region_50.51_spmd.clone, body=%wide.region_49.50_spmd.clone.sunk | while | flops 983043 | bytes 4718759 | solution.py:178
  1047.4 16.5 all_gather.11
  1105.7 76.3 %while.430 = (s32[]{:T(128)}, f32[12,256,64]{1,2,0:T(8,128)}, f32[4,64,12,64]{1,3,2,0:T(8,128)}, f32[4,12,256,64]{2,3,1,0:T(8,128)}, f32[4,64,12]{2,1,0:T(8,128)...) while((s32[]{:T(128)}, f32[12,256,64]{1,2,0:T(8,128)}, ...), condition=%wide.region_63.65_spmd.clone, body=%wide.region_61.64_spmd.clone.sunk | while | flops 353157888 | bytes 6104513 | solution.py:135
  1205.7 76.2 %while.433 = (s32[]{:T(128)}, f32[12,256,64]{1,2,0:T(8,128)}, f32[4,64,12,64]{1,3,2,0:T(8,128)}, f32[4,12,256,64]{2,3,1,0:T(8,128)}, f32[4,64,12]{2,1,0:T(8,128)...) while((s32[]{:T(128)}, f32[12,256,64]{1,2,0:T(8,128)}, ...), condition=%wide.region_94.96_spmd.clone, body=%wide.region_92.95_spmd.clone.sunk | while | flops 353157888 | bytes 6104513 | solution.py:135
  1299.1 78.8 %while.436 = (s32[]{:T(128)}, f32[12,256,64]{1,2,0:T(8,128)}, f32[4,64,12,64]{1,3,2,0:T(8,128)}, f32[4,12,256,64]{2,3,1,0:T(8,128)}, f32[4,64,12]{2,1,0:T(8,128)...) while((s32[]{:T(128)}, f32[12,256,64]{1,2,0:T(8,128)}, ...), condition=%wide.region_125.127_spmd.clone, body=%wide.region_123.126_spmd.clone.sunk | while | flops 353157888 | bytes 13968889 | solution.py:135
  1463.6 45.8 %all-reduce.36.cloned.1.call-done = bf16[256,2048]{1,0:T(8,128)(2,1)} async-done(((bf16[256,2048]{1,0:T(8,128)(2,1)}), bf16[256,2048]{1,0:T(8,128)(2,1)}) %all-reduce.36.cloned.1.call-update) | async-done | bytes 1048592 | tf_op jit(solution)/shard_map/psum | solution.py:414
  1528.4 15.4 while.444
  1543.8 48.0 %while.445 = (s32[]{:T(128)}, f32[12,256,64]{1,2,0:T(8,128)}, f32[12,1,1]{0,2,1:T(1,128)}, f32[12,256,64]{1,2,0:T(8,128)}, s32[]{:T(128)}, /*index=5*/s32[]{:T(128)}) while((s32[]{:T(128)}, f32[12,256,64]{1,2,0:T(8,128)}, f32[12,1,1]{0,2,1:T(1,128)}, f32[12,256,64]{1,2,0:T(8,128)}, s32[]{:T(128)}, /*index=5*/s32[]{:T(128)}) %tuple.1063), condition=%wide.region_69.71_spmd.clone, body=%wide.region_68.70_spmd.clone.sunk | while | flops 983043 | bytes 4718759 | solution.py:178
  1546.4 11.7 collective-permute-done.3
  1562.8 11.4 collective-permute-done.3
  1595.8 222.8 %while.431 = (s32[]{:T(128)}, f32[12,256,64]{1,2,0:T(8,128)}, f32[4,64,12,64]{3,1,2,0:T(8,128)}, bf16[4,64,256]{2,1,0:T(8,128)(2,1)}, bf16[4,64,256]{2,1,0:T(8,1...) while((s32[]{:T(128)}, f32[12,256,64]{1,2,0:T(8,128)}, ...), condition=%wide.region_80.82_spmd.clone, body=%wide.region_70.81_spmd.clone.sunk | while | flops 870767360 | bytes 17563604 | solution.py:135
  1833.2 11.6 while.429
  1883.0 22.3 reduce-scatter.4.cloned.1.call-done
  1917.2 39.1 %all-reduce.38.cloned.1.call-done = bf16[256,1072]{0,1:T(8,128)(2,1)} async-done(((bf16[256,1072]{0,1:T(8,128)(2,1)}), bf16[256,1072]{0,1:T(8,128)(2,1)}) %all-reduce.38.cloned.1.call-update) | async-done | bytes 548880 | tf_op jit(solution)/shard_map/psum | solution.py:493
  1976.2 39.9 %all-reduce.40.cloned.1.call-done = bf16[256,2048]{1,0:T(8,128)(2,1)} async-done(((bf16[256,2048]{1,0:T(8,128)(2,1)}), bf16[256,2048]{1,0:T(8,128)(2,1)}) %all-reduce.40.cloned.1.call-update) | async-done | bytes 1048592 | tf_op jit(solution)/shard_map/psum | solution.py:529
  2069.6 36.2 %all-reduce.42.cloned.1.call-done = bf16[256,2048]{1,0:T(8,128)(2,1)} async-done(((bf16[256,2048]{1,0:T(8,128)(2,1)}), bf16[256,2048]{1,0:T(8,128)(2,1)}) %all-reduce.42.cloned.1.call-update) | async-done | bytes 1048592 | tf_op jit(solution)/shard_map/psum | solution.py:414
  2123.8 15.3 while.446
  2139.1 48.0 %while.447 = (s32[]{:T(128)}, f32[12,256,64]{1,2,0:T(8,128)}, f32[12,1,1]{0,2,1:T(1,128)S(1)}, f32[12,256,64]{1,2,0:T(8,128)}, s32[]{:T(128)}, /*index=5*/s32[]{:T(128)}) while((s32[]{:T(128)}, f32[12,256,64]{1,2,0:T(8,128)}, f32[12,1,1]{0,2,1:T(1,128)S(1)}, f32[12,256,64]{1,2,0:T(8,128)}, s32[]{:T(128)}, ...), condition=%wide.region_100.102_spmd.clone, body=%wide.region_99.101_spmd.clone.sunk | while | flops 983043 | bytes 4718759 | solution.py:178
  2141.7 11.7 collective-permute-done.4
  2158.2 11.4 collective-permute-done.4
  2191.1 231.1 %while.434 = (s32[]{:T(128)}, f32[12,256,64]{1,2,0:T(8,128)}, f32[4,64,12,64]{3,1,2,0:T(8,128)}, bf16[4,64,256]{2,1,0:T(8,128)(2,1)}, bf16[4,64,256]{2,1,0:T(8,1...) while((s32[]{:T(128)}, f32[12,256,64]{1,2,0:T(8,128)}, ...), condition=%wide.region_111.113_spmd.clone, body=%wide.region_101.112_spmd.clone.sunk | while | flops 870767360 | bytes 14942357 | solution.py:135
  2426.4 11.7 while.432
  2461.0 33.3 reduce-scatter.6.cloned.1.call-done
  2505.1 31.9 all-reduce.44.cloned.1.call-done
  2554.8 42.0 %all-reduce.46.cloned.1.call-done = bf16[256,2048]{1,0:T(8,128)(2,1)} async-done(((bf16[256,2048]{1,0:T(8,128)(2,1)}), bf16[256,2048]{1,0:T(8,128)(2,1)}) %all-reduce.46.cloned.1.call-update) | async-done | bytes 1048592 | tf_op jit(solution)/shard_map/psum | solution.py:529
  2642.9 40.8 %all-reduce.48.cloned.1.call-done = bf16[256,2048]{1,0:T(8,128)(2,1)} async-done(((bf16[256,2048]{1,0:T(8,128)(2,1)}), bf16[256,2048]{1,0:T(8,128)(2,1)}) %all-reduce.48.cloned.1.call-update) | async-done | bytes 1048592 | tf_op jit(solution)/shard_map/psum | solution.py:414
  2712.8 15.3 while.448
  2728.1 48.0 %while.449 = (s32[]{:T(128)}, f32[12,256,64]{1,2,0:T(8,128)}, f32[12,1,1]{0,2,1:T(1,128)S(1)}, f32[12,256,64]{1,2,0:T(8,128)}, s32[]{:T(128)}, /*index=5*/s32[]{:T(128)}) while((s32[]{:T(128)}, f32[12,256,64]{1,2,0:T(8,128)}, f32[12,1,1]{0,2,1:T(1,128)S(1)}, f32[12,256,64]{1,2,0:T(8,128)}, s32[]{:T(128)}, ...), condition=%wide.region_131.133_spmd.clone, body=%wide.region_130.132_spmd.clone.sunk | while | flops 983043 | bytes 4718759 | solution.py:178
  2730.7 11.7 collective-permute-done.5
  2747.1 11.4 collective-permute-done.5
  2780.0 231.5 %while.437 = (s32[]{:T(128)}, f32[12,256,64]{1,2,0:T(8,128)}, f32[4,64,12,64]{3,1,2,0:T(8,128)}, bf16[4,64,256]{2,1,0:T(8,128)(2,1)}, bf16[4,64,256]{2,1,0:T(8,1...) while((s32[]{:T(128)}, f32[12,256,64]{1,2,0:T(8,128)}, ...), condition=%wide.region_142.144_spmd.clone, body=%wide.region_132.143_spmd.clone.sunk | while | flops 870767360 | bytes 14942357 | solution.py:135
  3026.5 11.8 while.435
  3070.3 22.8 reduce-scatter.8.cloned.1.call-done
  3107.8 27.4 all-reduce.50.cloned.1.call-done
  3177.0 21.9 all-reduce.56.cloned.1.call-done
  3206.5 82.0 %all-reduce.54.cloned.1.call-done = (bf16[256,2048]{1,0:T(8,128)(2,1)}, bf16[256,2048]{1,0:T(8,128)(2,1)}) async-done(((bf16[256,2048]{1,0:T(8,128)(2,1)}, bf16[256,2048]{1,0:T(8,128)(2,1)}), (bf16[256,2048]{1,0:T(8,128)(2,1)}, bf16[256,2048]{1,0:T(8,128)(2,1)})) %all-reduce.54.cloned.1.call-update) | async-done | bytes 2097168 | tf_op jit(solution)/shard_map/psum | solution.py:380
  3299.4 176.4 %all-reduce.52.cloned.1.call-done = (f32[1,8,16,2048]{3,2,1,0:T(8,128)}, f32[1,8,16,1072]{3,2,1,0:T(8,128)}, f32[1,8,16,2048]{3,2,1,0:T(8,128)}, f32[1,8,16,2048]{3,2,1,0:T(8,128)}, f32[1,8,16,2048]{3,2,1,0:T(8,128)}) async-done(((f32[1,8,16,2048]{3,2,1,0:T(8,128)}, f32[1,8,16,1072]{3,2,1,0:T(8,128)}, f32[1,8,16,2048]{3,2,1,0:T(8,128)}, f32[1,8,16,2048]{3,2,1,0:T(8,128)}, f32[1,8,16,2048]{3,2,1,0:T(8,128)}), ...) | async-done | bytes 4743184 | tf_op jit(solution)/shard_map/psum | solution.py:723
  (2633 shorter events, 2524.2 us)
Async XLA Ops:
  7.2 254.4 %copy-start = (bf16[1,768,2048]{2,1,0:T(8,128)(2,1)S(1)}, bf16[1,768,2048]{2,1,0:T(8,128)(2,1)}, u32[]{:S(2)}) copy-start(bf16[1,768,2048]{2,1,0:T(8,128)(2,1)} %param.161) | copy-start | bytes 9437188
  7.2 328.0 %all-reduce.26.cloned.1.call-start = ((), (), s32[]{:S(2)}) async-start(), calls=%async_computation.3 | async-start | bytes 2097152 | tf_op jit(solution)/shard_map/psum | solution.py:372
  41.2 1005.0 %copy-start.270 = (f32[256]{0:T(256)}, f32[256]{0:T(256)S(1)}, u32[]{:S(2)}) copy-start(f32[256]{0:T(256)S(1)} %fusion.1189) | copy-start | bytes 3076
  159.6 13.2 collective-permute-start
  176.3 12.0 collective-permute-start
  191.8 11.2 collective-permute-start
  265.6 139.4 %all-reduce.28.cloned.1.call-start = ((), (), s32[]{:S(2)}) async-start(), calls=%async_computation.4 | async-start | bytes 2097152 | tf_op jit(solution)/shard_map/psum | solution.py:380
  266.5 449.4 %copy-start.109 = (f32[1,2048]{1,0:T(1,128)}, f32[1,2048]{1,0:T(1,128)S(1)}, u32[]{:S(2)}) copy-start(f32[1,2048]{1,0:T(1,128)S(1)} %mul.2968) | copy-start | bytes 24580
  353.8 359.9 %all-reduce.30.cloned.1.call-start = ((), (), s32[]{:S(2)}) async-start(), calls=%async_computation.5 | async-start | bytes 2097152 | tf_op jit(solution)/shard_map/psum | solution.py:372
  409.3 8.8 collective-permute-start.6
  554.1 11.2 collective-permute-start.1
  568.9 11.5 collective-permute-start.1
  583.9 10.7 collective-permute-start.1
  652.5 129.9 %all-reduce.32.cloned.1.call-start = ((), (), s32[]{:S(2)}) async-start(), calls=%async_computation.6 | async-start | bytes 2097152 | tf_op jit(solution)/shard_map/psum | solution.py:380
  728.0 75.4 %slice-start.10 = ((s8[4390912]{0:T(1024)(128)(4,1)}), s8[196608]{0:T(1024)(128)(4,1)S(1)}, s32[]{:S(2)}) async-start(s8[4390912]{0:T(1024)(128)(4,1)} %bitcast.2507), calls=%async_computation.32 | async-start | bytes 393216
  731.1 690.1 %all-reduce.34.cloned.1.call-start = ((), (), s32[]{:S(2)}) async-start(), calls=%async_computation.7 | async-start | bytes 2097152 | tf_op jit(solution)/shard_map/psum | solution.py:372
  786.7 10.7 collective-permute-start.7
  982.9 11.2 collective-permute-start.2
  997.6 11.5 collective-permute-start.2
  1012.6 10.6 collective-permute-start.2
  1082.9 426.5 %all-reduce.36.cloned.1.call-start = ((), (), s32[]{:S(2)}) async-start(), calls=%async_computation.8 | async-start | bytes 2097152 | tf_op jit(solution)/shard_map/psum | solution.py:414
  1427.3 86.5 %copy-start.292 = (f32[256]{0:T(256)}, f32[256]{0:T(256)S(1)}, u32[]{:S(2)}) copy-start(f32[256]{0:T(256)S(1)} %get-tuple-element.4489) | copy-start | bytes 3076
  1427.3 86.5 %copy-start.322 = (f32[256]{0:T(256)}, f32[256]{0:T(256)S(1)}, u32[]{:S(2)}) copy-start(f32[256]{0:T(256)S(1)} %get-tuple-element.4488) | copy-start | bytes 3076
  1448.1 457.1 %reduce-scatter.4.cloned.1.call-start = ((), (), s32[]{:S(2)}) async-start(), calls=%async_computation.9 | async-start | bytes 655360 | tf_op jit(solution)/shard_map/reduce_scatter | solution.py:469
  1545.1 13.0 collective-permute-start.3
  1561.5 12.7 collective-permute-start.3
  1577.7 12.1 collective-permute-start.3
  1849.4 106.9 %all-reduce.38.cloned.1.call-start = ((), (), s32[]{:S(2)}) async-start(), calls=%async_computation.10 | async-start | bytes 1097728 | tf_op jit(solution)/shard_map/psum | solution.py:493
  1909.1 107.0 %all-reduce.40.cloned.1.call-start = ((), (), s32[]{:S(2)}) async-start(), calls=%async_computation.11 | async-start | bytes 2097152 | tf_op jit(solution)/shard_map/psum | solution.py:529
  1964.1 141.7 %all-reduce.42.cloned.1.call-start = ((), (), s32[]{:S(2)}) async-start(), calls=%async_computation.12 | async-start | bytes 2097152 | tf_op jit(solution)/shard_map/psum | solution.py:414
  2024.4 16.2 collective-permute-start.8
  2054.1 440.3 %reduce-scatter.6.cloned.1.call-start = ((), (), s32[]{:S(2)}) async-start(), calls=%async_computation.13 | async-start | bytes 655360 | tf_op jit(solution)/shard_map/reduce_scatter | solution.py:469
  2140.4 13.0 collective-permute-start.4
  2156.9 12.7 collective-permute-start.4
  2173.1 12.1 collective-permute-start.4
  2438.1 98.8 %all-reduce.44.cloned.1.call-start = ((), (), s32[]{:S(2)}) async-start(), calls=%async_computation.14 | async-start | bytes 1097728 | tf_op jit(solution)/shard_map/psum | solution.py:493
  2497.9 98.8 %all-reduce.46.cloned.1.call-start = ((), (), s32[]{:S(2)}) async-start(), calls=%async_computation.15 | async-start | bytes 2097152 | tf_op jit(solution)/shard_map/psum | solution.py:529
  2544.8 138.9 %all-reduce.48.cloned.1.call-start = ((), (), s32[]{:S(2)}) async-start(), calls=%async_computation.16 | async-start | bytes 2097152 | tf_op jit(solution)/shard_map/psum | solution.py:414
  2604.7 15.0 collective-permute-start.9
  2631.6 461.6 %reduce-scatter.8.cloned.1.call-start = ((), (), s32[]{:S(2)}) async-start(), calls=%async_computation.17 | async-start | bytes 655360 | tf_op jit(solution)/shard_map/reduce_scatter | solution.py:469
  2729.4 13.0 collective-permute-start.5
  2745.8 12.7 collective-permute-start.5
  2762.0 12.1 collective-permute-start.5
  3046.9 88.3 %all-reduce.50.cloned.1.call-start = ((), (), s32[]{:S(2)}) async-start(), calls=%async_computation.18 | async-start | bytes 1097728 | tf_op jit(solution)/shard_map/psum | solution.py:493
  3096.4 102.5 %all-reduce.56.cloned.1.call-start = ((), (), s32[]{:S(2)}) async-start(), calls=%async_computation.21 | async-start | bytes 3014656 | tf_op jit(solution)/shard_map/psum | solution.py:728
  3104.1 184.4 %all-reduce.54.cloned.1.call-start = ((), (), s32[]{:S(2)}) async-start(), calls=%async_computation.20 | async-start | bytes 4194304 | tf_op jit(solution)/shard_map/psum | solution.py:380
  3143.0 332.9 %all-reduce.52.cloned.1.call-start = ((), (), s32[]{:S(2)}) async-start(), calls=%async_computation.19 | async-start | bytes 9568256 | tf_op jit(solution)/shard_map/psum | solution.py:723
  3203.5 87.1 %copy-start.279 = (f32[256]{0:T(256)S(1)}, f32[256]{0:T(256)}, u32[]{:S(2)}) copy-start(f32[256]{0:T(256)} %compare_convert_fusion.3) | copy-start | bytes 3076
  (449 other events, 4055.2 us)
Sparse Core Ops, SparseCore 0:
  265.8 69.3 all-reduce.25
  353.9 51.1 all-reduce.27
  652.6 61.0 all-reduce.29
  731.2 51.1 all-reduce.31
  1083.0 60.9 all-reduce.33
  1448.3 61.0 all-reduce.35
  1849.6 55.6 reduce-scatter.3
  1909.2 47.0 all-reduce.37
  1964.2 51.8 all-reduce.39
  2054.2 51.5 all-reduce.41
  2438.3 56.0 reduce-scatter.5
  2498.1 38.8 all-reduce.43
  2544.9 51.8 all-reduce.45
  2631.7 51.9 all-reduce.47
  3047.0 46.0 reduce-scatter.7
  3096.5 38.7 all-reduce.49
  3138.9 59.9 all-reduce.55
  3202.3 86.1 all-reduce.53
  3295.5 180.3 all-reduce.51
where the time goes:
time: 3540 us; the launch traced here: 3490 us
  waiting for transfers between devices  986 us (28%)
  matrix products  955 us (27%)
  local copies, waits for them, and re-layouts  948 us (27%)
  other arithmetic  446 us (13%)
  starting transfers between devices  66.9 us (2%)
  blocking collectives  49.5 us (1%)
    dot_general x105, matrix products, high_dot(): jnp.dot(first_operand, second_operand, precision=lax.Precision.HIGHEST, p...  177 us
    psum x1, waiting for transfers between devices, shards(): lax.psum((partial_sums[0], partial_sums[3], partial_sums[6], partial_sums...  176 us
    ppermute x22, waiting for transfers between devices, shifted(): lax.ppermute(value, axis, [(source, source + steps) for source in range(f...  160 us
    dynamic_update_slice x36, local copies, waits for them, and re-layouts, scan_states(): lax.scan(jax.checkpoint(scan_block_step), state_start, pieces)  159 us
    psum x3, waiting for transfers between devices, layer_forward(): lax.psum(feed_part.astype(jnp.bfloat16), 'wt').astype(jnp.float32)  149 us
    dot_general x48, matrix products, scan_block_step(): jnp.einsum('jh,jn,jhp->hnp', tail_weight, block_in_map, block_inputs, pre...  137 us
    dot_general x48, matrix products, scan_block_step(): jnp.einsum('ijh,jhp->ihp', weights, block_inputs, precision=lax.Precision...  124 us
    psum x3, waiting for transfers between devices, hybrid_layer_backward(): lax.psum(feed_norm_part.astype(jnp.bfloat16), 'wt').astype(jnp.float32)  123 us
  transfers between devices with their start and end apart: 41, of which 36 were waited for; matrix products, arithmetic and copies ran while one was open for 19% of the time, Pallas kernels for 0%

commit v1 on v0

v1 whole, which is shorter than its diff:
```python
import functools

import jax
import jax.numpy as jnp
from jax import lax
from jax.experimental import pallas as pl
from jax.experimental.pallas import tpu as pltpu
from jax.sharding import PartitionSpec as P

QHEADS = 8
KVHEADS = 2
HEAD = 128
MHEAD = 64
NSTATE = 256
KEY_BLOCK = 256
PAIR = 2 * MHEAD

epsilon = 1e-05
rope_base = 10000.0
masked_score = -1e30
BF = jnp.bfloat16
F32 = jnp.float32
HIGH = lax.Precision.HIGHEST


def mm(a, b):
    return jnp.dot(a.astype(BF), b.astype(BF), preferred_element_type=F32)


def mm_t(a, b):
    return lax.dot_general(
        a.astype(BF), b.astype(BF), (((1,), (1,)), ((), ())), preferred_element_type=F32
    )


def t_mm(a, b):
    return lax.dot_general(
        a.astype(BF), b.astype(BF), (((0,), (0,)), ((), ())), preferred_element_type=F32
    )


def rms_scale(vector):
    return lax.rsqrt(jnp.mean(vector * vector, axis=-1, keepdims=True) + epsilon)


def norm_back(vector, grad_normed, gain_vec):
    scale_now = rms_scale(vector)
    weighted = grad_normed * gain_vec
    return weighted * scale_now - vector * scale_now**3 * jnp.mean(
        weighted * vector, axis=-1, keepdims=True
    )


def vmem_call(kernel, out_shape, **kwargs):
    return pl.pallas_call(
        kernel,
        out_shape=out_shape,
        compiler_params=pltpu.CompilerParams(vmem_limit_bytes=56 * 1024 * 1024),
        **kwargs,
    )


def pair_lanes(rows, left, right):
    lane = lax.broadcasted_iota(jnp.int32, (rows, PAIR), 1)
    return jnp.where(lane < MHEAD, left, right)


def scan_forward_kernel(x_ref, b_ref, c_ref, dt_ref, cum_ref, cumt_ref, y_ref, state_ref, tail_scr):
    rows = x_ref.shape[0]
    heads = dt_ref.shape[1]
    gram = mm_t(c_ref[...], b_ref[...])
    row = lax.broadcasted_iota(jnp.int32, (rows, rows), 0)
    col = lax.broadcasted_iota(jnp.int32, (rows, rows), 1)
    gram = jnp.where(row >= col, gram, 0.0)
    cum = cum_ref[...]
    dt = dt_ref[...]
    cumt = cumt_ref[...]
    tail = jnp.exp(cum[rows - 1 : rows, :] - cum)
    for pair in range(heads // 2):
        one, two = 2 * pair, 2 * pair + 1
        lanes = slice(PAIR * pair, PAIR * (pair + 1))
        scaled = x_ref[:, lanes] * pair_lanes(rows, dt[:, one : one + 1], dt[:, two : two + 1])
        scaled_low = scaled.astype(BF)
        tail_scr[:, lanes] = (
            scaled * pair_lanes(rows, tail[:, one : one + 1], tail[:, two : two + 1])
        ).astype(BF)
        parts = []
        for head in (one, two):
            decay = jnp.exp(jnp.minimum(cum[:, head : head + 1] - cumt[head : head + 1, :], 0.0))
            parts.append(mm((gram * decay), scaled_low))
        y_ref[:, lanes] = pair_lanes(rows, parts[0], parts[1])
    state_ref[...] = t_mm(b_ref[...], tail_scr[...]).astype(state_ref.dtype)


def scan_forward(x, b_low, c_low, dt, cum, cumt):
    rows, width = x.shape
    return vmem_call(
        scan_forward_kernel,
        (
            jax.ShapeDtypeStruct((rows, width), F32),
            jax.ShapeDtypeStruct((b_low.shape[1], width), BF),
        ),
        scratch_shapes=[pltpu.VMEM((rows, width), BF)],
    )(x, b_low, c_low, dt, cum, cumt)


def scan_backward_kernel(
    x_ref, dy_ref, b_ref, c_ref, dt_ref, cum_ref, cumt_ref, z_ref, db_ref, dc_ref
):
    rows = x_ref.shape[0]
    heads = dt_ref.shape[1]
    gram_t = mm_t(b_ref[...], c_ref[...])
    row = lax.broadcasted_iota(jnp.int32, (rows, rows), 0)
    col = lax.broadcasted_iota(jnp.int32, (rows, rows), 1)
    causal = col >= row
    gram_t = jnp.where(causal, gram_t, 0.0)
    cum = cum_ref[...]
    dt = dt_ref[...]
    cumt = cumt_ref[...]
    grad_gram_t = jnp.zeros((rows, rows), F32)
    lane = lax.broadcasted_iota(jnp.int32, (rows, PAIR), 1)
    for pair in range(heads // 2):
        one, two = 2 * pair, 2 * pair + 1
        lanes = slice(PAIR * pair, PAIR * (pair + 1))
        scaled_low = (
            x_ref[:, lanes] * pair_lanes(rows, dt[:, one : one + 1], dt[:, two : two + 1])
        ).astype(BF)
        dy = dy_ref[:, lanes]
        parts = []
        for head in (one, two):
            decay = jnp.exp(jnp.minimum(cumt[head : head + 1, :] - cum[:, head : head + 1], 0.0))
            parts.append(mm(gram_t * decay, dy))
            mine = (lane < MHEAD) if head == one else (lane >= MHEAD)
            outer = mm_t(jnp.where(mine, scaled_low, jnp.zeros_like(scaled_low)), dy)
            grad_gram_t = grad_gram_t + decay * outer
        z_ref[:, lanes] = pair_lanes(rows, parts[0], parts[1])
    grad_low = jnp.where(causal, grad_gram_t, 0.0).astype(BF)
    db_ref[...] = mm(grad_low, c_ref[...])
    dc_ref[...] = t_mm(grad_low, b_ref[...])


def scan_backward(x, dy_low, b_low, c_low, dt, cum, cumt):
    rows, width = x.shape
    states = b_low.shape[1]
    return vmem_call(
        scan_backward_kernel,
        (
            jax.ShapeDtypeStruct((rows, width), F32),
            jax.ShapeDtypeStruct((rows, states), F32),
            jax.ShapeDtypeStruct((rows, states), F32),
        ),
    )(x, dy_low, b_low, c_low, dt, cum, cumt)


def block_mask(scores_shape, span, block, ctx_index, length):
    row = lax.broadcasted_iota(jnp.int32, scores_shape, 0)
    query_pos = ctx_index * span + lax.rem(row, span)
    key_pos = block * KEY_BLOCK + lax.broadcasted_iota(jnp.int32, scores_shape, 1)
    return (key_pos <= query_pos) & (key_pos < length)


def attend_forward_kernel(place_ref, q_ref, kv_ref, out_ref, lse_ref, top_scr, sum_scr):
    span = out_ref.shape[0]
    heads = q_ref.shape[0] // span
    length, ctx_index, blocks = place_ref[0], place_ref[1], place_ref[2]
    queries = q_ref[...]
    rows = queries.shape[0]
    top_scr[...] = jnp.full(top_scr.shape, masked_score, F32)
    sum_scr[...] = jnp.zeros(sum_scr.shape, F32)
    lse_ref[...] = jnp.zeros(lse_ref.shape, F32)

    def step(block, nothing):
        start = pl.multiple_of(block * KEY_BLOCK, KEY_BLOCK)
        keys = kv_ref[pl.ds(start, KEY_BLOCK), :HEAD]
        values = kv_ref[pl.ds(start, KEY_BLOCK), HEAD:]
        scores = HEAD ** (-0.5) * mm_t(queries, keys)
        allowed = block_mask(scores.shape, span, block, ctx_index, length)
        scores = jnp.where(allowed, scores, masked_score)
        top = top_scr[...]
        fresh_top = jnp.maximum(top, jnp.max(scores, axis=1, keepdims=True))
        shares = jnp.where(allowed, jnp.exp(scores - fresh_top), 0.0)
        fade = jnp.exp(top - fresh_top)
        lse_ref[...] = lse_ref[...] * fade + jnp.sum(shares, axis=1, keepdims=True)
        sum_scr[...] = sum_scr[...] * fade + mm(shares, values)
        top_scr[...] = fresh_top
        return nothing

    lax.fori_loop(0, blocks, step, 0)
    total = lse_ref[...]
    result = sum_scr[...] / total
    for head in range(heads):
        out_ref[:, head * HEAD : (head + 1) * HEAD] = result[head * span : (head + 1) * span, :]
    lse_ref[...] = top_scr[...] + jnp.log(total)


def attend_forward(place, query_rows, key_all, span):
    rows = query_rows.shape[0]
    return pl.pallas_call(
        attend_forward_kernel,
        out_shape=(
            jax.ShapeDtypeStruct((span, rows // span * HEAD), F32),
            jax.ShapeDtypeStruct((rows, 1), F32),
        ),
        in_specs=[
            pl.BlockSpec(memory_space=pltpu.SMEM),
            pl.BlockSpec(memory_space=pltpu.VMEM),
            pl.BlockSpec(memory_space=pltpu.VMEM),
        ],
        scratch_shapes=[pltpu.VMEM((rows, 1), F32), pltpu.VMEM((rows, HEAD), F32)],
        compiler_params=pltpu.CompilerParams(vmem_limit_bytes=56 * 1024 * 1024),
    )(place, query_rows, key_all)


def attend_backward_kernel(
    place_ref, q_ref, kv_ref, lse_ref, out_ref, grad_ref, dq_ref, dkv_ref, dq_scr
):
    span = out_ref.shape[0]
    heads = q_ref.shape[0] // span
    length, ctx_index, blocks = place_ref[0], place_ref[1], place_ref[2]
    queries = q_ref[...]
    grad_rows = jnp.concatenate(
        [grad_ref[:, head * HEAD : (head + 1) * HEAD] for head in range(heads)], axis=0
    )
    out_rows = jnp.concatenate(
        [out_ref[:, head * HEAD : (head + 1) * HEAD] for head in range(heads)], axis=0
    )
    delta = jnp.sum(grad_rows.astype(F32) * out_rows, axis=1, keepdims=True)
    lse = lse_ref[...]
    dq_scr[...] = jnp.zeros(dq_scr.shape, F32)
    dkv_ref[...] = jnp.zeros(dkv_ref.shape, dkv_ref.dtype)

    def step(block, nothing):
        start = pl.multiple_of(block * KEY_BLOCK, KEY_BLOCK)
        keys = kv_ref[pl.ds(start, KEY_BLOCK), :HEAD]
        values = kv_ref[pl.ds(start, KEY_BLOCK), HEAD:]
        scores = HEAD ** (-0.5) * mm_t(queries, keys)
        allowed = block_mask(scores.shape, span, block, ctx_index, length)
        shares = jnp.where(allowed, jnp.exp(jnp.where(allowed, scores, masked_score) - lse), 0.0)
        grad_share = mm_t(grad_rows, values)
        grad_score = (shares * (grad_share - delta)).astype(BF)
        dq_scr[...] += mm(grad_score, keys)
        dkv_ref[pl.ds(start, KEY_BLOCK), :HEAD] = (
            HEAD ** (-0.5) * t_mm(grad_score, queries)
        ).astype(dkv_ref.dtype)
        dkv_ref[pl.ds(start, KEY_BLOCK), HEAD:] = t_mm(shares, grad_rows).astype(dkv_ref.dtype)
        return nothing

    lax.fori_loop(0, blocks, step, 0)
    for head in range(heads):
        dq_ref[:, head * HEAD : (head + 1) * HEAD] = (
            HEAD ** (-0.5) * dq_scr[head * span : (head + 1) * span, :]
        )


def attend_backward(place, query_rows, key_all, lse, attended, grad_low):
    span = attended.shape[0]
    rows = query_rows.shape[0]
    vm = pl.BlockSpec(memory_space=pltpu.VMEM)
    return pl.pallas_call(
        attend_backward_kernel,
        out_shape=(
            jax.ShapeDtypeStruct(attended.shape, F32),
            jax.ShapeDtypeStruct(key_all.shape, BF),
        ),
        in_specs=[pl.BlockSpec(memory_space=pltpu.SMEM), vm, vm, vm, vm, vm],
        scratch_shapes=[pltpu.VMEM((rows, HEAD), F32)],
        compiler_params=pltpu.CompilerParams(vmem_limit_bytes=56 * 1024 * 1024),
    )(place, query_rows, key_all, lse, attended, grad_low)


def swap(value):
    return lax.ppermute(value, "section", [(0, 1), (1, 0)])


def shifted(value, steps):
    count = lax.axis_size("ctx")
    first, last = max(0, -steps), min(count, count - steps)
    return lax.ppermute(value, "ctx", [(source, source + steps) for source in range(first, last)])


def rope_tables(positions):
    half_width = HEAD // 2
    frequencies = rope_base ** (-jnp.arange(half_width, dtype=F32) / half_width)
    angles = positions.astype(F32)[:, None] * frequencies[None, :]
    return jnp.cos(angles), jnp.sin(angles)


def rotate(values, tables, direction):
    half_width = HEAD // 2
    cosine, sine = tables[0], direction * tables[1]
    heads = []
    for head in range(values.shape[1] // HEAD):
        first = values[:, head * HEAD : head * HEAD + half_width]
        second = values[:, head * HEAD + half_width : (head + 1) * HEAD]
        heads.append(first * cosine - second * sine)
        heads.append(second * cosine + first * sine)
    return jnp.concatenate(heads, axis=1)


def carried_states(local_state, total_decay, reverse):
    count = lax.axis_size("ctx")
    here = lax.axis_index("ctx")
    totals = lax.all_gather(total_decay, "ctx", axis=0)
    summed = jnp.zeros(local_state.shape, F32)
    between = jnp.zeros(total_decay.shape, F32)
    for steps in range(1, count):
        moved = shifted(local_state, -steps if reverse else steps).astype(F32)
        factor = jnp.repeat(jnp.exp(between), MHEAD)[None, :]
        summed = summed + factor * moved
        source = here + steps if reverse else here - steps
        passed = lax.dynamic_index_in_dim(
            totals, jnp.clip(source, 0, count - 1), 0, keepdims=False
        )
        between = between + passed
    return summed


def wide(per_head):
    return jnp.repeat(per_head, MHEAD, axis=1)


def head_sum(values):
    return jnp.sum(values.reshape(values.shape[0], -1, MHEAD), axis=2)


def low_sum(value):
    return lax.psum(value.astype(BF), "wt").astype(F32)


class Weights:
    pass


def layer_forward(entry_low, w, place):
    saved = {"entry": entry_low}
    entry = entry_low.astype(F32)
    normed = (entry * rms_scale(entry) * w.mixer_gain).astype(BF)
    small_in = mm_t(normed, w.mixin_down)
    small_in_low = small_in.astype(BF)
    query_proj = mm(normed, w.query) + mm(small_in_low, w.query_up)
    mamba_proj = mm(normed, w.mamba) + mm(small_in_low, w.mamba_up)
    shared = mm(normed, w.shared) + mm(small_in_low, w.shared_up)
    span = entry.shape[0]
    local_heads = query_proj.shape[1] // HEAD
    key_head = place.wt * local_heads // (QHEADS // KVHEADS)
    rotated = rotate(query_proj, place.tables, 1.0).astype(BF)
    query_rows = jnp.concatenate(
        [rotated[:, head * HEAD : (head + 1) * HEAD] for head in range(local_heads)], axis=0
    )
    key_part = lax.dynamic_slice_in_dim(shared, key_head * HEAD, HEAD, 1)
    value_part = lax.dynamic_slice_in_dim(shared, (KVHEADS + key_head) * HEAD, HEAD, 1)
    key_value = jnp.concatenate([rotate(key_part, place.tables, 1.0), value_part], axis=1)
    key_all = lax.all_gather(key_value.astype(BF), "ctx", axis=0, tiled=True)

    half = mamba_proj.shape[1] // 2
    heads = half // MHEAD
    gate_raw, inputs = mamba_proj[:, :half], mamba_proj[:, half:]
    offset = 2 * KVHEADS * HEAD
    input_map = shared[:, offset : offset + NSTATE].astype(BF)
    output_map = shared[:, offset + NSTATE : offset + 2 * NSTATE].astype(BF)
    step_raw = lax.dynamic_slice_in_dim(
        shared, offset + 2 * NSTATE + place.wt * heads, heads, 1
    )
    step_in = step_raw + w.step_bias
    step_sizes = jax.nn.softplus(step_in) * place.live[:, None]
    cum = jnp.cumsum(-w.decay_rate * step_sizes, axis=0)
    total = cum[-1]
    local_y, local_state = scan_forward(
        inputs, input_map, output_map, step_sizes, cum, cum.T
    )
    attended, lse = attend_forward(place.scalars, query_rows, key_all, span)
    state_in = carried_states(local_state, total, False).astype(BF)
    scanned = local_y + wide(jnp.exp(cum)) * mm(output_map, state_in)
    joined = scanned + jnp.repeat(w.skip_gain, MHEAD)[None, :] * inputs
    gated_low = (joined * jax.nn.silu(gate_raw)).astype(BF)
    attended_low = attended.astype(BF)
    small_mid = mm_t(attended_low, w.attnout_down) + mm_t(gated_low, w.mambaout_down)
    part = (
        mm(attended_low, w.attnout) + mm(gated_low, w.mambaout) + mm(small_mid, w.mixout_up)
    )
    hidden = entry + place.live[:, None] * low_sum(part)

    feed_normed = (hidden * rms_scale(hidden) * w.feed_gain).astype(BF)
    small_feed = mm_t(feed_normed, w.feedin_down)
    gateup = mm(feed_normed, w.gateup) + mm(small_feed, w.feedin_up)
    width = gateup.shape[1] // 2
    gate_value, up_value = gateup[:, :width], gateup[:, width:]
    inner = (jax.nn.silu(gate_value) * up_value).astype(BF)
    small_out = mm_t(inner, w.feedout_down)
    feed_part = mm(inner, w.down) + mm(small_out, w.feedout_up)
    result = hidden + low_sum(feed_part)
    saved.update(
        normed=normed,
        small_in=small_in_low,
        query_rows=query_rows,
        key_all=key_all,
        key_head=key_head,
        gate_raw=gate_raw,
        inputs=inputs,
        input_map=input_map,
        output_map=output_map,
        step_in=step_in,
        step_sizes=step_sizes,
        cum=cum,
        local_state=local_state,
        state_in=state_in,
        scanned=scanned,
        attended=attended,
        lse=lse,
        gated_low=gated_low,
        attended_low=attended_low,
        small_mid=small_mid,
        hidden=hidden,
        feed_normed=feed_normed,
        small_feed=small_feed,
        gate_value=gate_value,
        up_value=up_value,
        inner=inner,
        small_out=small_out,
    )
    return result, saved


def layer_backward(grad_out, w, place, s):
    grads = {}
    span = grad_out.shape[0]
    grad_feed = grad_out.astype(BF)
    grad_small_out = mm_t(grad_feed, w.feedout_up)
    grads["feedout_up"] = t_mm(s["small_out"], grad_feed)
    grads["feedout_down"] = t_mm(grad_small_out, s["inner"])
    grad_inner = mm_t(grad_feed, w.down) + mm(grad_small_out, w.feedout_down)
    gate_value, up_value = s["gate_value"], s["up_value"]
    sigmoid_gate = jax.nn.sigmoid(gate_value)
    grad_gate = grad_inner * up_value * sigmoid_gate * (1.0 + gate_value * (1.0 - sigmoid_gate))
    grad_up = grad_inner * gate_value * sigmoid_gate
    grad_gateup = jnp.concatenate([grad_gate, grad_up], axis=1).astype(BF)
    grad_small_feed = mm_t(grad_gateup, w.feedin_up)
    grads["feedin_up"] = t_mm(s["small_feed"], grad_gateup)
    grads["feedin_down"] = t_mm(grad_small_feed, s["feed_normed"])
    feed_norm_part = mm_t(grad_gateup, w.gateup) + mm(grad_small_feed, w.feedin_down)
    grad_hidden = grad_out + norm_back(s["hidden"], low_sum(feed_norm_part), w.feed_gain)

    grad_mixed = (grad_hidden * place.live[:, None]).astype(BF)
    grad_small_mid = mm_t(grad_mixed, w.mixout_up)
    grads["mixout_up"] = t_mm(s["small_mid"], grad_mixed)
    grads["attnout_down"] = t_mm(grad_small_mid, s["attended_low"])
    grads["mambaout_down"] = t_mm(grad_small_mid, s["gated_low"])
    grad_gated = mm_t(grad_mixed, w.mambaout) + mm(grad_small_mid, w.mambaout_down)
    gate_raw, inputs, scanned = s["gate_raw"], s["inputs"], s["scanned"]
    skip = jnp.repeat(w.skip_gain, MHEAD)[None, :]
    sigmoid_raw = jax.nn.sigmoid(gate_raw)
    silu_raw = gate_raw * sigmoid_raw
    dy_low = (grad_gated * silu_raw).astype(BF)
    dy = dy_low.astype(F32)
    grad_gates = (
        grad_gated * (scanned + skip * inputs) * sigmoid_raw * (1.0 + gate_raw * (1.0 - sigmoid_raw))
    )
    cum, step_sizes = s["cum"], s["step_sizes"]
    grown = wide(jnp.exp(cum))
    grown_dy = (grown * dy).astype(BF)
    local_grad = t_mm(s["output_map"], grown_dy)
    grad_state = carried_states(local_grad.astype(BF), cum[-1], True).astype(BF)

    grad_attended = (
        mm_t(grad_mixed, w.attnout) + mm(grad_small_mid, w.attnout_down)
    ).astype(BF)
    grad_query, grad_keyval = attend_backward(
        place.scalars, s["query_rows"], s["key_all"], s["lse"], s["attended"], grad_attended
    )
    own = lax.psum_scatter(grad_keyval, "ctx", scatter_dimension=0, tiled=True).astype(F32)

    z_local, db_local, dc_local = scan_backward(
        inputs, dy_low, s["input_map"], s["output_map"], step_sizes, cum, cum.T
    )
    dt_wide = wide(step_sizes)
    tail = wide(jnp.exp(cum[-1:] - cum))
    scaled_low = (inputs * dt_wide).astype(BF)
    scaled = scaled_low.astype(F32)
    z_tail = tail * mm(s["input_map"], grad_state)
    z_all = z_local + z_tail
    grad_inputs = dt_wide * z_all + skip * dy
    grad_map_in = db_local + mm_t((tail * scaled), grad_state)
    grad_map_out = dc_local + mm_t(grown_dy, s["state_in"])
    kept = jnp.sum(
        grad_state.astype(F32) * s["state_in"].astype(F32), axis=0
    )[None, :] * jnp.repeat(jnp.exp(cum[-1]), MHEAD)[None, :]
    edge = head_sum(jnp.sum(scaled * z_tail, axis=0, keepdims=True) + kept)
    through = head_sum(dy * scanned - scaled * z_all)
    cum_grad = edge + jnp.flip(jnp.cumsum(jnp.flip(through, 0), axis=0), 0)
    grad_steps = head_sum(inputs * z_all) - w.decay_rate * cum_grad
    grad_step = grad_steps * jax.nn.sigmoid(s["step_in"]) * place.live[:, None]

    heads = cum.shape[1]
    grad_query_low = rotate(grad_query, place.tables, -1.0).astype(BF)
    grad_keys = rotate(own[:, :HEAD], place.tables, -1.0)
    key_head = s["key_head"]
    offset = 2 * KVHEADS * HEAD
    keyval = jnp.zeros((span, offset), F32)
    keyval = lax.dynamic_update_slice_in_dim(keyval, grad_keys, key_head * HEAD, 1)
    keyval = lax.dynamic_update_slice_in_dim(
        keyval, own[:, HEAD:], (KVHEADS + key_head) * HEAD, 1
    )
    all_heads = w.shared.shape[1] - offset - 2 * NSTATE
    step_part = lax.dynamic_update_slice_in_dim(
        jnp.zeros((span, all_heads), F32), grad_step, place.wt * heads, 1
    )
    grad_shared = jnp.concatenate(
        [keyval, grad_map_in, grad_map_out, step_part], axis=1
    ).astype(BF)
    grad_mamba = jnp.concatenate([grad_gates, grad_inputs], axis=1).astype(BF)
    grad_small_in = (
        mm_t(grad_query_low, w.query_up)
        + mm_t(grad_mamba, w.mamba_up)
        + mm_t(grad_shared, w.shared_up)
    )
    grads["query_up"] = t_mm(s["small_in"], grad_query_low)
    grads["mamba_up"] = t_mm(s["small_in"], grad_mamba)
    grads["shared_up"] = t_mm(s["small_in"], grad_shared)
    grads["mixin_down"] = t_mm(grad_small_in, s["normed"])
    norm_part = (
        mm_t(grad_query_low, w.query)
        + mm_t(grad_mamba, w.mamba)
        + mm_t(grad_shared, w.shared)
        + mm(grad_small_in, w.mixin_down)
    )
    grad_entry = grad_hidden + norm_back(
        s["entry"].astype(F32), low_sum(norm_part), w.mixer_gain
    )
    return grad_entry, grads


FIXED = (
    "mixer_gain",
    "feed_gain",
    "decay_rate",
    "step_bias",
    "skip_gain",
    "query",
    "mamba",
    "shared",
    "attnout",
    "mambaout",
    "gateup",
    "down",
)
ADAPTERS = (
    "mixin_down",
    "query_up",
    "mamba_up",
    "shared_up",
    "attnout_down",
    "mambaout_down",
    "mixout_up",
    "feedin_down",
    "feedin_up",
    "feedout_down",
    "feedout_up",
)
REPLICATED = ("mixin_down", "shared_up", "mixout_up", "feedin_down", "feedout_up")


def shards(layer_input, cotangent, seq_lengths, adapter_ids, *params):
    section = lax.axis_index("section")
    ctx_index = lax.axis_index("ctx")
    micro_count, span = layer_input.shape[0], layer_input.shape[1]
    assert micro_count == 2 and lax.axis_size("section") == 2

    place = Weights()
    place.wt = lax.axis_index("wt")
    length = seq_lengths[section]
    positions = ctx_index * span + jnp.arange(span, dtype=jnp.int32)
    place.live = (positions < length).astype(F32)
    place.tables = rope_tables(positions)
    blocks = jnp.minimum(
        ((ctx_index + 1) * span + KEY_BLOCK - 1) // KEY_BLOCK, (length + KEY_BLOCK - 1) // KEY_BLOCK
    )
    place.scalars = jnp.stack([length, ctx_index, blocks]).astype(jnp.int32)

    own, other = {}, {}
    shapes = {}
    for name, item in zip(FIXED, params):
        value = item[0]
        if name in ("mamba", "gateup"):
            value = value.reshape(value.shape[0], -1)
        own[name] = value
        other[name] = swap(value)
    mine, theirs = adapter_ids[section], adapter_ids[1 - section]
    for name, item in zip(ADAPTERS, params[len(FIXED) :]):
        shapes[name] = item.shape[1:]
        flat = item[0].reshape(item.shape[1], item.shape[2], -1)
        own[name] = lax.dynamic_index_in_dim(flat, mine, 0, keepdims=False)
        other[name] = swap(lax.dynamic_index_in_dim(flat, theirs, 0, keepdims=False))

    layers = []
    for index in range(2):
        w = Weights()
        for name in own:
            setattr(w, name, jnp.where(section == index, own[name], other[name]))
        layers.append(w)

    entry = lax.dynamic_index_in_dim(layer_input, section, 0, keepdims=False)
    saved, outs = [], []
    for w in layers:
        result, kept = layer_forward(entry, w, place)
        entry = result.astype(BF)
        outs.append(entry)
        saved.append(kept)

    grad = lax.dynamic_index_in_dim(cotangent, section, 0, keepdims=False).astype(F32)
    grad_lows, grad_sets = [None, None], [None, None]
    for index in (1, 0):
        grad, found = layer_backward(grad, layers[index], place, saved[index])
        grad_low = grad.astype(BF)
        grad_lows[index] = grad_low
        grad = grad_low.astype(F32)
        summed = {}
        replicated = lax.psum(tuple(found[name] for name in REPLICATED), ("ctx", "wt"))
        summed.update(zip(REPLICATED, replicated))
        for name in ADAPTERS:
            if name not in REPLICATED:
                summed[name] = lax.psum(found[name].astype(BF), "ctx")
        grad_sets[index] = summed

    def by_layer(values):
        keep = jnp.where(section == 0, values[0], values[1])
        moved = swap(jnp.where(section == 0, values[1], values[0]))
        return keep, moved

    def stacked(values):
        keep, moved = by_layer(values)
        return jnp.stack(
            [jnp.where(section == 0, keep, moved), jnp.where(section == 0, moved, keep)]
        )[None]

    results = [stacked(outs), stacked(grad_lows)]
    for name in ADAPTERS:
        keep, moved = by_layer((grad_sets[0][name], grad_sets[1][name]))
        shape = shapes[name]
        total = jnp.zeros((shape[0],) + keep.shape, F32)
        total = total.at[mine].add(keep.astype(F32)).at[theirs].add(moved.astype(F32))
        results.append(total.reshape(shape)[None])
    return tuple(results)


def solution(mesh):
    in_specs = (
        P(None, "ctx", None),
        P(None, "ctx", None),
        P(),
        P(),
        P("section", None),
        P("section", None),
        P("section", "wt"),
        P("section", "wt"),
        P("section", "wt"),
        P("section", None, "wt"),
        P("section", None, None, "wt"),
        P("section", None, None),
        P("section", "wt", None),
        P("section", "wt", None),
        P("section", None, None, "wt"),
        P("section", "wt", None),
        P("section", None, None, None),
        P("section", None, None, "wt"),
        P("section", None, None, None, "wt"),
        P("section", None, None, None),
        P("section", None, None, "wt"),
        P("section", None, None, "wt"),
        P("section", None, None, None),
        P("section", None, None, None),
        P("section", None, None, None, "wt"),
        P("section", None, None, "wt"),
        P("section", None, None, None),
    )
    out_specs = (
        P("section", None, "ctx", None),
        P("section", None, "ctx", None),
    ) + in_specs[16:]
    return jax.shard_map(shards, mesh=mesh, in_specs=in_specs, out_specs=out_specs, check_vma=False)
```

time: 3540 us -> 1110 us (0.31); the launches traced: 3490 us -> 1100 us
  local copies, waits for them, and re-layouts: 948 us -> 102 us
  matrix products: 955 us -> 211 us
  waiting for transfers between devices: 986 us -> 518 us
  other arithmetic: 446 us -> 124 us
    dot_general x417 -> x104, matrix products: 924 us -> 211 us  [the longest x40 92.7 us: mm_t(): lax.dot_general(a.astype(BF), b.astype(BF), (((1,), (1,)), ((), ())), pre...]
    psum x16 -> x10, waiting for transfers between devices: 747 us -> 500 us  [the longest x7 346 us: low_sum(): return lax.psum(value.astype(BF), 'wt').astype(F32)]
    dynamic_update_slice x45 -> x4, local copies, waits for them, and re-layouts: 163 us -> 0.59 us  [the longest x2 0.53 us: layer_backward(): lax.dynamic_update_slice_in_dim(jnp.zeros((span, all_heads), F32), grad_s...]
    ppermute x22 -> x48, waiting for transfers between devices: 160 us -> 7.53 us  [the longest x12 7.39 us: shifted(): lax.ppermute(value, 'ctx', [(source, source + steps) for source in range(...]
    another operation x144 -> x37, local copies, waits for them, and re-layouts: 124 us -> 13.8 us
    squeeze x145 -> x11, local copies, waits for them, and re-layouts: 119 us -> 13.9 us  [shards(): lax.dynamic_index_in_dim(flat, theirs, 0, keepdims=False)]
    dynamic_slice x58 -> x2, local copies, waits for them, and re-layouts: 92 us -> 1.18 us  [the longest x1 0.59 us: shards(): length = seq_lengths[section]]
    unnamed x786 -> x487, local copies, waits for them, and re-layouts: 116 us -> 31.4 us
  transfers between devices with their start and end apart: 41 -> 60, of which waited for: 36 -> 13; matrix products, arithmetic and copies ran while one was open for 19% -> 27% of each run, Pallas kernels for 0% -> 2%
where the time goes in v1:
time: 1110 us; the launch traced here: 1100 us
  waiting for transfers between devices  518 us (47%)
  matrix products  211 us (19%)
  other arithmetic  124 us (11%)
  local copies, waits for them, and re-layouts  102 us (9%)
  blocking collectives  54.1 us (5%)
  starting transfers between devices  38.2 us (3%)
  Pallas kernels  28.4 us (3%)
  between operations  22.5 us (2%)
    psum x7, waiting for transfers between devices, low_sum(): return lax.psum(value.astype(BF), 'wt').astype(F32)  346 us
    psum x1, waiting for transfers between devices, shards(): lax.psum(tuple((found[name] for name in REPLICATED)), ('ctx', 'wt'))  111 us
    dot_general x40, matrix products, mm_t(): lax.dot_general(a.astype(BF), b.astype(BF), (((1,), (1,)), ((), ())), pre...  92.7 us
    dot_general x40, matrix products, mm(): return jnp.dot(a.astype(BF), b.astype(BF), preferred_element_type=F32)  87.1 us
    psum x2, waiting for transfers between devices, shards(): summed[name] = lax.psum(found[name].astype(BF), 'ctx')  42.2 us
    all_gather x2, blocking collectives, layer_forward(): key_all = lax.all_gather(key_value.astype(BF), 'ctx', axis=0, tiled=True)  34 us
    unnamed x487, local copies, waits for them, and re-layouts  31.4 us
    dot_general x24, matrix products, t_mm(): lax.dot_general(a.astype(BF), b.astype(BF), (((0,), (0,)), ((), ())), pre...  31 us
  transfers between devices with their start and end apart: 60, of which 13 were waited for; matrix products, arithmetic and copies ran while one was open for 27% of the time, Pallas kernels for 2%

profile of v1, /device:TPU:0, one launch (start us, length us, event | category | flops | bytes accessed | tf_op | source)
XLA Modules:
  0.0 1097.5 jit_solution(6881379853232578604)
XLA Ops:
  7.8 6.8 copy.210
  22.7 10.3 copy.212
  59.0 4.7 fusion.314
  66.7 9.3 all-gather
  84.4 5.1 convolution_add_fusion.7
  90.5 4.0 shard_map.355
  94.5 3.4 collective-permute-start.11
  102.8 20.8 %all_gather.14.kv_ref = bf16[1024,256]{1,0:T(8,128)(2,1)} all-gather(bf16[256,256]{1,0:T(8,128)(2,1)S(1)} %pad_maximum_fusion.18), channel_id=1, replica_groups=mesh['section'=2,'ctx'=4,'wt'=4] {'ctx'}, dimensions={0}, use_global_device_ids=true | all-gather | bytes 655360 | tf_op jit(solution)/shard_map/all_gather | solution.py:353
  124.4 3.4 shard_map.354
  149.4 48.0 %all-reduce.15.cloned.1.call-done = bf16[256,2048]{1,0:T(8,128)(2,1)} async-done(((bf16[256,2048]{1,0:T(8,128)(2,1)}), bf16[256,2048]{1,0:T(8,128)(2,1)}) %all-reduce.15.cloned.1.call-update) | async-done | bytes 1048592 | tf_op jit(solution)/shard_map/psum | solution.py:327
  203.1 5.7 fusion.12
  216.0 52.7 %all-reduce.17.cloned.1.call-done = bf16[256,2048]{1,0:T(8,128)(2,1)} async-done(((bf16[256,2048]{1,0:T(8,128)(2,1)}), bf16[256,2048]{1,0:T(8,128)(2,1)}) %all-reduce.17.cloned.1.call-update) | async-done | bytes 1048592 | tf_op jit(solution)/shard_map/psum | solution.py:327
  274.0 5.2 fusion.315
  284.8 4.7 convolution_add_fusion.6
  291.6 4.0 shard_map.357
  295.6 4.1 collective-permute-start.26
  299.7 3.4 collective-permute-start.27
  307.5 10.7 all-gather.1
  328.3 13.2 %all_gather.16.kv_ref = bf16[1024,256]{1,0:T(8,128)(2,1)} all-gather(bf16[256,256]{1,0:T(8,128)(2,1)S(1)} %pad_maximum_fusion.19), channel_id=1, replica_groups=mesh['section'=2,'ctx'=4,'wt'=4] {'ctx'}, dimensions={0}, use_global_device_ids=true | all-gather | bytes 655360 | tf_op jit(solution)/shard_map/all_gather | solution.py:353
  342.3 3.4 shard_map.356
  349.7 4.0 fusion.47
  372.8 40.1 %all-reduce.19.cloned.1.call-done = bf16[256,2048]{1,0:T(8,128)(2,1)} async-done(((bf16[256,2048]{1,0:T(8,128)(2,1)}), bf16[256,2048]{1,0:T(8,128)(2,1)}) %all-reduce.19.cloned.1.call-update) | async-done | bytes 1048592 | tf_op jit(solution)/shard_map/psum | solution.py:327
  418.0 5.9 fusion.10
  424.0 4.9 multiply_convert_fusion.7
  432.6 7.1 fusion.15
  448.0 4.5 fusion.19
  452.4 38.5 %all-reduce.21.cloned.1.call-done = bf16[256,2048]{1,0:T(8,128)(2,1)} async-done(((bf16[256,2048]{1,0:T(8,128)(2,1)}), bf16[256,2048]{1,0:T(8,128)(2,1)}) %all-reduce.21.cloned.1.call-update) | async-done | bytes 1048592 | tf_op jit(solution)/shard_map/psum | solution.py:327
  497.8 4.9 multiply_convert_fusion.15
  509.1 3.8 shard_map.359
  530.3 3.4 fusion.65
  553.7 6.2 fusion.23
  561.6 5.3 fusion.41
  579.4 48.9 %all-reduce.23.cloned.1.call-done = bf16[256,2048]{1,0:T(8,128)(2,1)} async-done(((bf16[256,2048]{1,0:T(8,128)(2,1)}), bf16[256,2048]{1,0:T(8,128)(2,1)}) %all-reduce.23.cloned.1.call-update) | async-done | bytes 1048592 | tf_op jit(solution)/shard_map/psum | solution.py:327
  643.3 6.9 fusion.14
  652.3 33.0 %all-reduce.33.cloned.1.call-done = (bf16[16,2048]{1,0:T(8,128)(2,1)}, bf16[16,2048]{1,0:T(8,128)(2,1)}) async-done(((bf16[16,2048]{1,0:T(8,128)(2,1)}, bf16[16,2048]{1,0:T(8,128)(2,1)}), (bf16[16,2048]{1,0:T(8,128)(2,1)}, bf16[16,2048]{1,0:T(8,128)(2,1)})) %all-reduce.33.cloned.1.call-update) | async-done | bytes 131088 | tf_op jit(solution)/shard_map/psum | solution.py:621
  691.6 3.1 broadcast_in_dim_reshape.5
  694.7 45.4 %all-reduce.25.cloned.1.call-done = bf16[256,2048]{1,0:T(8,128)(2,1)} async-done(((bf16[256,2048]{1,0:T(8,128)(2,1)}), bf16[256,2048]{1,0:T(8,128)(2,1)}) %all-reduce.25.cloned.1.call-update) | async-done | bytes 1048592 | tf_op jit(solution)/shard_map/psum | solution.py:327
  743.0 3.7 multiply_convert_fusion
  749.0 4.1 multiply_convert_fusion.12
  759.1 3.8 shard_map.361
  774.5 5.5 collective-permute-done.34
  782.1 3.4 fusion.71
  817.3 6.2 fusion.22
  823.6 9.3 all-reduce.31.cloned.1.call-done
  849.8 10.8 reduce-scatter.5.cloned.1.call-done
  870.0 3.9 fusion.40
  875.6 110.9 %all-reduce.27.cloned.1.call-done = (f32[16,2048]{1,0:T(8,128)}, f32[16,2048]{1,0:T(8,128)}, f32[16,1072]{1,0:T(8,128)}, f32[16,1072]{1,0:T(8,128)}, f32[16,2048...) async-done(((f32[16,2048]{1,0:T(8,128)}, f32[16,2048]{1,0:T(8,128)}, ...) | async-done | bytes 1185808 | tf_op jit(solution)/shard_map/psum | solution.py:617
  1002.4 72.8 %all-reduce.29.cloned.1.call-done = (bf16[256,2048]{1,0:T(8,128)(2,1)}, bf16[256,2048]{1,0:T(8,128)(2,1)}) async-done(((bf16[256,2048]{1,0:T(8,128)(2,1)}, bf16[256,2048]{1,0:T(8,128)(2,1)}), (bf16[256,2048]{1,0:T(8,128)(2,1)}, bf16[256,2048]{1,0:T(8,128)(2,1)})) %all-reduce.29.cloned.1.call-update) | async-done | bytes 2097168 | tf_op jit(solution)/shard_map/psum | solution.py:327
  (929 shorter events, 351.8 us)
Async XLA Ops:
  7.2 190.2 %all-reduce.15.cloned.1.call-start = ((), (), s32[]{:S(2)}) async-start(), calls=%async_computation.2 | async-start | bytes 2097152 | tf_op jit(solution)/shard_map/psum | solution.py:327
  7.2 51.8 %collective-permute-start.4 = (bf16[2048,1072]{0,1:T(8,128)(2,1)}, bf16[2048,1072]{0,1:T(8,128)(2,1)}, u32[]{:S(2)}, u32[]{:S(2)}) collective-permute-start(bf16[2048,1072]{0,1:T(8,128)(2,1)} %bitcast.561), channel_id=1, source_target_pairs={{0,16},{16,0},{1,17},{17,1},{2,18},{18,2},{3,19},{19,3},{4,20},{20... | collective-permute-start | bytes 13172744 | tf_op jit(solution)/shard_map/ppermute | solution.py:272
  14.6 69.8 %collective-permute-start.7 = (bf16[2048,1536]{1,0:T(8,128)(2,1)}, bf16[2048,1536]{1,0:T(8,128)(2,1)}, u32[]{:S(2)}, u32[]{:S(2)}) collective-permute-start(bf16[2048,1536]{1,0:T(8,128)(2,1)} %bitcast.130), channel_id=1, source_target_pairs={{0,16},{16,0},{1,17},{17,1},{2,18},{18,2},{3,19},{19,3},{4,20},{20... | collective-permute-start | bytes 18874376 | tf_op jit(solution)/shard_map/ppermute | solution.py:272
  18.7 33.1 %collective-permute-start.2 = (bf16[16,2048]{1,0:T(8,128)(2,1)}, bf16[16,2048]{1,0:T(8,128)(2,1)}, u32[]{:S(2)}, u32[]{:S(2)}) collective-permute-start(bf16[16,2048]{1,0:T(8,128)(2,1)} %dynamic-slice_bitcast_fusion.4), channel_id=1, source_target_pairs={{0,16},{16,0},{1,17},{17,1},{2,18},{18,2},{3,19},{19,3},{4,20},{20... | collective-permute-start | bytes 196616 | tf_op jit(solution)/shard_map/ppermute | solution.py:272
  19.2 30.9 %collective-permute-start = (bf16[2048]{0:T(1024)(128)(2,1)S(1)}, bf16[2048]{0:T(1024)(128)(2,1)}, u32[]{:S(2)}, u32[]{:S(2)}) collective-permute-start(bf16[2048]{0:T(1024)(128)(2,1)S(1)} %reduce.56), channel_id=1, source_target_pairs={{0,16},{16,0},{1,17},{17,1},{2,18},{18,2},{3,19},{19,3},{4,20},{20... | collective-permute-start | bytes 12296 | tf_op jit(solution)/shard_map/ppermute | solution.py:272
  19.3 25.8 %collective-permute-start.9 = (f32[12]{0:T(128)S(1)}, f32[12]{0:T(128)}, u32[]{:S(2)}, u32[]{:S(2)}) collective-permute-start(f32[12]{0:T(128)S(1)} %bitcast.558), channel_id=1, source_target_pairs={{0,16},{16,0},{1,17},{17,1},{2,18},{18,2},{3,19},{19,3},{4,20},{20... | collective-permute-start | bytes 152 | tf_op jit(solution)/shard_map/ppermute | solution.py:272
  50.1 7.9 collective-permute-start.1
  54.9 80.1 %collective-permute-start.15 = (bf16[768,2048]{1,0:T(8,128)(2,1)}, bf16[768,2048]{1,0:T(8,128)(2,1)}, u32[]{:S(2)}, u32[]{:S(2)}) collective-permute-start(bf16[768,2048]{1,0:T(8,128)(2,1)} %bitcast.27), channel_id=1, source_target_pairs={{0,16},{16,0},{1,17},{17,1},{2,18},{18,2},{3,19},{19,3},{4,20},{20... | collective-permute-start | bytes 9437192 | tf_op jit(solution)/shard_map/ppermute | solution.py:272
  56.0 147.1 %collective-permute-start.20 = (bf16[2048,2048]{1,0:T(8,128)(2,1)}, bf16[2048,2048]{1,0:T(8,128)(2,1)}, u32[]{:S(2)}, u32[]{:S(2)}) collective-permute-start(bf16[2048,2048]{1,0:T(8,128)(2,1)} %bitcast.509), channel_id=1, source_target_pairs={{0,16},{16,0},{1,17},{17,1},{2,18},{18,2},{3,19},{19,3},{4,20},{20... | collective-permute-start | bytes 25165832 | tf_op jit(solution)/shard_map/ppermute | solution.py:272
  94.5 33.3 %collective-permute-start.11 = (bf16[256,768]{1,0:T(8,128)(2,1)}, bf16[256,768]{1,0:T(8,128)(2,1)S(1)}, u32[]{:S(2)}, u32[]{:S(2)}) collective-permute-start(bf16[256,768]{1,0:T(8,128)(2,1)} %get-tuple-element.297), channel_id=1, source_target_pairs={{0,4},{4,8},{8,12},{1,5},{5,9},{9,13},{2,6},{6,10},{10,14},{3,7},{... | collective-permute-start | bytes 1179656 | tf_op jit(solution)/shard_map/ppermute | solution.py:278
  97.9 30.0 %collective-permute-start.12 = (bf16[256,768]{1,0:T(8,128)(2,1)}, bf16[256,768]{1,0:T(8,128)(2,1)S(1)}, u32[]{:S(2)}, u32[]{:S(2)}) collective-permute-start(bf16[256,768]{1,0:T(8,128)(2,1)} %get-tuple-element.297), channel_id=1, source_target_pairs={{0,8},{4,12},{1,9},{5,13},{2,10},{6,14},{3,11},{7,15},{16,24},{20,... | collective-permute-start | bytes 1179656 | tf_op jit(solution)/shard_map/ppermute | solution.py:278
  100.3 28.0 %collective-permute-start.13 = (bf16[256,768]{1,0:T(8,128)(2,1)}, bf16[256,768]{1,0:T(8,128)(2,1)S(1)}, u32[]{:S(2)}, u32[]{:S(2)}) collective-permute-start(bf16[256,768]{1,0:T(8,128)(2,1)} %get-tuple-element.297), channel_id=1, source_target_pairs={{0,12},{1,13},{2,14},{3,15},{16,28},{17,29},{18,30},{19,31}} | collective-permute-start | bytes 1179656 | tf_op jit(solution)/shard_map/ppermute | solution.py:278
  128.3 5.3 collective-permute-start.18
  131.3 6.7 collective-permute-start.6
  140.6 128.1 %all-reduce.17.cloned.1.call-start = ((), (), s32[]{:S(2)}) async-start(), calls=%async_computation.3 | async-start | bytes 2097152 | tf_op jit(solution)/shard_map/psum | solution.py:327
  141.2 7.1 collective-permute-start.19
  143.8 56.6 %collective-permute-start.21 = (bf16[16,2048]{1,0:T(8,128)(2,1)}, bf16[16,2048]{1,0:T(8,128)(2,1)}, u32[]{:S(2)}, u32[]{:S(2)}) collective-permute-start(bf16[16,2048]{1,0:T(8,128)(2,1)} %dynamic-slice_bitcast_fusion.2), channel_id=1, source_target_pairs={{0,16},{16,0},{1,17},{17,1},{2,18},{18,2},{3,19},{19,3},{4,20},{20... | collective-permute-start | bytes 196616 | tf_op jit(solution)/shard_map/ppermute | solution.py:272
  143.8 68.9 %collective-permute-start.23 = (bf16[1024,2048]{1,0:T(8,128)(2,1)}, bf16[1024,2048]{1,0:T(8,128)(2,1)}, u32[]{:S(2)}, u32[]{:S(2)}) collective-permute-start(bf16[1024,2048]{1,0:T(8,128)(2,1)} %bitcast.562), channel_id=1, source_target_pairs={{0,16},{16,0},{1,17},{17,1},{2,18},{18,2},{3,19},{19,3},{4,20},{20... | collective-permute-start | bytes 12582920 | tf_op jit(solution)/shard_map/ppermute | solution.py:272
  145.4 56.4 %collective-permute-start.22 = (bf16[16,2048]{1,0:T(8,128)(2,1)}, bf16[16,2048]{1,0:T(8,128)(2,1)}, u32[]{:S(2)}, u32[]{:S(2)}) collective-permute-start(bf16[16,2048]{1,0:T(8,128)(2,1)} %dynamic-slice_bitcast_fusion.1), channel_id=1, source_target_pairs={{0,16},{16,0},{1,17},{17,1},{2,18},{18,2},{3,19},{19,3},{4,20},{20... | collective-permute-start | bytes 196616 | tf_op jit(solution)/shard_map/ppermute | solution.py:272
  148.3 61.0 %collective-permute-start.24 = (bf16[16,1024]{1,0:T(8,128)(2,1)}, bf16[16,1024]{1,0:T(8,128)(2,1)}, u32[]{:S(2)}, u32[]{:S(2)}) collective-permute-start(bf16[16,1024]{1,0:T(8,128)(2,1)} %dynamic-slice_bitcast_fusion.7), channel_id=1, source_target_pairs={{0,16},{16,0},{1,17},{17,1},{2,18},{18,2},{3,19},{19,3},{4,20},{20... | collective-permute-start | bytes 98312 | tf_op jit(solution)/shard_map/ppermute | solution.py:272
  200.4 11.0 %collective-permute-start.25 = (bf16[16,2048]{1,0:T(8,128)(2,1)S(1)}, bf16[16,2048]{1,0:T(8,128)(2,1)S(1)}, u32[]{:S(2)}, u32[]{:S(2)}) collective-permute-start(bf16[16,2048]{1,0:T(8,128)(2,1)S(1)} %copy-done.160), channel_id=1, source_target_pairs={{0,16},{16,0},{1,17},{17,1},{2,18},{18,2},{3,19},{19,3},{4,20},{20... | collective-permute-start | bytes 196616 | tf_op jit(solution)/shard_map/ppermute | solution.py:272
  215.1 197.9 %all-reduce.19.cloned.1.call-start = ((), (), s32[]{:S(2)}) async-start(), calls=%async_computation.4 | async-start | bytes 2097152 | tf_op jit(solution)/shard_map/psum | solution.py:327
  295.6 50.1 %collective-permute-start.26 = (bf16[256,768]{1,0:T(8,128)(2,1)}, bf16[256,768]{1,0:T(8,128)(2,1)}, u32[]{:S(2)}, u32[]{:S(2)}) collective-permute-start(bf16[256,768]{1,0:T(8,128)(2,1)} %get-tuple-element.300), channel_id=1, source_target_pairs={{0,4},{4,8},{8,12},{1,5},{5,9},{9,13},{2,6},{6,10},{10,14},{3,7},{... | collective-permute-start | bytes 1179656 | tf_op jit(solution)/shard_map/ppermute | solution.py:278
  299.7 46.0 %collective-permute-start.27 = (bf16[256,768]{1,0:T(8,128)(2,1)}, bf16[256,768]{1,0:T(8,128)(2,1)}, u32[]{:S(2)}, u32[]{:S(2)}) collective-permute-start(bf16[256,768]{1,0:T(8,128)(2,1)} %get-tuple-element.300), channel_id=1, source_target_pairs={{0,8},{4,12},{1,9},{5,13},{2,10},{6,14},{3,11},{7,15},{16,24},{20,... | collective-permute-start | bytes 1179656 | tf_op jit(solution)/shard_map/ppermute | solution.py:278
  303.1 42.6 %collective-permute-start.28 = (bf16[256,768]{1,0:T(8,128)(2,1)}, bf16[256,768]{1,0:T(8,128)(2,1)}, u32[]{:S(2)}, u32[]{:S(2)}) collective-permute-start(bf16[256,768]{1,0:T(8,128)(2,1)} %get-tuple-element.300), channel_id=1, source_target_pairs={{0,12},{1,13},{2,14},{3,15},{16,28},{17,29},{18,30},{19,31}} | collective-permute-start | bytes 1179656 | tf_op jit(solution)/shard_map/ppermute | solution.py:278
  358.7 132.2 %all-reduce.21.cloned.1.call-start = ((), (), s32[]{:S(2)}) async-start(), calls=%async_computation.5 | async-start | bytes 2097152 | tf_op jit(solution)/shard_map/psum | solution.py:327
  439.7 120.2 %reduce-scatter.3.cloned.1.call-start = ((), (), s32[]{:S(2)}) async-start(), calls=%async_computation.6 | async-start | bytes 655360 | tf_op jit(solution)/shard_map/reduce_scatter | solution.py:470
  504.9 21.2 %collective-permute-start.30 = (bf16[256,768]{1,0:T(8,128)(2,1)}, bf16[256,768]{1,0:T(8,128)(2,1)}, u32[]{:S(2)}, u32[]{:S(2)}) collective-permute-start(bf16[256,768]{1,0:T(8,128)(2,1)} %convolution_convert_fusion.5), channel_id=1, source_target_pairs={{4,0},{8,4},{12,8},{5,1},{9,5},{13,9},{6,2},{10,6},{14,10},{7,3},{... | collective-permute-start | bytes 1179656 | tf_op jit(solution)/shard_map/ppermute | solution.py:278
  506.5 21.5 %collective-permute-start.31 = (bf16[256,768]{1,0:T(8,128)(2,1)}, bf16[256,768]{1,0:T(8,128)(2,1)}, u32[]{:S(2)}, u32[]{:S(2)}) collective-permute-start(bf16[256,768]{1,0:T(8,128)(2,1)} %convolution_convert_fusion.5), channel_id=1, source_target_pairs={{8,0},{12,4},{9,1},{13,5},{10,2},{14,6},{11,3},{15,7},{24,16},{28,... | collective-permute-start | bytes 1179656 | tf_op jit(solution)/shard_map/ppermute | solution.py:278
  507.8 20.2 %collective-permute-start.32 = (bf16[256,768]{1,0:T(8,128)(2,1)}, bf16[256,768]{1,0:T(8,128)(2,1)}, u32[]{:S(2)}, u32[]{:S(2)}) collective-permute-start(bf16[256,768]{1,0:T(8,128)(2,1)} %convolution_convert_fusion.5), channel_id=1, source_target_pairs={{12,0},{13,1},{14,2},{15,3},{28,16},{29,17},{30,18},{31,19}} | collective-permute-start | bytes 1179656 | tf_op jit(solution)/shard_map/ppermute | solution.py:278
  521.5 106.8 %all-reduce.23.cloned.1.call-start = ((), (), s32[]{:S(2)}) async-start(), calls=%async_computation.7 | async-start | bytes 2097152 | tf_op jit(solution)/shard_map/psum | solution.py:327
  572.8 112.4 %all-reduce.33.cloned.1.call-start = ((), (), s32[]{:S(2)}) async-start(), calls=%async_computation.13 | async-start | bytes 262144 | tf_op jit(solution)/shard_map/psum | solution.py:621
  641.8 98.3 %all-reduce.25.cloned.1.call-start = ((), (), s32[]{:S(2)}) async-start(), calls=%async_computation.8 | async-start | bytes 2097152 | tf_op jit(solution)/shard_map/psum | solution.py:327
  652.0 180.8 %all-reduce.31.cloned.1.call-start = ((), (), s32[]{:S(2)}) async-start(), calls=%async_computation.12 | async-start | bytes 491520 | tf_op jit(solution)/shard_map/psum | solution.py:621
  755.2 19.2 %collective-permute-start.33 = (bf16[256,768]{1,0:T(8,128)(2,1)}, bf16[256,768]{1,0:T(8,128)(2,1)}, u32[]{:S(2)}, u32[]{:S(2)}) collective-permute-start(bf16[256,768]{1,0:T(8,128)(2,1)} %convolution_convert_fusion.4), channel_id=1, source_target_pairs={{4,0},{8,4},{12,8},{5,1},{9,5},{13,9},{6,2},{10,6},{14,10},{7,3},{... | collective-permute-start | bytes 1179656 | tf_op jit(solution)/shard_map/ppermute | solution.py:278
  756.5 23.4 %collective-permute-start.34 = (bf16[256,768]{1,0:T(8,128)(2,1)}, bf16[256,768]{1,0:T(8,128)(2,1)}, u32[]{:S(2)}, u32[]{:S(2)}) collective-permute-start(bf16[256,768]{1,0:T(8,128)(2,1)} %convolution_convert_fusion.4), channel_id=1, source_target_pairs={{8,0},{12,4},{9,1},{13,5},{10,2},{14,6},{11,3},{15,7},{24,16},{28,... | collective-permute-start | bytes 1179656 | tf_op jit(solution)/shard_map/ppermute | solution.py:278
  757.8 22.1 %collective-permute-start.35 = (bf16[256,768]{1,0:T(8,128)(2,1)}, bf16[256,768]{1,0:T(8,128)(2,1)}, u32[]{:S(2)}, u32[]{:S(2)}) collective-permute-start(bf16[256,768]{1,0:T(8,128)(2,1)} %convolution_convert_fusion.4), channel_id=1, source_target_pairs={{12,0},{13,1},{14,2},{15,3},{28,16},{29,17},{30,18},{31,19}} | collective-permute-start | bytes 1179656 | tf_op jit(solution)/shard_map/ppermute | solution.py:278
  787.1 73.5 %reduce-scatter.5.cloned.1.call-start = ((), (), s32[]{:S(2)}) async-start(), calls=%async_computation.9 | async-start | bytes 655360 | tf_op jit(solution)/shard_map/reduce_scatter | solution.py:470
  789.4 197.2 %all-reduce.27.cloned.1.call-start = ((), (), s32[]{:S(2)}) async-start(), calls=%async_computation.10 | async-start | bytes 2392064 | tf_op jit(solution)/shard_map/psum | solution.py:617
  833.7 9.8 collective-permute-start.46
  835.9 6.9 collective-permute-start.42
  837.9 7.2 collective-permute-start.39
  868.3 206.8 %all-reduce.29.cloned.1.call-start = ((), (), s32[]{:S(2)}) async-start(), calls=%async_computation.11 | async-start | bytes 4194304 | tf_op jit(solution)/shard_map/psum | solution.py:327
  987.5 11.8 %collective-permute-start.47 = (f32[16,2048]{1,0:T(8,128)S(1)}, f32[16,2048]{1,0:T(8,128)S(1)}, u32[]{:S(2)}, u32[]{:S(2)}) collective-permute-start(f32[16,2048]{1,0:T(8,128)S(1)} %broadcast_select_fusion.62), channel_id=1, source_target_pairs={{0,16},{16,0},{1,17},{17,1},{2,18},{18,2},{3,19},{19,3},{4,20},{20... | collective-permute-start | bytes 393224 | tf_op jit(solution)/shard_map/ppermute | solution.py:272
  989.3 11.7 %collective-permute-start.44 = (f32[16,2048]{1,0:T(8,128)S(1)}, f32[16,2048]{1,0:T(8,128)S(1)}, u32[]{:S(2)}, u32[]{:S(2)}) collective-permute-start(f32[16,2048]{1,0:T(8,128)S(1)} %broadcast_select_fusion.64), channel_id=1, source_target_pairs={{0,16},{16,0},{1,17},{17,1},{2,18},{18,2},{3,19},{19,3},{4,20},{20... | collective-permute-start | bytes 393224 | tf_op jit(solution)/shard_map/ppermute | solution.py:272
  992.3 88.0 %collective-permute-start.43 = (f32[16,2048]{1,0:T(8,128)}, f32[16,2048]{1,0:T(8,128)S(1)}, u32[]{:S(2)}, u32[]{:S(2)}) collective-permute-start(f32[16,2048]{1,0:T(8,128)} %broadcast_select_fusion.65), channel_id=1, source_target_pairs={{0,16},{16,0},{1,17},{17,1},{2,18},{18,2},{3,19},{19,3},{4,20},{20... | collective-permute-start | bytes 393224 | tf_op jit(solution)/shard_map/ppermute | solution.py:272
  995.9 87.9 %collective-permute-start.37 = (f32[16,2048]{1,0:T(8,128)}, f32[16,2048]{1,0:T(8,128)S(1)}, u32[]{:S(2)}, u32[]{:S(2)}) collective-permute-start(f32[16,2048]{1,0:T(8,128)} %broadcast_select_fusion.66), channel_id=1, source_target_pairs={{0,16},{16,0},{1,17},{17,1},{2,18},{18,2},{3,19},{19,3},{4,20},{20... | collective-permute-start | bytes 393224 | tf_op jit(solution)/shard_map/ppermute | solution.py:272
  1080.2 5.9 collective-permute-start.36
  (248 other events, 2936.5 us)
Sparse Core Ops, SparseCore 0:
  140.7 56.6 all-reduce.14
  215.2 53.4 all-reduce.16
  358.9 53.9 all-reduce.18
  439.8 51.1 all-reduce.20
  521.6 30.1 reduce-scatter.2
  573.0 55.3 all-reduce.22
  641.9 43.3 all-reduce.32
  688.2 51.8 all-reduce.24
  787.3 45.5 all-reduce.30
  835.5 25.0 reduce-scatter.4
  868.4 118.0 all-reduce.26
  989.4 85.7 all-reduce.28

commit v2 on v1

--- a/solution.py
+++ b/solution.py
@@ -272,10 +272,24 @@
     return lax.ppermute(value, "section", [(0, 1), (1, 0)])
 
 
+def after(value, *others):
+    return lax.optimization_barrier((value,) + others)[0]
+
+
 def shifted(value, steps):
     count = lax.axis_size("ctx")
     first, last = max(0, -steps), min(count, count - steps)
     return lax.ppermute(value, "ctx", [(source, source + steps) for source in range(first, last)])
+
+
+def exchange_sum(value, axis):
+    count = lax.axis_size(axis)
+    bit = 1
+    while bit < count:
+        moved = lax.ppermute(value, axis, [(place, place ^ bit) for place in range(count)])
+        value = (value.astype(F32) + moved.astype(F32)).astype(value.dtype)
+        bit *= 2
+    return value
 
 
 def rope_tables(positions):
@@ -297,22 +311,43 @@
     return jnp.concatenate(heads, axis=1)
 
 
-def carried_states(local_state, total_decay, reverse):
+def gathered_rows(own, ctx_index):
+    span = own.shape[0]
     count = lax.axis_size("ctx")
-    here = lax.axis_index("ctx")
-    totals = lax.all_gather(total_decay, "ctx", axis=0)
-    summed = jnp.zeros(local_state.shape, F32)
-    between = jnp.zeros(total_decay.shape, F32)
+    rows = jnp.zeros((count * span, own.shape[1]), own.dtype)
+    for steps in range(count - 1, 0, -1):
+        place = jnp.maximum(ctx_index - steps, 0) * span
+        rows = lax.dynamic_update_slice_in_dim(rows, shifted(own, steps), place, 0)
+    return lax.dynamic_update_slice_in_dim(rows, own, ctx_index * span, 0)
+
+
+def returned_rows(rows, span, ctx_index):
+    count = lax.axis_size("ctx")
+    total = lax.dynamic_slice_in_dim(rows, ctx_index * span, span, 0).astype(F32)
     for steps in range(1, count):
-        moved = shifted(local_state, -steps if reverse else steps).astype(F32)
-        factor = jnp.repeat(jnp.exp(between), MHEAD)[None, :]
-        summed = summed + factor * moved
-        source = here + steps if reverse else here - steps
-        passed = lax.dynamic_index_in_dim(
-            totals, jnp.clip(source, 0, count - 1), 0, keepdims=False
-        )
-        between = between + passed
+        place = jnp.maximum(ctx_index - steps, 0) * span
+        part = lax.dynamic_slice_in_dim(rows, place, span, 0)
+        total = total + shifted(part, -steps).astype(F32)
+    return total
+
+
+def carried_states(payload, states, reverse):
+    count = lax.axis_size("ctx")
+    summed = jnp.zeros((states, payload.shape[1]), F32)
+    between = jnp.ones((1, payload.shape[1]), F32)
+    for steps in range(1, count):
+        moved = shifted(payload, -steps if reverse else steps).astype(F32)
+        summed = summed + between * moved[:states]
+        between = between * (moved[states : states + 1] + moved[states + 1 : states + 2])
     return summed
+
+
+def state_payload(state, total):
+    decay = jnp.repeat(jnp.exp(total), MHEAD)[None, :]
+    high = decay.astype(BF)
+    low = (decay - high.astype(F32)).astype(BF)
+    pad = jnp.zeros((14, decay.shape[1]), BF)
+    return jnp.concatenate([state.astype(BF), high, low, pad], axis=0)
 
 
 def wide(per_head):
@@ -331,26 +366,25 @@
     pass
 
 
-def layer_forward(entry_low, w, place):
+def layer_forward(entry_low, w, place, last):
     saved = {"entry": entry_low}
     entry = entry_low.astype(F32)
     normed = (entry * rms_scale(entry) * w.mixer_gain).astype(BF)
-    small_in = mm_t(normed, w.mixin_down)
-    small_in_low = small_in.astype(BF)
-    query_proj = mm(normed, w.query) + mm(small_in_low, w.query_up)
-    mamba_proj = mm(normed, w.mamba) + mm(small_in_low, w.mamba_up)
-    shared = mm(normed, w.shared) + mm(small_in_low, w.shared_up)
+    small_in = mm_t(normed, w.mixin_down).astype(BF)
+    shared = mm(normed, w.shared) + mm(small_in, w.shared_up)
+    query_proj = mm(normed, w.query) + mm(small_in, w.query_up)
+    mamba_proj = mm(normed, w.mamba) + mm(small_in, w.mamba_up)
     span = entry.shape[0]
     local_heads = query_proj.shape[1] // HEAD
     key_head = place.wt * local_heads // (QHEADS // KVHEADS)
+    key_part = lax.dynamic_slice_in_dim(shared, key_head * HEAD, HEAD, 1)
+    value_part = lax.dynamic_slice_in_dim(shared, (KVHEADS + key_head) * HEAD, HEAD, 1)
+    key_value = jnp.concatenate([rotate(key_part, place.tables, 1.0), value_part], axis=1)
+    key_all = gathered_rows(key_value.astype(BF), place.ctx)
     rotated = rotate(query_proj, place.tables, 1.0).astype(BF)
     query_rows = jnp.concatenate(
         [rotated[:, head * HEAD : (head + 1) * HEAD] for head in range(local_heads)], axis=0
     )
-    key_part = lax.dynamic_slice_in_dim(shared, key_head * HEAD, HEAD, 1)
-    value_part = lax.dynamic_slice_in_dim(shared, (KVHEADS + key_head) * HEAD, HEAD, 1)
-    key_value = jnp.concatenate([rotate(key_part, place.tables, 1.0), value_part], axis=1)
-    key_all = lax.all_gather(key_value.astype(BF), "ctx", axis=0, tiled=True)
 
     half = mamba_proj.shape[1] // 2
     heads = half // MHEAD
@@ -363,13 +397,13 @@
     )
     step_in = step_raw + w.step_bias
     step_sizes = jax.nn.softplus(step_in) * place.live[:, None]
-    cum = jnp.cumsum(-w.decay_rate * step_sizes, axis=0)
-    total = cum[-1]
+    cum = jnp.dot(place.lower, -w.decay_rate * step_sizes, precision=HIGH)
     local_y, local_state = scan_forward(
         inputs, input_map, output_map, step_sizes, cum, cum.T
     )
+    state_sum = carried_states(state_payload(local_state, cum[-1]), NSTATE, False)
     attended, lse = attend_forward(place.scalars, query_rows, key_all, span)
-    state_in = carried_states(local_state, total, False).astype(BF)
+    state_in = state_sum.astype(BF)
     scanned = local_y + wide(jnp.exp(cum)) * mm(output_map, state_in)
     joined = scanned + jnp.repeat(w.skip_gain, MHEAD)[None, :] * inputs
     gated_low = (joined * jax.nn.silu(gate_raw)).astype(BF)
@@ -381,17 +415,16 @@
     hidden = entry + place.live[:, None] * low_sum(part)
 
     feed_normed = (hidden * rms_scale(hidden) * w.feed_gain).astype(BF)
-    small_feed = mm_t(feed_normed, w.feedin_down)
+    small_feed = mm_t(feed_normed, w.feedin_down).astype(BF)
     gateup = mm(feed_normed, w.gateup) + mm(small_feed, w.feedin_up)
     width = gateup.shape[1] // 2
     gate_value, up_value = gateup[:, :width], gateup[:, width:]
     inner = (jax.nn.silu(gate_value) * up_value).astype(BF)
     small_out = mm_t(inner, w.feedout_down)
-    feed_part = mm(inner, w.down) + mm(small_out, w.feedout_up)
-    result = hidden + low_sum(feed_part)
+    feed_part = (mm(inner, w.down) + mm(small_out, w.feedout_up)).astype(BF)
     saved.update(
         normed=normed,
-        small_in=small_in_low,
+        small_in=small_in,
         query_rows=query_rows,
         key_all=key_all,
         key_head=key_head,
@@ -402,28 +435,28 @@
         step_in=step_in,
         step_sizes=step_sizes,
         cum=cum,
-        local_state=local_state,
         state_in=state_in,
         scanned=scanned,
         attended=attended,
         lse=lse,
         gated_low=gated_low,
         attended_low=attended_low,
-        small_mid=small_mid,
+        small_mid=exchange_sum(small_mid, "wt"),
         hidden=hidden,
         feed_normed=feed_normed,
         small_feed=small_feed,
         gate_value=gate_value,
         up_value=up_value,
         inner=inner,
-        small_out=small_out,
-    )
-    return result, saved
-
-
-def layer_backward(grad_out, w, place, s):
+        small_out=exchange_sum(small_out, "wt"),
+    )
+    if last:
+        return feed_part, saved
+    return hidden + low_sum(feed_part), saved
+
+
+def feed_backward(grad_out, w, place, s):
     grads = {}
-    span = grad_out.shape[0]
     grad_feed = grad_out.astype(BF)
     grad_small_out = mm_t(grad_feed, w.feedout_up)
     grads["feedout_up"] = t_mm(s["small_out"], grad_feed)
@@ -436,10 +469,15 @@
     grad_gateup = jnp.concatenate([grad_gate, grad_up], axis=1).astype(BF)
     grad_small_feed = mm_t(grad_gateup, w.feedin_up)
     grads["feedin_up"] = t_mm(s["small_feed"], grad_gateup)
-    grads["feedin_down"] = t_mm(grad_small_feed, s["feed_normed"])
     feed_norm_part = mm_t(grad_gateup, w.gateup) + mm(grad_small_feed, w.feedin_down)
-    grad_hidden = grad_out + norm_back(s["hidden"], low_sum(feed_norm_part), w.feed_gain)
-
+    summed = low_sum(feed_norm_part)
+    grads["feedin_down"] = t_mm(exchange_sum(grad_small_feed, "wt"), s["feed_normed"])
+    return grad_out + norm_back(s["hidden"], summed, w.feed_gain), grads
+
+
+def mixer_backward(grad_hidden, w, place, s):
+    grads = {}
+    span = grad_hidden.shape[0]
     grad_mixed = (grad_hidden * place.live[:, None]).astype(BF)
     grad_small_mid = mm_t(grad_mixed, w.mixout_up)
     grads["mixout_up"] = t_mm(s["small_mid"], grad_mixed)
@@ -459,7 +497,7 @@
     grown = wide(jnp.exp(cum))
     grown_dy = (grown * dy).astype(BF)
     local_grad = t_mm(s["output_map"], grown_dy)
-    grad_state = carried_states(local_grad.astype(BF), cum[-1], True).astype(BF)
+    grad_state = carried_states(state_payload(local_grad, cum[-1]), NSTATE, True).astype(BF)
 
     grad_attended = (
         mm_t(grad_mixed, w.attnout) + mm(grad_small_mid, w.attnout_down)
@@ -467,7 +505,7 @@
     grad_query, grad_keyval = attend_backward(
         place.scalars, s["query_rows"], s["key_all"], s["lse"], s["attended"], grad_attended
     )
-    own = lax.psum_scatter(grad_keyval, "ctx", scatter_dimension=0, tiled=True).astype(F32)
+    own = returned_rows(grad_keyval, span, place.ctx)
 
     z_local, db_local, dc_local = scan_backward(
         inputs, dy_low, s["input_map"], s["output_map"], step_sizes, cum, cum.T
@@ -486,7 +524,7 @@
     )[None, :] * jnp.repeat(jnp.exp(cum[-1]), MHEAD)[None, :]
     edge = head_sum(jnp.sum(scaled * z_tail, axis=0, keepdims=True) + kept)
     through = head_sum(dy * scanned - scaled * z_all)
-    cum_grad = edge + jnp.flip(jnp.cumsum(jnp.flip(through, 0), axis=0), 0)
+    cum_grad = edge + jnp.dot(place.lower.T, through, precision=HIGH)
     grad_steps = head_sum(inputs * z_all) - w.decay_rate * cum_grad
     grad_step = grad_steps * jax.nn.sigmoid(s["step_in"]) * place.live[:, None]
 
@@ -513,19 +551,18 @@
         + mm_t(grad_mamba, w.mamba_up)
         + mm_t(grad_shared, w.shared_up)
     )
-    grads["query_up"] = t_mm(s["small_in"], grad_query_low)
-    grads["mamba_up"] = t_mm(s["small_in"], grad_mamba)
-    grads["shared_up"] = t_mm(s["small_in"], grad_shared)
-    grads["mixin_down"] = t_mm(grad_small_in, s["normed"])
     norm_part = (
         mm_t(grad_query_low, w.query)
         + mm_t(grad_mamba, w.mamba)
         + mm_t(grad_shared, w.shared)
         + mm(grad_small_in, w.mixin_down)
     )
-    grad_entry = grad_hidden + norm_back(
-        s["entry"].astype(F32), low_sum(norm_part), w.mixer_gain
-    )
+    summed = low_sum(norm_part)
+    grads["query_up"] = t_mm(s["small_in"], grad_query_low)
+    grads["mamba_up"] = t_mm(s["small_in"], grad_mamba)
+    grads["shared_up"] = t_mm(s["small_in"], grad_shared)
+    grads["mixin_down"] = t_mm(grad_small_in, s["normed"])
+    grad_entry = grad_hidden + norm_back(s["entry"].astype(F32), summed, w.mixer_gain)
     return grad_entry, grads
 
 
@@ -556,7 +593,12 @@
     "feedout_down",
     "feedout_up",
 )
-REPLICATED = ("mixin_down", "shared_up", "mixout_up", "feedin_down", "feedout_up")
+PARTIAL = ("mixin_down", "shared_up")
+GROUPS = (
+    ("shared", "query", "mamba"),
+    ("attnout", "mambaout"),
+    ("gateup", "down"),
+)
 
 
 def shards(layer_input, cotangent, seq_lengths, adapter_ids, *params):
@@ -567,64 +609,88 @@
 
     place = Weights()
     place.wt = lax.axis_index("wt")
+    place.ctx = ctx_index
     length = seq_lengths[section]
     positions = ctx_index * span + jnp.arange(span, dtype=jnp.int32)
     place.live = (positions < length).astype(F32)
     place.tables = rope_tables(positions)
+    row = lax.broadcasted_iota(jnp.int32, (span, span), 0)
+    col = lax.broadcasted_iota(jnp.int32, (span, span), 1)
+    place.lower = (row >= col).astype(F32)
     blocks = jnp.minimum(
         ((ctx_index + 1) * span + KEY_BLOCK - 1) // KEY_BLOCK, (length + KEY_BLOCK - 1) // KEY_BLOCK
     )
     place.scalars = jnp.stack([length, ctx_index, blocks]).astype(jnp.int32)
 
-    own, other = {}, {}
-    shapes = {}
+    own, other, shapes = {}, {}, {}
     for name, item in zip(FIXED, params):
-        value = item[0]
-        if name in ("mamba", "gateup"):
-            value = value.reshape(value.shape[0], -1)
-        own[name] = value
-        other[name] = swap(value)
+        own[name] = item[0]
     mine, theirs = adapter_ids[section], adapter_ids[1 - section]
     for name, item in zip(ADAPTERS, params[len(FIXED) :]):
         shapes[name] = item.shape[1:]
-        flat = item[0].reshape(item.shape[1], item.shape[2], -1)
-        own[name] = lax.dynamic_index_in_dim(flat, mine, 0, keepdims=False)
-        other[name] = swap(lax.dynamic_index_in_dim(flat, theirs, 0, keepdims=False))
+        own[name] = lax.dynamic_index_in_dim(item[0], mine, 0, keepdims=False)
+        other[name] = swap(lax.dynamic_index_in_dim(item[0], theirs, 0, keepdims=False))
+    done = []
+    for group in GROUPS:
+        for name in group:
+            other[name] = swap(after(own[name], *done))
+        done = [other[name] for name in group]
+    for name in own:
+        if name not in other:
+            other[name] = swap(own[name])
 
     layers = []
     for index in range(2):
         w = Weights()
         for name in own:
-            setattr(w, name, jnp.where(section == index, own[name], other[name]))
+            value = jnp.where(section == index, own[name], other[name])
+            if value.ndim == 3:
+                value = value.reshape(value.shape[0], -1)
+            if name in FIXED[5:]:
+                value = lax.optimization_barrier(value)
+            setattr(w, name, value)
         layers.append(w)
 
     entry = lax.dynamic_index_in_dim(layer_input, section, 0, keepdims=False)
-    saved, outs = [], []
-    for w in layers:
-        result, kept = layer_forward(entry, w, place)
-        entry = result.astype(BF)
-        outs.append(entry)
-        saved.append(kept)
-
-    grad = lax.dynamic_index_in_dim(cotangent, section, 0, keepdims=False).astype(F32)
-    grad_lows, grad_sets = [None, None], [None, None]
-    for index in (1, 0):
-        grad, found = layer_backward(grad, layers[index], place, saved[index])
-        grad_low = grad.astype(BF)
-        grad_lows[index] = grad_low
-        grad = grad_low.astype(F32)
-        summed = {}
-        replicated = lax.psum(tuple(found[name] for name in REPLICATED), ("ctx", "wt"))
-        summed.update(zip(REPLICATED, replicated))
-        for name in ADAPTERS:
-            if name not in REPLICATED:
-                summed[name] = lax.psum(found[name].astype(BF), "ctx")
-        grad_sets[index] = summed
+    result, saved_first = layer_forward(entry, layers[0], place, False)
+    first_out = result.astype(BF)
+    last_part, saved_second = layer_forward(first_out, layers[1], place, True)
 
     def by_layer(values):
         keep = jnp.where(section == 0, values[0], values[1])
-        moved = swap(jnp.where(section == 0, values[1], values[0]))
-        return keep, moved
+        return keep, swap(jnp.where(section == 0, values[1], values[0]))
+
+    def reduced(found):
+        names = list(found)
+        packed = jnp.concatenate(
+            [found[name].astype(BF).reshape(found[name].shape[0], -1) for name in names], axis=1
+        )
+        return names, [found[name].shape[1] for name in names], packed
+
+    def summed_grads(found):
+        partial = {name: found[name] for name in found if name in PARTIAL}
+        whole = {name: found[name] for name in found if name not in PARTIAL}
+        names, widths, packed = reduced(whole)
+        if partial:
+            more, extra, part = reduced(partial)
+            names, widths = names + more, widths + extra
+            packed = jnp.concatenate([packed, exchange_sum(part, "wt")], axis=1)
+        return names, widths, exchange_sum(packed, "ctx")
+
+    grad = lax.dynamic_index_in_dim(cotangent, section, 0, keepdims=False).astype(F32)
+    kept_sets = []
+    grad_hidden, feed_grads = feed_backward(grad, layers[1], place, saved_second)
+    last_part = after(last_part, grad_hidden)
+    second_out = (saved_second["hidden"] + low_sum(last_part)).astype(BF)
+    grad, mixer_grads = mixer_backward(grad_hidden, layers[1], place, saved_second)
+    second_grad = grad.astype(BF)
+    second_sets = [summed_grads(feed_grads), summed_grads(mixer_grads)]
+
+    grad_hidden, feed_grads = feed_backward(second_grad.astype(F32), layers[0], place, saved_first)
+    first_sets = [summed_grads(feed_grads)]
+    grad, mixer_grads = mixer_backward(grad_hidden, layers[0], place, saved_first)
+    first_grad = grad.astype(BF)
+    first_sets.append(summed_grads(mixer_grads))
 
     def stacked(values):
         keep, moved = by_layer(values)
@@ -632,14 +698,21 @@
             [jnp.where(section == 0, keep, moved), jnp.where(section == 0, moved, keep)]
         )[None]
 
-    results = [stacked(outs), stacked(grad_lows)]
-    for name in ADAPTERS:
-        keep, moved = by_layer((grad_sets[0][name], grad_sets[1][name]))
-        shape = shapes[name]
-        total = jnp.zeros((shape[0],) + keep.shape, F32)
-        total = total.at[mine].add(keep.astype(F32)).at[theirs].add(moved.astype(F32))
-        results.append(total.reshape(shape)[None])
-    return tuple(results)
+    found = {}
+    adapters = jnp.arange(params[len(FIXED)].shape[1], dtype=jnp.int32)[:, None, None]
+    for first_set, second_set in zip(first_sets, second_sets):
+        keep, moved = by_layer((first_set[2], second_set[2]))
+        start = 0
+        for name, width in zip(first_set[0], first_set[1]):
+            lanes = slice(start, start + width)
+            start += width
+            total = jnp.where(adapters == mine, keep[None, :, lanes].astype(F32), 0.0)
+            total = total + jnp.where(adapters == theirs, moved[None, :, lanes].astype(F32), 0.0)
+            found[name] = total.reshape(shapes[name])[None]
+    return (
+        stacked((first_out, second_out)),
+        stacked((first_grad, second_grad)),
+    ) + tuple(found[name] for name in ADAPTERS)
 
 
 def solution(mesh):

time: 1110 us -> 956 us (0.86)
  waiting for transfers between devices: 518 us -> 373 us
  blocking collectives: 54.1 us -> 0 us
  other arithmetic: 124 us -> 173 us
  starting transfers between devices: 38.2 us -> 86.5 us
  matrix products: 211 us -> 164 us
    psum x3 -> x0, waiting for transfers between devices: 153 us -> none  [the longest x1 111 us: shards(): lax.psum(tuple((found[name] for name in REPLICATED)), ('ctx', 'wt'))]
    select_n x15, other arithmetic: 10.9 us -> 66.8 us  [the longest x11 56.7 us: shards(): value = jnp.where(section == index, own[name], other[name])]
    all_gather x4 -> x0, blocking collectives: 54.1 us -> none  [the longest x2 34 us: layer_forward(): key_all = lax.all_gather(key_value.astype(BF), 'ctx', axis=0, tiled=True)]
    psum x7, waiting for transfers between devices: 346 us -> 295 us  [low_sum(): return lax.psum(value.astype(BF), 'wt').astype(F32)]
    ppermute x12 -> x24, waiting for transfers between devices: 7.39 us -> 46.2 us  [shifted(): lax.ppermute(value, 'ctx', [(source, source + steps) for source in range(...]
    ppermute x0 -> x24, starting transfers between devices: none -> 31.4 us  [exchange_sum(): lax.ppermute(value, axis, [(place, place ^ bit) for place in range(count)])]
    ppermute x0 -> x24, waiting for transfers between devices: none -> 31.1 us  [exchange_sum(): lax.ppermute(value, axis, [(place, place ^ bit) for place in range(count)])]
    dot_general x40, matrix products: 92.7 us -> 65.2 us  [mm_t(): lax.dot_general(a.astype(BF), b.astype(BF), (((1,), (1,)), ((), ())), pre...]
  transfers between devices with their start and end apart: 60 -> 82, of which waited for: 13 -> 27; matrix products, arithmetic and copies ran while one was open for 27% -> 41% of each run, Pallas kernels for 2% -> 3%
where the time goes in v2:
time: 956 us; the launch traced here: 945 us
  waiting for transfers between devices  373 us (39%)
  other arithmetic  173 us (18%)
  matrix products  164 us (17%)
  local copies, waits for them, and re-layouts  97.8 us (10%)
  starting transfers between devices  86.5 us (9%)
  Pallas kernels  28.1 us (3%)
  between operations  22.9 us (2%)
    psum x7, waiting for transfers between devices, low_sum(): return lax.psum(value.astype(BF), 'wt').astype(F32)  295 us
    dot_general x40, matrix products, mm(): return jnp.dot(a.astype(BF), b.astype(BF), preferred_element_type=F32)  76.9 us
    dot_general x40, matrix products, mm_t(): lax.dot_general(a.astype(BF), b.astype(BF), (((1,), (1,)), ((), ())), pre...  65.2 us
    select_n x11, other arithmetic, shards(): value = jnp.where(section == index, own[name], other[name])  56.7 us
    ppermute x24, starting transfers between devices, shifted(): lax.ppermute(value, 'ctx', [(source, source + steps) for source in range(...  46.3 us
    ppermute x24, waiting for transfers between devices, shifted(): lax.ppermute(value, 'ctx', [(source, source + steps) for source in range(...  46.2 us
    unnamed x554, local copies, waits for them, and re-layouts  38.4 us
    ppermute x24, starting transfers between devices, exchange_sum(): lax.ppermute(value, axis, [(place, place ^ bit) for place in range(count)])  31.4 us
  transfers between devices with their start and end apart: 82, of which 27 were waited for; matrix products, arithmetic and copies ran while one was open for 41% of the time, Pallas kernels for 3%

profile of v2, /device:TPU:0, one launch (start us, length us, event | category | flops | bytes accessed | tf_op | source)
XLA Modules:
  0.0 945.3 jit_solution(15816164077874108558)
XLA Ops:
  47.0 4.8 broadcast_select_fusion.4
  51.9 4.6 fusion.319
  58.7 6.4 collective-permute-start.6
  79.3 13.0 %broadcast_select_fusion.2 = (bf16[2048,2,768]{2,1,0:T(2,128)(2,1)}, bf16[2048,2,768]{2,1,0:T(2,128)(2,1)S(1)}) fusion(bf16[2048,2,768]{2,1,0:T(2,128)(2,1)} %collective-permute-done.9, pred[]{:T(512)S(6)} %eq.23, bf16[1,2048,2,768]{3,2,1,0:T(2,128)(2,1)} %param.37, pred[]{:T(512)S(6)} %eq.22), kind=kLoop, calls=%fused_computation.2 | loop fusion | flops 6291456 | bytes 25165826 | tf_op jit(solution)/shard_map/jit(_where)/select_n | solution.py:646
  97.6 3.9 shard_map.355
  112.1 3.3 shard_map.354
  116.0 6.8 collective-permute-done.15
  133.5 5.3 broadcast_select_fusion.8
  150.4 45.9 %all-reduce.9.cloned.1.call-done = bf16[256,2048]{1,0:T(8,128)(2,1)} async-done(((bf16[256,2048]{1,0:T(8,128)(2,1)}), bf16[256,2048]{1,0:T(8,128)(2,1)}) %all-reduce.9.cloned.1.call-update) | async-done | bytes 1048592 | tf_op jit(solution)/shard_map/psum | solution.py:362
  201.2 6.5 broadcast_select_fusion.6
  208.2 16.5 %broadcast_select_fusion = (bf16[2048,2,1024]{2,1,0:T(2,128)(2,1)}, bf16[2048,2,1024]{2,1,0:T(2,128)(2,1)}) fusion(bf16[2048,2,1024]{2,1,0:T(2,128)(2,1)} %collective-permute-done.23, pred[]{:T(512)S(6)} %eq.23, bf16[1,2048,2,1024]{3,2,1,0:T(2,128)(2,1)S(1)} %bitcast.325, pred[]{:T(512)S(6)} %eq.22), kind=kLoop, calls=%fused_computation | loop fusion | flops 8388608 | bytes 33554432 | tf_op jit(solution)/shard_map/jit(_where)/select_n | solution.py:646
  224.7 10.3 %copy.192 = bf16[256,8,2,1024]{3,1,2,0:T(8,128)(2,1)} copy(bf16[256,8,2,1024]{3,2,1,0:T(2,128)(2,1)} %bitcast.320) | data formatting | bytes 16777216
  235.0 5.7 fusion.322
  249.5 6.8 copy.194
  256.3 43.6 %all-reduce.11.cloned.1.call-done = bf16[256,2048]{1,0:T(8,128)(2,1)} async-done(((bf16[256,2048]{1,0:T(8,128)(2,1)}), bf16[256,2048]{1,0:T(8,128)(2,1)}) %all-reduce.11.cloned.1.call-update) | async-done | bytes 1048592 | tf_op jit(solution)/shard_map/psum | solution.py:362
  305.2 3.8 fusion.320
  311.2 4.6 fusion.298
  318.0 4.0 shard_map.357
  323.9 4.1 collective-permute-start.32
  328.1 3.4 collective-permute-start.33
  354.8 3.3 shard_map.356
  383.9 10.3 %copy.196 = bf16[256,8,2,1024]{3,1,2,0:T(8,128)(2,1)} copy(bf16[256,8,2,1024]{3,2,1,0:T(2,128)(2,1)} %bitcast.319) | data formatting | bytes 16777216
  400.9 28.6 %all-reduce.13.cloned.1.call-done = bf16[256,2048]{1,0:T(8,128)(2,1)} async-done(((bf16[256,2048]{1,0:T(8,128)(2,1)}), bf16[256,2048]{1,0:T(8,128)(2,1)}) %all-reduce.13.cloned.1.call-update) | async-done | bytes 1048592 | tf_op jit(solution)/shard_map/psum | solution.py:362
  432.5 6.1 fusion.324
  460.0 4.4 collective-permute-done.71
  466.3 4.5 fusion.11
  471.5 32.6 %all-reduce.15.cloned.1.call-done = bf16[256,2048]{1,0:T(8,128)(2,1)} async-done(((bf16[256,2048]{1,0:T(8,128)(2,1)}), bf16[256,2048]{1,0:T(8,128)(2,1)}) %all-reduce.15.cloned.1.call-update) | async-done | bytes 1048592 | tf_op jit(solution)/shard_map/psum | solution.py:362
  514.5 3.8 shard_map.359
  542.3 7.0 collective-permute-done.36
  549.3 4.2 collective-permute-start.73
  553.6 7.7 collective-permute-done.37
  564.6 3.2 fusion.100
  580.7 3.8 fusion.296
  594.9 5.8 collective-permute-done.58
  601.4 40.0 %all-reduce.17.cloned.1.call-done = bf16[256,2048]{1,0:T(8,128)(2,1)} async-done(((bf16[256,2048]{1,0:T(8,128)(2,1)}), bf16[256,2048]{1,0:T(8,128)(2,1)}) %all-reduce.17.cloned.1.call-update) | async-done | bytes 1048592 | tf_op jit(solution)/shard_map/psum | solution.py:362
  666.5 5.7 fusion.91
  681.3 46.1 %all-reduce.19.cloned.1.call-done = bf16[256,2048]{1,0:T(8,128)(2,1)} async-done(((bf16[256,2048]{1,0:T(8,128)(2,1)}), bf16[256,2048]{1,0:T(8,128)(2,1)}) %all-reduce.19.cloned.1.call-update) | async-done | bytes 1048592 | tf_op jit(solution)/shard_map/psum | solution.py:362
  730.2 3.7 multiply_convert_fusion
  739.8 3.8 shard_map.361
  765.7 3.6 collective-permute-done.42
  769.4 15.4 %collective-permute-done.43 = bf16[272,768]{1,0:T(8,128)(2,1)S(1)} collective-permute-done((bf16[272,768]{1,0:T(8,128)(2,1)S(1)}, bf16[272,768]{1,0:T(8,128)(2,1)S(1)}, u32[]{:S(2)}, u32[]{:S(2)}) %collective-permute-start.43) | collective-permute-done | bytes 417824 | tf_op jit(solution)/shard_map/ppermute | solution.py:282
  785.2 3.5 fusion.66
  816.3 3.8 fusion.295
  822.3 4.9 collective-permute-done.52
  828.6 5.0 collective-permute-done.53
  835.3 4.9 collective-permute-done.54
  861.9 58.8 %all-reduce.21.cloned.1.call-done = (bf16[256,2048]{1,0:T(8,128)(2,1)}, bf16[256,2048]{1,0:T(8,128)(2,1)}) async-done(((bf16[256,2048]{1,0:T(8,128)(2,1)}, bf16[256,2048]{1,0:T(8,128)(2,1)}), (bf16[256,2048]{1,0:T(8,128)(2,1)}, bf16[256,2048]{1,0:T(8,128)(2,1)})) %all-reduce.21.cloned.1.call-update) | async-done | bytes 2097168 | tf_op jit(solution)/shard_map/psum | solution.py:362
  922.9 4.1 broadcast_select_fusion.13
  (1020 shorter events, 390.2 us)
Async XLA Ops:
  7.2 189.0 %all-reduce.9.cloned.1.call-start = ((), (), s32[]{:S(2)}) async-start(), calls=%async_computation | async-start | bytes 2097152 | tf_op jit(solution)/shard_map/psum | solution.py:362
  7.2 39.6 %collective-permute-start.9 = (bf16[2048,2,768]{2,1,0:T(2,128)(2,1)}, bf16[2048,2,768]{2,1,0:T(2,128)(2,1)}, u32[]{:S(2)}, u32[]{:S(2)}) collective-permute-start(bf16[2048,2,768]{2,1,0:T(2,128)(2,1)} %bitcast.340), channel_id=1, source_target_pairs={{0,16},{16,0},{1,17},{17,1},{2,18},{18,2},{3,19},{19,3},{4,20},{20... | collective-permute-start | bytes 18874376 | tf_op jit(solution)/shard_map/ppermute | solution.py:272
  7.8 39.1 %collective-permute-start.4 = (bf16[2048,1072]{0,1:T(8,128)(2,1)}, bf16[2048,1072]{0,1:T(8,128)(2,1)}, u32[]{:S(2)}, u32[]{:S(2)}) collective-permute-start(bf16[2048,1072]{0,1:T(8,128)(2,1)} %bitcast.341), channel_id=1, source_target_pairs={{0,16},{16,0},{1,17},{17,1},{2,18},{18,2},{3,19},{19,3},{4,20},{20... | collective-permute-start | bytes 13172744 | tf_op jit(solution)/shard_map/ppermute | solution.py:272
  11.9 27.1 %collective-permute-start.2 = (bf16[16,2048]{1,0:T(8,128)(2,1)S(1)}, bf16[16,2048]{1,0:T(8,128)(2,1)S(1)}, u32[]{:S(2)}, u32[]{:S(2)}) collective-permute-start(bf16[16,2048]{1,0:T(8,128)(2,1)S(1)} %dynamic-slice_bitcast_fusion.4), channel_id=1, source_target_pairs={{0,16},{16,0},{1,17},{17,1},{2,18},{18,2},{3,19},{19,3},{4,20},{20... | collective-permute-start | bytes 196616 | tf_op jit(solution)/shard_map/ppermute | solution.py:272
  13.1 23.2 %collective-permute-start = (bf16[2048]{0:T(1024)(128)(2,1)S(1)}, bf16[2048]{0:T(1024)(128)(2,1)S(1)}, u32[]{:S(2)}, u32[]{:S(2)}) collective-permute-start(bf16[2048]{0:T(1024)(128)(2,1)S(1)} %reduce.2), channel_id=1, source_target_pairs={{0,16},{16,0},{1,17},{17,1},{2,18},{18,2},{3,19},{19,3},{4,20},{20... | collective-permute-start | bytes 12296 | tf_op jit(solution)/shard_map/ppermute | solution.py:272
  13.3 18.1 %collective-permute-start.12 = (f32[12]{0:T(128)}, f32[12]{0:T(128)S(1)}, u32[]{:S(2)}, u32[]{:S(2)}) collective-permute-start(f32[12]{0:T(128)} %bitcast.369), channel_id=1, source_target_pairs={{0,16},{16,0},{1,17},{17,1},{2,18},{18,2},{3,19},{19,3},{4,20},{20... | collective-permute-start | bytes 152 | tf_op jit(solution)/shard_map/ppermute | solution.py:272
  46.9 31.9 %collective-permute-start.18 = (bf16[768,2048]{1,0:T(8,128)(2,1)}, bf16[768,2048]{1,0:T(8,128)(2,1)}, u32[]{:S(2)}, u32[]{:S(2)}) collective-permute-start(bf16[768,2048]{1,0:T(8,128)(2,1)} %bitcast.24), channel_id=1, source_target_pairs={{0,16},{16,0},{1,17},{17,1},{2,18},{18,2},{3,19},{19,3},{4,20},{20... | collective-permute-start | bytes 9437192 | tf_op jit(solution)/shard_map/ppermute | solution.py:272
  58.7 46.2 %collective-permute-start.6 = (bf16[256,256]{1,0:T(8,128)(2,1)}, bf16[256,256]{1,0:T(8,128)(2,1)}, u32[]{:S(2)}, u32[]{:S(2)}) collective-permute-start(bf16[256,256]{1,0:T(8,128)(2,1)} %pad_maximum_fusion.28), channel_id=1, source_target_pairs={{0,12},{1,13},{2,14},{3,15},{16,28},{17,29},{18,30},{19,31}} | collective-permute-start | bytes 393224 | tf_op jit(solution)/shard_map/ppermute | solution.py:282
  65.1 42.1 %collective-permute-start.7 = (bf16[256,256]{1,0:T(8,128)(2,1)}, bf16[256,256]{1,0:T(8,128)(2,1)}, u32[]{:S(2)}, u32[]{:S(2)}) collective-permute-start(bf16[256,256]{1,0:T(8,128)(2,1)} %pad_maximum_fusion.28), channel_id=1, source_target_pairs={{0,8},{4,12},{1,9},{5,13},{2,10},{6,14},{3,11},{7,15},{16,24},{20,... | collective-permute-start | bytes 393224 | tf_op jit(solution)/shard_map/ppermute | solution.py:282
  67.0 43.1 %collective-permute-start.8 = (bf16[256,256]{1,0:T(8,128)(2,1)}, bf16[256,256]{1,0:T(8,128)(2,1)}, u32[]{:S(2)}, u32[]{:S(2)}) collective-permute-start(bf16[256,256]{1,0:T(8,128)(2,1)} %pad_maximum_fusion.28), channel_id=1, source_target_pairs={{0,4},{4,8},{8,12},{1,5},{5,9},{9,13},{2,6},{6,10},{10,14},{3,7},{... | collective-permute-start | bytes 393224 | tf_op jit(solution)/shard_map/ppermute | solution.py:282
  78.8 128.9 %collective-permute-start.23 = (bf16[2048,2,1024]{2,1,0:T(2,128)(2,1)}, bf16[2048,2,1024]{2,1,0:T(2,128)(2,1)}, u32[]{:S(2)}, u32[]{:S(2)}) collective-permute-start(bf16[2048,2,1024]{2,1,0:T(2,128)(2,1)} %bitcast.323), channel_id=1, source_target_pairs={{0,16},{16,0},{1,17},{17,1},{2,18},{18,2},{3,19},{19,3},{4,20},{20... | collective-permute-start | bytes 25165832 | tf_op jit(solution)/shard_map/ppermute | solution.py:272
  103.5 11.9 %collective-permute-start.14 = (bf16[272,768]{1,0:T(8,128)(2,1)}, bf16[272,768]{1,0:T(8,128)(2,1)S(1)}, u32[]{:S(2)}, u32[]{:S(2)}) collective-permute-start(bf16[272,768]{1,0:T(8,128)(2,1)} %fusion.86), channel_id=1, source_target_pairs={{0,4},{4,8},{8,12},{1,5},{5,9},{9,13},{2,6},{6,10},{10,14},{3,7},{... | collective-permute-start | bytes 1253384 | tf_op jit(solution)/shard_map/ppermute | solution.py:282
  104.8 18.0 %collective-permute-start.15 = (bf16[272,768]{1,0:T(8,128)(2,1)}, bf16[272,768]{1,0:T(8,128)(2,1)S(1)}, u32[]{:S(2)}, u32[]{:S(2)}) collective-permute-start(bf16[272,768]{1,0:T(8,128)(2,1)} %fusion.86), channel_id=1, source_target_pairs={{0,8},{4,12},{1,9},{5,13},{2,10},{6,14},{3,11},{7,15},{16,24},{20,... | collective-permute-start | bytes 1253384 | tf_op jit(solution)/shard_map/ppermute | solution.py:282
  107.1 16.3 %collective-permute-start.16 = (bf16[272,768]{1,0:T(8,128)(2,1)}, bf16[272,768]{1,0:T(8,128)(2,1)}, u32[]{:S(2)}, u32[]{:S(2)}) collective-permute-start(bf16[272,768]{1,0:T(8,128)(2,1)} %fusion.86), channel_id=1, source_target_pairs={{0,12},{1,13},{2,14},{3,15},{16,28},{17,29},{18,30},{19,31}} | collective-permute-start | bytes 1253384 | tf_op jit(solution)/shard_map/ppermute | solution.py:282
  110.1 17.0 %collective-permute-start.20 = (bf16[16,768]{1,0:T(8,128)(2,1)S(1)}, bf16[16,768]{1,0:T(8,128)(2,1)S(1)}, u32[]{:S(2)}, u32[]{:S(2)}) collective-permute-start(bf16[16,768]{1,0:T(8,128)(2,1)S(1)} %copy-done.213), channel_id=1, source_target_pairs={{0,16},{16,0},{1,17},{17,1},{2,18},{18,2},{3,19},{19,3},{4,20},{20... | collective-permute-start | bytes 73736 | tf_op jit(solution)/shard_map/ppermute | solution.py:272
  115.4 12.7 %collective-permute-start.19 = (bf16[16,256]{1,0:T(8,128)(2,1)S(1)}, bf16[16,256]{1,0:T(8,128)(2,1)S(1)}, u32[]{:S(2)}, u32[]{:S(2)}) collective-permute-start(bf16[16,256]{1,0:T(8,128)(2,1)S(1)} %copy-done.229), channel_id=1, source_target_pairs={{0,16},{16,0},{1,17},{17,1},{2,18},{18,2},{3,19},{19,3},{4,20},{20... | collective-permute-start | bytes 24584 | tf_op jit(solution)/shard_map/ppermute | solution.py:272
  123.4 24.2 %collective-permute-start.22 = (bf16[2048]{0:T(1024)(128)(2,1)S(1)}, bf16[2048]{0:T(1024)(128)(2,1)S(1)}, u32[]{:S(2)}, u32[]{:S(2)}) collective-permute-start(bf16[2048]{0:T(1024)(128)(2,1)S(1)} %copy-done.223), channel_id=1, source_target_pairs={{0,16},{16,0},{1,17},{17,1},{2,18},{18,2},{3,19},{19,3},{4,20},{20... | collective-permute-start | bytes 12296 | tf_op jit(solution)/shard_map/ppermute | solution.py:272
  130.4 70.8 %collective-permute-start.26 = (bf16[1024,2048]{1,0:T(8,128)(2,1)}, bf16[1024,2048]{1,0:T(8,128)(2,1)}, u32[]{:S(2)}, u32[]{:S(2)}) collective-permute-start(bf16[1024,2048]{1,0:T(8,128)(2,1)} %bitcast.36), channel_id=1, source_target_pairs={{0,16},{16,0},{1,17},{17,1},{2,18},{18,2},{3,19},{19,3},{4,20},{20... | collective-permute-start | bytes 12582920 | tf_op jit(solution)/shard_map/ppermute | solution.py:272
  142.0 157.9 %all-reduce.11.cloned.1.call-start = ((), (), s32[]{:S(2)}) async-start(), calls=%async_computation.1 | async-start | bytes 2097152 | tf_op jit(solution)/shard_map/psum | solution.py:362
  143.9 55.3 %collective-permute-start.24 = (bf16[16,2048]{1,0:T(8,128)(2,1)}, bf16[16,2048]{1,0:T(8,128)(2,1)S(1)}, u32[]{:S(2)}, u32[]{:S(2)}) collective-permute-start(bf16[16,2048]{1,0:T(8,128)(2,1)} %dynamic-slice_bitcast_fusion.2), channel_id=1, source_target_pairs={{0,16},{16,0},{1,17},{17,1},{2,18},{18,2},{3,19},{19,3},{4,20},{20... | collective-permute-start | bytes 196616 | tf_op jit(solution)/shard_map/ppermute | solution.py:272
  147.6 95.2 %collective-permute-start.27 = (bf16[16,1024]{1,0:T(8,128)(2,1)S(1)}, bf16[16,1024]{1,0:T(8,128)(2,1)S(1)}, u32[]{:S(2)}, u32[]{:S(2)}) collective-permute-start(bf16[16,1024]{1,0:T(8,128)(2,1)S(1)} %dynamic-slice_bitcast_fusion.7), channel_id=1, source_target_pairs={{0,16},{16,0},{1,17},{17,1},{2,18},{18,2},{3,19},{19,3},{4,20},{20... | collective-permute-start | bytes 98312 | tf_op jit(solution)/shard_map/ppermute | solution.py:272
  148.4 95.9 %collective-permute-start.28 = (bf16[16,2048]{1,0:T(8,128)(2,1)}, bf16[16,2048]{1,0:T(8,128)(2,1)S(1)}, u32[]{:S(2)}, u32[]{:S(2)}) collective-permute-start(bf16[16,2048]{1,0:T(8,128)(2,1)} %dynamic-slice_bitcast_fusion), channel_id=1, source_target_pairs={{0,16},{16,0},{1,17},{17,1},{2,18},{18,2},{3,19},{19,3},{4,20},{20... | collective-permute-start | bytes 196616 | tf_op jit(solution)/shard_map/ppermute | solution.py:272
  248.5 180.9 %all-reduce.13.cloned.1.call-start = ((), (), s32[]{:S(2)}) async-start(), calls=%async_computation.2 | async-start | bytes 2097152 | tf_op jit(solution)/shard_map/psum | solution.py:362
  323.9 34.1 %collective-permute-start.32 = (bf16[272,768]{1,0:T(8,128)(2,1)}, bf16[272,768]{1,0:T(8,128)(2,1)}, u32[]{:S(2)}, u32[]{:S(2)}) collective-permute-start(bf16[272,768]{1,0:T(8,128)(2,1)} %fusion.84), channel_id=1, source_target_pairs={{0,4},{4,8},{8,12},{1,5},{5,9},{9,13},{2,6},{6,10},{10,14},{3,7},{... | collective-permute-start | bytes 1253384 | tf_op jit(solution)/shard_map/ppermute | solution.py:282
  328.1 31.1 %collective-permute-start.33 = (bf16[272,768]{1,0:T(8,128)(2,1)}, bf16[272,768]{1,0:T(8,128)(2,1)}, u32[]{:S(2)}, u32[]{:S(2)}) collective-permute-start(bf16[272,768]{1,0:T(8,128)(2,1)} %fusion.84), channel_id=1, source_target_pairs={{0,8},{4,12},{1,9},{5,13},{2,10},{6,14},{3,11},{7,15},{16,24},{20,... | collective-permute-start | bytes 1253384 | tf_op jit(solution)/shard_map/ppermute | solution.py:282
  331.5 28.9 %collective-permute-start.34 = (bf16[272,768]{1,0:T(8,128)(2,1)}, bf16[272,768]{1,0:T(8,128)(2,1)}, u32[]{:S(2)}, u32[]{:S(2)}) collective-permute-start(bf16[272,768]{1,0:T(8,128)(2,1)} %fusion.84), channel_id=1, source_target_pairs={{0,12},{1,13},{2,14},{3,15},{16,28},{17,29},{18,30},{19,31}} | collective-permute-start | bytes 1253384 | tf_op jit(solution)/shard_map/ppermute | solution.py:282
  341.3 10.8 %collective-permute-start.30 = (bf16[256,256]{1,0:T(8,128)(2,1)}, bf16[256,256]{1,0:T(8,128)(2,1)}, u32[]{:S(2)}, u32[]{:S(2)}) collective-permute-start(bf16[256,256]{1,0:T(8,128)(2,1)} %pad_maximum_fusion.29), channel_id=1, source_target_pairs={{0,8},{4,12},{1,9},{5,13},{2,10},{6,14},{3,11},{7,15},{16,24},{20,... | collective-permute-start | bytes 393224 | tf_op jit(solution)/shard_map/ppermute | solution.py:282
  369.9 134.3 %all-reduce.15.cloned.1.call-start = ((), (), s32[]{:S(2)}) async-start(), calls=%async_computation.3 | async-start | bytes 2097152 | tf_op jit(solution)/shard_map/psum | solution.py:362
  374.8 19.4 %collective-permute-start.62 = (f32[256,16]{0,1:T(8,128)S(1)}, f32[256,16]{0,1:T(8,128)S(1)}, u32[]{:S(2)}, u32[]{:S(2)}) collective-permute-start(f32[256,16]{0,1:T(8,128)S(1)} %copy-done.155), channel_id=1, source_target_pairs={{0,1},{1,0},{2,3},{3,2},{4,5},{5,4},{6,7},{7,6},{8,9},{9,8},{10,11... | collective-permute-start | bytes 49160 | tf_op jit(solution)/shard_map/ppermute | solution.py:289
  376.4 22.1 %collective-permute-start.55 = (f32[256,16]{0,1:T(8,128)S(1)}, f32[256,16]{0,1:T(8,128)S(1)}, u32[]{:S(2)}, u32[]{:S(2)}) collective-permute-start(f32[256,16]{0,1:T(8,128)S(1)} %convolution_add_fusion.30), channel_id=1, source_target_pairs={{0,1},{1,0},{2,3},{3,2},{4,5},{5,4},{6,7},{7,6},{8,9},{9,8},{10,11... | collective-permute-start | bytes 49160 | tf_op jit(solution)/shard_map/ppermute | solution.py:289
  382.1 373.4 %collective-permute-start.50 = (f32[256,16]{0,1:T(8,128)}, f32[256,16]{0,1:T(8,128)}, u32[]{:S(2)}, u32[]{:S(2)}) collective-permute-start(f32[256,16]{0,1:T(8,128)} %add.878), channel_id=1, source_target_pairs={{0,2},{1,3},{2,0},{3,1},{4,6},{5,7},{6,4},{7,5},{8,10},{9,11},{10,... | collective-permute-start | bytes 49160 | tf_op jit(solution)/shard_map/ppermute | solution.py:289
  394.8 256.7 %collective-permute-start.63 = (f32[256,16]{0,1:T(8,128)}, f32[256,16]{0,1:T(8,128)}, u32[]{:S(2)}, u32[]{:S(2)}) collective-permute-start(f32[256,16]{0,1:T(8,128)} %add.897), channel_id=1, source_target_pairs={{0,2},{1,3},{2,0},{3,1},{4,6},{5,7},{6,4},{7,5},{8,10},{9,11},{10,... | collective-permute-start | bytes 49160 | tf_op jit(solution)/shard_map/ppermute | solution.py:289
  399.1 130.7 %collective-permute-start.56 = (f32[256,16]{0,1:T(8,128)}, f32[256,16]{0,1:T(8,128)}, u32[]{:S(2)}, u32[]{:S(2)}) collective-permute-start(f32[256,16]{0,1:T(8,128)} %add.884), channel_id=1, source_target_pairs={{0,2},{1,3},{2,0},{3,1},{4,6},{5,7},{6,4},{7,5},{8,10},{9,11},{10,... | collective-permute-start | bytes 49160 | tf_op jit(solution)/shard_map/ppermute | solution.py:289
  451.8 189.6 %all-reduce.17.cloned.1.call-start = ((), (), s32[]{:S(2)}) async-start(), calls=%async_computation.4 | async-start | bytes 2097152 | tf_op jit(solution)/shard_map/psum | solution.py:362
  535.3 14.0 %collective-permute-start.36 = (bf16[272,768]{1,0:T(8,128)(2,1)}, bf16[272,768]{1,0:T(8,128)(2,1)S(1)}, u32[]{:S(2)}, u32[]{:S(2)}) collective-permute-start(bf16[272,768]{1,0:T(8,128)(2,1)} %fusion.85), channel_id=1, source_target_pairs={{4,0},{8,4},{12,8},{5,1},{9,5},{13,9},{6,2},{10,6},{14,10},{7,3},{... | collective-permute-start | bytes 1253384 | tf_op jit(solution)/shard_map/ppermute | solution.py:282
  536.6 24.7 %collective-permute-start.37 = (bf16[272,768]{1,0:T(8,128)(2,1)}, bf16[272,768]{1,0:T(8,128)(2,1)S(1)}, u32[]{:S(2)}, u32[]{:S(2)}) collective-permute-start(bf16[272,768]{1,0:T(8,128)(2,1)} %fusion.85), channel_id=1, source_target_pairs={{8,0},{12,4},{9,1},{13,5},{10,2},{14,6},{11,3},{15,7},{24,16},{28,... | collective-permute-start | bytes 1253384 | tf_op jit(solution)/shard_map/ppermute | solution.py:282
  539.2 22.2 %collective-permute-start.38 = (bf16[272,768]{1,0:T(8,128)(2,1)}, bf16[272,768]{1,0:T(8,128)(2,1)S(1)}, u32[]{:S(2)}, u32[]{:S(2)}) collective-permute-start(bf16[272,768]{1,0:T(8,128)(2,1)} %fusion.85), channel_id=1, source_target_pairs={{12,0},{13,1},{14,2},{15,3},{28,16},{29,17},{30,18},{31,19}} | collective-permute-start | bytes 1253384 | tf_op jit(solution)/shard_map/ppermute | solution.py:282
  549.3 122.9 %collective-permute-start.73 = (bf16[16,7168]{1,0:T(8,128)(2,1)}, bf16[16,7168]{1,0:T(8,128)(2,1)}, u32[]{:S(2)}, u32[]{:S(2)}) collective-permute-start(bf16[16,7168]{1,0:T(8,128)(2,1)} %add_convert_fusion.7), channel_id=1, source_target_pairs={{0,8},{4,12},{8,0},{12,4},{1,9},{5,13},{9,1},{13,5},{2,10},{6,14},... | collective-permute-start | bytes 688136 | tf_op jit(solution)/shard_map/ppermute | solution.py:289
  591.8 135.6 %all-reduce.19.cloned.1.call-start = ((), (), s32[]{:S(2)}) async-start(), calls=%async_computation.5 | async-start | bytes 2097152 | tf_op jit(solution)/shard_map/psum | solution.py:362
  601.4 58.9 %collective-permute-start.59 = (bf16[16,7984]{1,0:T(8,128)(2,1)}, bf16[16,7984]{1,0:T(8,128)(2,1)S(1)}, u32[]{:S(2)}, u32[]{:S(2)}) collective-permute-start(bf16[16,7984]{1,0:T(8,128)(2,1)} %fusion.201), channel_id=1, source_target_pairs={{0,4},{4,0},{8,12},{12,8},{1,5},{5,1},{9,13},{13,9},{2,6},{6,2},{1... | collective-permute-start | bytes 766472 | tf_op jit(solution)/shard_map/ppermute | solution.py:289
  662.0 173.3 %collective-permute-start.60 = (bf16[16,7984]{1,0:T(8,128)(2,1)}, bf16[16,7984]{1,0:T(8,128)(2,1)}, u32[]{:S(2)}, u32[]{:S(2)}) collective-permute-start(bf16[16,7984]{1,0:T(8,128)(2,1)} %add_convert_fusion.3), channel_id=1, source_target_pairs={{0,8},{4,12},{8,0},{12,4},{1,9},{5,13},{9,1},{13,5},{2,10},{6,14},... | collective-permute-start | bytes 766472 | tf_op jit(solution)/shard_map/ppermute | solution.py:289
  677.0 243.7 %all-reduce.21.cloned.1.call-start = ((), (), s32[]{:S(2)}) async-start(), calls=%async_computation.6 | async-start | bytes 4194304 | tf_op jit(solution)/shard_map/psum | solution.py:362
  749.8 11.1 %collective-permute-start.45 = (bf16[256,256]{1,0:T(8,128)(2,1)S(1)}, bf16[256,256]{1,0:T(8,128)(2,1)S(1)}, u32[]{:S(2)}, u32[]{:S(2)}) collective-permute-start(bf16[256,256]{1,0:T(8,128)(2,1)S(1)} %get-tuple-element.134), channel_id=1, source_target_pairs={{4,0},{8,4},{12,8},{5,1},{9,5},{13,9},{6,2},{10,6},{14,10},{7,3},{... | collective-permute-start | bytes 393224 | tf_op jit(solution)/shard_map/ppermute | solution.py:282
  751.1 11.6 %collective-permute-start.46 = (bf16[256,256]{1,0:T(8,128)(2,1)S(1)}, bf16[256,256]{1,0:T(8,128)(2,1)S(1)}, u32[]{:S(2)}, u32[]{:S(2)}) collective-permute-start(bf16[256,256]{1,0:T(8,128)(2,1)S(1)} %get-tuple-element.136), channel_id=1, source_target_pairs={{8,0},{12,4},{9,1},{13,5},{10,2},{14,6},{11,3},{15,7},{24,16},{28,... | collective-permute-start | bytes 393224 | tf_op jit(solution)/shard_map/ppermute | solution.py:282
  752.4 11.6 %collective-permute-start.47 = (bf16[256,256]{1,0:T(8,128)(2,1)S(1)}, bf16[256,256]{1,0:T(8,128)(2,1)S(1)}, u32[]{:S(2)}, u32[]{:S(2)}) collective-permute-start(bf16[256,256]{1,0:T(8,128)(2,1)S(1)} %get-tuple-element.135), channel_id=1, source_target_pairs={{12,0},{13,1},{14,2},{15,3},{28,16},{29,17},{30,18},{31,19}} | collective-permute-start | bytes 393224 | tf_op jit(solution)/shard_map/ppermute | solution.py:282
  755.5 13.8 %collective-permute-start.42 = (bf16[272,768]{1,0:T(8,128)(2,1)S(1)}, bf16[272,768]{1,0:T(8,128)(2,1)S(1)}, u32[]{:S(2)}, u32[]{:S(2)}) collective-permute-start(bf16[272,768]{1,0:T(8,128)(2,1)S(1)} %fusion.87), channel_id=1, source_target_pairs={{4,0},{8,4},{12,8},{5,1},{9,5},{13,9},{6,2},{10,6},{14,10},{7,3},{... | collective-permute-start | bytes 1253384 | tf_op jit(solution)/shard_map/ppermute | solution.py:282
  760.9 23.9 %collective-permute-start.43 = (bf16[272,768]{1,0:T(8,128)(2,1)S(1)}, bf16[272,768]{1,0:T(8,128)(2,1)S(1)}, u32[]{:S(2)}, u32[]{:S(2)}) collective-permute-start(bf16[272,768]{1,0:T(8,128)(2,1)S(1)} %fusion.87), channel_id=1, source_target_pairs={{8,0},{12,4},{9,1},{13,5},{10,2},{14,6},{11,3},{15,7},{24,16},{28,... | collective-permute-start | bytes 1253384 | tf_op jit(solution)/shard_map/ppermute | solution.py:282
  762.7 22.2 %collective-permute-start.44 = (bf16[272,768]{1,0:T(8,128)(2,1)S(1)}, bf16[272,768]{1,0:T(8,128)(2,1)S(1)}, u32[]{:S(2)}, u32[]{:S(2)}) collective-permute-start(bf16[272,768]{1,0:T(8,128)(2,1)S(1)} %fusion.87), channel_id=1, source_target_pairs={{12,0},{13,1},{14,2},{15,3},{28,16},{29,17},{30,18},{31,19}} | collective-permute-start | bytes 1253384 | tf_op jit(solution)/shard_map/ppermute | solution.py:282
  (307 other events, 4052.5 us)
Sparse Core Ops, SparseCore 0:
  142.1 54.0 all-reduce.8
  248.7 51.1 all-reduce.10
  370.0 59.4 all-reduce.12
  452.0 52.1 all-reduce.14
  591.9 49.4 all-reduce.16
  677.1 50.2 all-reduce.18
  835.4 85.2 all-reduce.20

commit v3 on v2

--- a/solution.py
+++ b/solution.py
@@ -152,6 +152,102 @@
     )(x, dy_low, b_low, c_low, dt, cum, cumt)
 
 
+def scan_close_kernel(
+    x_ref,
+    dy_ref,
+    z_ref,
+    y_ref,
+    b_ref,
+    grad_state_ref,
+    state_ref,
+    db_ref,
+    dc_ref,
+    dt_ref,
+    cum_ref,
+    step_ref,
+    live_ref,
+    rate_ref,
+    skip_ref,
+    dx_ref,
+    db_out_ref,
+    dc_out_ref,
+    dstep_ref,
+    through_scr,
+    step_scr,
+    edge_scr,
+    tail_scr,
+    grown_scr,
+):
+    rows, width = x_ref.shape
+    heads = dt_ref.shape[1]
+    cum = cum_ref[...]
+    dt = dt_ref[...]
+    last = cum[rows - 1 : rows, :]
+    tail = jnp.exp(last - cum)
+    grown = jnp.exp(cum)
+    whole = jnp.exp(last)
+    for pair in range(heads // 2):
+        one, two = 2 * pair, 2 * pair + 1
+        lanes = slice(PAIR * pair, PAIR * (pair + 1))
+        dt_pair = pair_lanes(rows, dt[:, one : one + 1], dt[:, two : two + 1])
+        tail_pair = pair_lanes(rows, tail[:, one : one + 1], tail[:, two : two + 1])
+        grown_pair = pair_lanes(rows, grown[:, one : one + 1], grown[:, two : two + 1])
+        whole_pair = pair_lanes(1, whole[:, one : one + 1], whole[:, two : two + 1])
+        x = x_ref[:, lanes]
+        dy = dy_ref[:, lanes].astype(F32)
+        grad_state = grad_state_ref[:, lanes]
+        z_tail = tail_pair * mm(b_ref[...], grad_state)
+        z_all = z_ref[:, lanes] + z_tail
+        dx_ref[:, lanes] = (dt_pair * z_all + skip_ref[:, lanes] * dy).astype(dx_ref.dtype)
+        scaled = (x * dt_pair).astype(BF).astype(F32)
+        tail_scr[:, lanes] = (tail_pair * scaled).astype(BF)
+        grown_scr[:, lanes] = (grown_pair * dy).astype(BF)
+        through_scr[:, lanes] = dy * y_ref[:, lanes] - scaled * z_all
+        step_scr[:, lanes] = x * z_all
+        kept = jnp.sum(
+            grad_state.astype(F32) * state_ref[:, lanes].astype(F32), axis=0, keepdims=True
+        )
+        edge = jnp.sum(scaled * z_tail, axis=0, keepdims=True) + kept * whole_pair
+        edge_scr[:, lanes] = jnp.broadcast_to(edge, (edge_scr.shape[0], PAIR))
+    db_out_ref[...] = (db_ref[...] + mm_t(tail_scr[...], grad_state_ref[...])).astype(BF)
+    dc_out_ref[...] = (dc_ref[...] + mm_t(grown_scr[...], state_ref[...])).astype(BF)
+    lane = lax.broadcasted_iota(jnp.int32, (width, heads), 0)
+    head = lax.broadcasted_iota(jnp.int32, (width, heads), 1)
+    member = ((lane >= head * MHEAD) & (lane < (head + 1) * MHEAD)).astype(F32)
+    row = lax.broadcasted_iota(jnp.int32, (rows, rows), 0)
+    col = lax.broadcasted_iota(jnp.int32, (rows, rows), 1)
+    later = (col >= row).astype(F32)
+
+    def exact(a, b):
+        return jnp.dot(a, b, precision=HIGH, preferred_element_type=F32)
+
+    cum_grad = exact(later, exact(through_scr[...], member))
+    cum_grad = cum_grad + exact(edge_scr[...], member)[0:1, :]
+    grad_steps = exact(step_scr[...], member) - rate_ref[...] * cum_grad
+    dstep_ref[...] = grad_steps * live_ref[...] / (1.0 + jnp.exp(-step_ref[...]))
+
+
+def scan_close(x, dy_low, z, y, b_low, grad_state, state, db, dc, dt, cum, step, live, rate, skip):
+    rows, width = x.shape
+    states, heads = b_low.shape[1], dt.shape[1]
+    return vmem_call(
+        scan_close_kernel,
+        (
+            jax.ShapeDtypeStruct((rows, width), BF),
+            jax.ShapeDtypeStruct((rows, states), BF),
+            jax.ShapeDtypeStruct((rows, states), BF),
+            jax.ShapeDtypeStruct((rows, heads), F32),
+        ),
+        scratch_shapes=[
+            pltpu.VMEM((rows, width), F32),
+            pltpu.VMEM((rows, width), F32),
+            pltpu.VMEM((8, width), F32),
+            pltpu.VMEM((rows, width), BF),
+            pltpu.VMEM((rows, width), BF),
+        ],
+    )(x, dy_low, z, y, b_low, grad_state, state, db, dc, dt, cum, step, live, rate, skip)
+
+
 def block_mask(scores_shape, span, block, ctx_index, length):
     row = lax.broadcasted_iota(jnp.int32, scores_shape, 0)
     query_pos = ctx_index * span + lax.rem(row, span)
@@ -363,11 +459,13 @@
 
 
 class Weights:
-    pass
-
-
-def layer_forward(entry_low, w, place, last):
-    saved = {"entry": entry_low}
+    def keep(self, **values):
+        self.__dict__.update(values)
+
+
+def mixer_forward(entry_low, w, place):
+    saved = Weights()
+    saved.entry = entry_low
     entry = entry_low.astype(F32)
     normed = (entry * rms_scale(entry) * w.mixer_gain).astype(BF)
     small_in = mm_t(normed, w.mixin_down).astype(BF)
@@ -412,17 +510,7 @@
     part = (
         mm(attended_low, w.attnout) + mm(gated_low, w.mambaout) + mm(small_mid, w.mixout_up)
     )
-    hidden = entry + place.live[:, None] * low_sum(part)
-
-    feed_normed = (hidden * rms_scale(hidden) * w.feed_gain).astype(BF)
-    small_feed = mm_t(feed_normed, w.feedin_down).astype(BF)
-    gateup = mm(feed_normed, w.gateup) + mm(small_feed, w.feedin_up)
-    width = gateup.shape[1] // 2
-    gate_value, up_value = gateup[:, :width], gateup[:, width:]
-    inner = (jax.nn.silu(gate_value) * up_value).astype(BF)
-    small_out = mm_t(inner, w.feedout_down)
-    feed_part = (mm(inner, w.down) + mm(small_out, w.feedout_up)).astype(BF)
-    saved.update(
+    saved.keep(
         normed=normed,
         small_in=small_in,
         query_rows=query_rows,
@@ -441,50 +529,71 @@
         lse=lse,
         gated_low=gated_low,
         attended_low=attended_low,
-        small_mid=exchange_sum(small_mid, "wt"),
+        small_mid=small_mid,
+    )
+    return part.astype(BF), saved
+
+
+def feed_forward(entry_low, part, w, place, saved):
+    mixed = after(lax.psum(part, "wt"), w.gateup, w.down)
+    hidden = entry_low.astype(F32) + place.live[:, None] * mixed.astype(F32)
+    feed_normed = (hidden * rms_scale(hidden) * w.feed_gain).astype(BF)
+    small_feed = mm_t(feed_normed, w.feedin_down).astype(BF)
+    gateup = mm(feed_normed, w.gateup) + mm(small_feed, w.feedin_up)
+    width = gateup.shape[1] // 2
+    gate_value, up_value = gateup[:, :width], gateup[:, width:]
+    inner = (jax.nn.silu(gate_value) * up_value).astype(BF)
+    small_out = mm_t(inner, w.feedout_down)
+    feed_part = (mm(inner, w.down) + mm(small_out, w.feedout_up)).astype(BF)
+    saved.keep(
         hidden=hidden,
         feed_normed=feed_normed,
         small_feed=small_feed,
         gate_value=gate_value,
         up_value=up_value,
         inner=inner,
-        small_out=exchange_sum(small_out, "wt"),
-    )
-    if last:
-        return feed_part, saved
-    return hidden + low_sum(feed_part), saved
-
-
-def feed_backward(grad_out, w, place, s):
-    grads = {}
+        small_out=small_out,
+    )
+    return feed_part
+
+
+def feed_backward(grad_out, w, place, s, finish):
+    grads = Weights()
     grad_feed = grad_out.astype(BF)
     grad_small_out = mm_t(grad_feed, w.feedout_up)
-    grads["feedout_up"] = t_mm(s["small_out"], grad_feed)
-    grads["feedout_down"] = t_mm(grad_small_out, s["inner"])
     grad_inner = mm_t(grad_feed, w.down) + mm(grad_small_out, w.feedout_down)
-    gate_value, up_value = s["gate_value"], s["up_value"]
+    gate_value, up_value = s.gate_value, s.up_value
     sigmoid_gate = jax.nn.sigmoid(gate_value)
     grad_gate = grad_inner * up_value * sigmoid_gate * (1.0 + gate_value * (1.0 - sigmoid_gate))
     grad_up = grad_inner * gate_value * sigmoid_gate
     grad_gateup = jnp.concatenate([grad_gate, grad_up], axis=1).astype(BF)
     grad_small_feed = mm_t(grad_gateup, w.feedin_up)
-    grads["feedin_up"] = t_mm(s["small_feed"], grad_gateup)
     feed_norm_part = mm_t(grad_gateup, w.gateup) + mm(grad_small_feed, w.feedin_down)
-    summed = low_sum(feed_norm_part)
-    grads["feedin_down"] = t_mm(exchange_sum(grad_small_feed, "wt"), s["feed_normed"])
-    return grad_out + norm_back(s["hidden"], summed, w.feed_gain), grads
-
-
-def mixer_backward(grad_hidden, w, place, s):
-    grads = {}
+    summed = lax.psum(feed_norm_part.astype(BF), "wt")
+    small_all = exchange_sum(
+        jnp.concatenate(
+            [part.astype(BF) for part in (s.small_mid, s.small_out, grad_small_feed)], axis=1
+        ),
+        "wt",
+    )
+    rank = grad_small_feed.shape[1]
+    s.small_mid = small_all[:, :rank]
+    grads.feedout_up = t_mm(small_all[:, rank : 2 * rank], grad_feed)
+    grads.feedout_down = t_mm(grad_small_out, s.inner)
+    grads.feedin_up = t_mm(s.small_feed, grad_gateup)
+    grads.feedin_down = t_mm(small_all[:, 2 * rank :], s.feed_normed)
+    found = finish(grads)
+    summed = after(summed, found[2]).astype(F32)
+    return grad_out + norm_back(s.hidden, summed, w.feed_gain), found
+
+
+def mixer_backward(grad_hidden, w, place, s, finish, before=()):
+    grads = Weights()
     span = grad_hidden.shape[0]
     grad_mixed = (grad_hidden * place.live[:, None]).astype(BF)
     grad_small_mid = mm_t(grad_mixed, w.mixout_up)
-    grads["mixout_up"] = t_mm(s["small_mid"], grad_mixed)
-    grads["attnout_down"] = t_mm(grad_small_mid, s["attended_low"])
-    grads["mambaout_down"] = t_mm(grad_small_mid, s["gated_low"])
     grad_gated = mm_t(grad_mixed, w.mambaout) + mm(grad_small_mid, w.mambaout_down)
-    gate_raw, inputs, scanned = s["gate_raw"], s["inputs"], s["scanned"]
+    gate_raw, inputs, scanned = s.gate_raw, s.inputs, s.scanned
     skip = jnp.repeat(w.skip_gain, MHEAD)[None, :]
     sigmoid_raw = jax.nn.sigmoid(gate_raw)
     silu_raw = gate_raw * sigmoid_raw
@@ -493,45 +602,49 @@
     grad_gates = (
         grad_gated * (scanned + skip * inputs) * sigmoid_raw * (1.0 + gate_raw * (1.0 - sigmoid_raw))
     )
-    cum, step_sizes = s["cum"], s["step_sizes"]
+    cum, step_sizes = s.cum, s.step_sizes
     grown = wide(jnp.exp(cum))
     grown_dy = (grown * dy).astype(BF)
-    local_grad = t_mm(s["output_map"], grown_dy)
-    grad_state = carried_states(state_payload(local_grad, cum[-1]), NSTATE, True).astype(BF)
+    local_grad = t_mm(s.output_map, grown_dy)
+    payload = state_payload(local_grad, cum[-1])
+    grad_state = carried_states(payload, NSTATE, True).astype(BF)
+    dy_now, grad_mid, small_now = lax.optimization_barrier(
+        (dy_low, grad_mixed, grad_small_mid, payload)
+    )[:3]
 
     grad_attended = (
-        mm_t(grad_mixed, w.attnout) + mm(grad_small_mid, w.attnout_down)
+        mm_t(grad_mid, w.attnout) + mm(small_now, w.attnout_down)
     ).astype(BF)
     grad_query, grad_keyval = attend_backward(
-        place.scalars, s["query_rows"], s["key_all"], s["lse"], s["attended"], grad_attended
-    )
-    own = returned_rows(grad_keyval, span, place.ctx)
+        place.scalars, s.query_rows, s.key_all, s.lse, s.attended, grad_attended
+    )
+    own = returned_rows(after(grad_keyval, grad_state), span, place.ctx)
 
     z_local, db_local, dc_local = scan_backward(
-        inputs, dy_low, s["input_map"], s["output_map"], step_sizes, cum, cum.T
-    )
-    dt_wide = wide(step_sizes)
-    tail = wide(jnp.exp(cum[-1:] - cum))
-    scaled_low = (inputs * dt_wide).astype(BF)
-    scaled = scaled_low.astype(F32)
-    z_tail = tail * mm(s["input_map"], grad_state)
-    z_all = z_local + z_tail
-    grad_inputs = dt_wide * z_all + skip * dy
-    grad_map_in = db_local + mm_t((tail * scaled), grad_state)
-    grad_map_out = dc_local + mm_t(grown_dy, s["state_in"])
-    kept = jnp.sum(
-        grad_state.astype(F32) * s["state_in"].astype(F32), axis=0
-    )[None, :] * jnp.repeat(jnp.exp(cum[-1]), MHEAD)[None, :]
-    edge = head_sum(jnp.sum(scaled * z_tail, axis=0, keepdims=True) + kept)
-    through = head_sum(dy * scanned - scaled * z_all)
-    cum_grad = edge + jnp.dot(place.lower.T, through, precision=HIGH)
-    grad_steps = head_sum(inputs * z_all) - w.decay_rate * cum_grad
-    grad_step = grad_steps * jax.nn.sigmoid(s["step_in"]) * place.live[:, None]
+        inputs, dy_now, s.input_map, s.output_map, step_sizes, cum, cum.T
+    )
+    grad_inputs, grad_map_in, grad_map_out, grad_step = scan_close(
+        inputs,
+        dy_low,
+        z_local,
+        scanned,
+        s.input_map,
+        grad_state,
+        s.state_in,
+        db_local,
+        dc_local,
+        step_sizes,
+        cum,
+        s.step_in,
+        place.live[:, None],
+        w.decay_rate[None, :],
+        skip,
+    )
 
     heads = cum.shape[1]
     grad_query_low = rotate(grad_query, place.tables, -1.0).astype(BF)
     grad_keys = rotate(own[:, :HEAD], place.tables, -1.0)
-    key_head = s["key_head"]
+    key_head = s.key_head
     offset = 2 * KVHEADS * HEAD
     keyval = jnp.zeros((span, offset), F32)
     keyval = lax.dynamic_update_slice_in_dim(keyval, grad_keys, key_head * HEAD, 1)
@@ -543,9 +656,9 @@
         jnp.zeros((span, all_heads), F32), grad_step, place.wt * heads, 1
     )
     grad_shared = jnp.concatenate(
-        [keyval, grad_map_in, grad_map_out, step_part], axis=1
-    ).astype(BF)
-    grad_mamba = jnp.concatenate([grad_gates, grad_inputs], axis=1).astype(BF)
+        [keyval.astype(BF), grad_map_in, grad_map_out, step_part.astype(BF)], axis=1
+    )
+    grad_mamba = jnp.concatenate([grad_gates.astype(BF), grad_inputs], axis=1)
     grad_small_in = (
         mm_t(grad_query_low, w.query_up)
         + mm_t(grad_mamba, w.mamba_up)
@@ -557,13 +670,20 @@
         + mm_t(grad_shared, w.shared)
         + mm(grad_small_in, w.mixin_down)
     )
-    summed = low_sum(norm_part)
-    grads["query_up"] = t_mm(s["small_in"], grad_query_low)
-    grads["mamba_up"] = t_mm(s["small_in"], grad_mamba)
-    grads["shared_up"] = t_mm(s["small_in"], grad_shared)
-    grads["mixin_down"] = t_mm(grad_small_in, s["normed"])
-    grad_entry = grad_hidden + norm_back(s["entry"].astype(F32), summed, w.mixer_gain)
-    return grad_entry, grads
+    norm_part = after(norm_part.astype(BF), *before)
+    summed = lax.psum(norm_part, "wt")
+    grads.mixout_up = t_mm(s.small_mid, grad_mixed)
+    grads.attnout_down = t_mm(grad_small_mid, s.attended_low)
+    grads.mambaout_down = t_mm(grad_small_mid, s.gated_low)
+    grads.query_up = t_mm(s.small_in, grad_query_low)
+    grads.mamba_up = t_mm(s.small_in, grad_mamba)
+    grads.shared_up = t_mm(s.small_in, grad_shared)
+    grads.mixin_down = t_mm(grad_small_in, s.normed)
+    found = finish(grads, *((summed,) if before else ()))
+    grad_entry = grad_hidden + norm_back(
+        s.entry.astype(F32), summed.astype(F32), w.mixer_gain
+    )
+    return grad_entry, found
 
 
 FIXED = (
@@ -594,6 +714,11 @@
     "feedout_up",
 )
 PARTIAL = ("mixin_down", "shared_up")
+PACKS = (
+    ("mixin_down", "mamba_up", "query_up", "shared_up"),
+    ("mixout_up", "mambaout_down", "attnout_down"),
+    ("feedin_down", "feedin_up", "feedout_up", "feedout_down"),
+)
 GROUPS = (
     ("shared", "query", "mamba"),
     ("attnout", "mambaout"),
@@ -622,43 +747,72 @@
     )
     place.scalars = jnp.stack([length, ctx_index, blocks]).astype(jnp.int32)
 
-    own, other, shapes = {}, {}, {}
+    own, items, shapes = {}, {}, {}
     for name, item in zip(FIXED, params):
         own[name] = item[0]
     mine, theirs = adapter_ids[section], adapter_ids[1 - section]
     for name, item in zip(ADAPTERS, params[len(FIXED) :]):
         shapes[name] = item.shape[1:]
-        own[name] = lax.dynamic_index_in_dim(item[0], mine, 0, keepdims=False)
-        other[name] = swap(lax.dynamic_index_in_dim(item[0], theirs, 0, keepdims=False))
+        items[name] = item[0]
+    layers = (Weights(), Weights())
+
+    def packed_items(names, which):
+        return jnp.concatenate(
+            [
+                lax.dynamic_index_in_dim(items[name], which, 0, keepdims=False).reshape(
+                    items[name].shape[1], -1
+                )
+                for name in names
+            ],
+            axis=1,
+        )
+
+    def place_pack(names, widths, kept, moved):
+        for index, w in enumerate(layers):
+            value = jnp.where(section == index, kept, moved)
+            start = 0
+            for name, width in zip(names, widths):
+                setattr(w, name, value[..., start : start + width])
+                start += width
+
+    def exchange_pack(number, *gates):
+        names = PACKS[number]
+        widths = [items[name][0, 0].size for name in names]
+        moved = swap(after(packed_items(names, theirs), *gates))
+        place_pack(names, widths, packed_items(names, mine), moved)
+
+    vectors = FIXED[:5]
+    joined = jnp.concatenate([own[name].astype(F32) for name in vectors])
+    place_pack(vectors, [own[name].size for name in vectors], joined, swap(joined))
+    exchange_pack(0)
     done = []
     for group in GROUPS:
+        moved = {name: swap(after(own[name], *done)) for name in group}
+        done = done or list(moved.values())
         for name in group:
-            other[name] = swap(after(own[name], *done))
-        done = [other[name] for name in group]
-    for name in own:
-        if name not in other:
-            other[name] = swap(own[name])
-
-    layers = []
-    for index in range(2):
-        w = Weights()
-        for name in own:
-            value = jnp.where(section == index, own[name], other[name])
-            if value.ndim == 3:
-                value = value.reshape(value.shape[0], -1)
-            if name in FIXED[5:]:
-                value = lax.optimization_barrier(value)
-            setattr(w, name, value)
-        layers.append(w)
-
+            for index, w in enumerate(layers):
+                value = jnp.where(section == index, own[name], moved[name])
+                if value.ndim == 3:
+                    value = value.reshape(value.shape[0], -1)
+                setattr(w, name, lax.optimization_barrier(value))
+    exchange_pack(1, *done)
+
+    first, second = layers
     entry = lax.dynamic_index_in_dim(layer_input, section, 0, keepdims=False)
-    result, saved_first = layer_forward(entry, layers[0], place, False)
-    first_out = result.astype(BF)
-    last_part, saved_second = layer_forward(first_out, layers[1], place, True)
-
-    def by_layer(values):
-        keep = jnp.where(section == 0, values[0], values[1])
-        return keep, swap(jnp.where(section == 0, values[1], values[0]))
+    part, saved_first = mixer_forward(entry, first, place)
+    exchange_pack(2, part)
+    feed_part = feed_forward(entry, part, first, place, saved_first)
+    following = [getattr(second, name) for name in GROUPS[0] + GROUPS[1]]
+    fed = after(lax.psum(feed_part, "wt"), *following)
+    first_out = (saved_first.hidden + fed.astype(F32)).astype(BF)
+    part, saved_second = mixer_forward(first_out, second, place)
+    last_part = feed_forward(first_out, part, second, place, saved_second)
+
+    def forth(value):
+        return lax.ppermute(value, "section", [(0, 1)])
+
+    def back(value):
+        return lax.ppermute(value, "section", [(1, 0)])
 
     def reduced(found):
         names = list(found)
@@ -667,41 +821,47 @@
         )
         return names, [found[name].shape[1] for name in names], packed
 
-    def summed_grads(found):
+    def summed_grads(grads, *gates):
+        found = vars(grads)
         partial = {name: found[name] for name in found if name in PARTIAL}
         whole = {name: found[name] for name in found if name not in PARTIAL}
         names, widths, packed = reduced(whole)
+        packed = after(packed, *gates)
         if partial:
             more, extra, part = reduced(partial)
+            part = after(part, *gates)
             names, widths = names + more, widths + extra
             packed = jnp.concatenate([packed, exchange_sum(part, "wt")], axis=1)
         return names, widths, exchange_sum(packed, "ctx")
 
     grad = lax.dynamic_index_in_dim(cotangent, section, 0, keepdims=False).astype(F32)
-    kept_sets = []
-    grad_hidden, feed_grads = feed_backward(grad, layers[1], place, saved_second)
+    grad_hidden, found = feed_backward(grad, second, place, saved_second, summed_grads)
+    second_sets = [found]
     last_part = after(last_part, grad_hidden)
-    second_out = (saved_second["hidden"] + low_sum(last_part)).astype(BF)
-    grad, mixer_grads = mixer_backward(grad_hidden, layers[1], place, saved_second)
+    second_out = (saved_second.hidden + low_sum(last_part)).astype(BF)
+    grad, found = mixer_backward(
+        grad_hidden, second, place, saved_second, summed_grads, (second_out,)
+    )
     second_grad = grad.astype(BF)
-    second_sets = [summed_grads(feed_grads), summed_grads(mixer_grads)]
-
-    grad_hidden, feed_grads = feed_backward(second_grad.astype(F32), layers[0], place, saved_first)
-    first_sets = [summed_grads(feed_grads)]
-    grad, mixer_grads = mixer_backward(grad_hidden, layers[0], place, saved_first)
+    second_sets.append(found)
+    grad_hidden, found = feed_backward(
+        second_grad.astype(F32), first, place, saved_first, summed_grads
+    )
+    first_sets = [found]
+    grad, found = mixer_backward(grad_hidden, first, place, saved_first, summed_grads)
     first_grad = grad.astype(BF)
-    first_sets.append(summed_grads(mixer_grads))
-
-    def stacked(values):
-        keep, moved = by_layer(values)
-        return jnp.stack(
-            [jnp.where(section == 0, keep, moved), jnp.where(section == 0, moved, keep)]
+    first_sets.append(found)
+
+    def stacked(early, late):
+        return jnp.where(
+            section == 0, jnp.stack([early, back(early)]), jnp.stack([forth(late), late])
         )[None]
 
     found = {}
     adapters = jnp.arange(params[len(FIXED)].shape[1], dtype=jnp.int32)[:, None, None]
     for first_set, second_set in zip(first_sets, second_sets):
-        keep, moved = by_layer((first_set[2], second_set[2]))
+        keep = jnp.where(section == 0, first_set[2], second_set[2])
+        moved = jnp.where(section == 0, back(first_set[2]), forth(second_set[2]))
         start = 0
         for name, width in zip(first_set[0], first_set[1]):
             lanes = slice(start, start + width)
@@ -710,8 +870,8 @@
             total = total + jnp.where(adapters == theirs, moved[None, :, lanes].astype(F32), 0.0)
             found[name] = total.reshape(shapes[name])[None]
     return (
-        stacked((first_out, second_out)),
-        stacked((first_grad, second_grad)),
+        stacked(first_out, second_out),
+        stacked(first_grad, second_grad),
     ) + tuple(found[name] for name in ADAPTERS)
 
 

time: 956 us -> 844 us (0.88)
  waiting for transfers between devices: 373 us -> 288 us
  matrix products: 164 us -> 141 us
  Pallas kernels: 28.1 us -> 45.1 us
  other arithmetic: 173 us -> 156 us
    psum x7 -> x1, waiting for transfers between devices: 295 us -> 0.01 us  [low_sum(): return lax.psum(value.astype(BF), 'wt').astype(F32)]
    psum x0 -> x7, waiting for transfers between devices: none -> 214 us  [the longest x2 84.6 us: mixer_backward(): summed = lax.psum(norm_part, 'wt')]
    dot_general x40 -> x38, matrix products: 76.9 us -> 59.6 us  [mm(): return jnp.dot(a.astype(BF), b.astype(BF), preferred_element_type=F32)]
    pallas_call x0 -> x2, Pallas kernels: none -> 16.5 us  [scan_close(): vmem_call(scan_close_kernel, (jax.ShapeDtypeStruct((rows, width), BF), ja...]
    ppermute x0 -> x8, starting transfers between devices: none -> 15.5 us  [the longest x4 9.61 us: forth(): return lax.ppermute(value, 'section', [(0, 1)])]
    ppermute x24, waiting for transfers between devices: 46.2 us -> 31.5 us  [shifted(): lax.ppermute(value, 'ctx', [(source, source + steps) for source in range(...]
    dot_general x40 -> x36, matrix products: 65.2 us -> 55.6 us  [mm_t(): lax.dot_general(a.astype(BF), b.astype(BF), (((1,), (1,)), ((), ())), pre...]
    ppermute x24 -> x16, waiting for transfers between devices: 31.1 us -> 39.8 us  [exchange_sum(): lax.ppermute(value, axis, [(place, place ^ bit) for place in range(count)])]
  transfers between devices with their start and end apart: 82 -> 67, of which waited for: 27 -> 25; matrix products, arithmetic and copies ran while one was open for 41% -> 39% of each run, Pallas kernels for 3% -> 5%
where the time goes in v3:
time: 844 us; the launch traced here: 834 us
  waiting for transfers between devices  288 us (34%)
  other arithmetic  156 us (18%)
  matrix products  141 us (17%)
  starting transfers between devices  93.7 us (11%)
  local copies, waits for them, and re-layouts  88.3 us (10%)
  Pallas kernels  45.1 us (5%)
  between operations  21.7 us (3%)
    psum x2, waiting for transfers between devices, mixer_backward(): summed = lax.psum(norm_part, 'wt')  84.6 us
    dot_general x38, matrix products, mm(): return jnp.dot(a.astype(BF), b.astype(BF), preferred_element_type=F32)  59.6 us
    dot_general x36, matrix products, mm_t(): lax.dot_general(a.astype(BF), b.astype(BF), (((1,), (1,)), ((), ())), pre...  55.6 us
    ppermute x24, starting transfers between devices, shifted(): lax.ppermute(value, 'ctx', [(source, source + steps) for source in range(...  51.1 us
    psum x2, waiting for transfers between devices, feed_forward(): mixed = after(lax.psum(part, 'wt'), w.gateup, w.down)  49.9 us
    select_n x7, other arithmetic, shards(): value = jnp.where(section == index, own[name], moved[name])  48 us
    unnamed x422, local copies, waits for them, and re-layouts  44.8 us
    psum x1, waiting for transfers between devices, shards(): fed = after(lax.psum(feed_part, 'wt'), *following)  43.6 us
  transfers between devices with their start and end apart: 67, of which 25 were waited for; matrix products, arithmetic and copies ran while one was open for 39% of the time, Pallas kernels for 5%

profile of v3, /device:TPU:0, one launch (start us, length us, event | category | flops | bytes accessed | tf_op | source)
XLA Modules:
  0.0 833.6 jit_solution(5779832219618619653)
XLA Ops:
  42.2 4.9 broadcast_select_fusion.4
  51.1 5.1 collective-permute-start.5
  71.3 3.5 shard_map.354
  75.5 12.9 %broadcast_select_fusion.2 = (bf16[2048,2,768]{2,1,0:T(2,128)(2,1)}, bf16[2048,2,768]{2,1,0:T(2,128)(2,1)S(1)}) fusion(bf16[2048,2,768]{2,1,0:T(2,128)(2,1)} %collective-permute-done.7, pred[]{:T(512)S(6)} %eq.23, bf16[1,2048,2,768]{3,2,1,0:T(2,128)(2,1)} %param.37, pred[]{:T(512)S(6)} %eq.22), kind=kLoop, calls=%fused_computation.2 | loop fusion | flops 6291456 | bytes 25165826 | tf_op jit(solution)/shard_map/jit(_where)/select_n | solution.py:794
  94.5 4.2 shard_map.355
  99.9 6.0 collective-permute-start.11
  110.4 15.2 %collective-permute-done.10 = bf16[272,768]{1,0:T(8,128)(2,1)S(1)} collective-permute-done((bf16[272,768]{1,0:T(8,128)(2,1)S(1)}, bf16[272,768]{1,0:T(8,128)(2,1)S(1)}, u32[]{:S(2)}, u32[]{:S(2)}) %collective-permute-start.10) | collective-permute-done | bytes 417824 | tf_op jit(solution)/shard_map/ppermute | solution.py:378
  132.8 4.0 broadcast_select_fusion.8
  142.6 5.9 broadcast_select_fusion.6
  148.5 16.7 %broadcast_select_fusion = (bf16[2048,2,1024]{2,1,0:T(2,128)(2,1)}, bf16[2048,2,1024]{2,1,0:T(2,128)(2,1)}) fusion(bf16[2048,2,1024]{2,1,0:T(2,128)(2,1)} %collective-permute-done.14, pred[]{:T(512)S(6)} %eq.23, bf16[1,2048,2,1024]{3,2,1,0:T(2,128)(2,1)} %param.41, pred[]{:T(512)S(6)} %eq.22), kind=kLoop, calls=%fused_computation | loop fusion | flops 8388608 | bytes 33554432 | tf_op jit(solution)/shard_map/jit(_where)/select_n | solution.py:794
  165.2 10.2 %copy.85 = bf16[256,8,2,1024]{3,1,2,0:T(8,128)(2,1)} copy(bf16[256,8,2,1024]{3,2,1,0:T(2,128)(2,1)} %bitcast.239) | data formatting | bytes 16777216
  175.5 18.6 %all-reduce.9.cloned.1.call-done = bf16[256,2048]{1,0:T(8,128)(2,1)} async-done(((bf16[256,2048]{1,0:T(8,128)(2,1)}), bf16[256,2048]{1,0:T(8,128)(2,1)}) %all-reduce.9.cloned.1.call-update) | async-done | bytes 1048592 | tf_op jit(solution)/shard_map/psum | solution.py:538
  197.1 6.1 fusion.332
  211.2 6.8 copy.88
  217.9 43.6 %all-reduce.11.cloned.1.call-done = bf16[256,2048]{1,0:T(8,128)(2,1)} async-done(((bf16[256,2048]{1,0:T(8,128)(2,1)}), bf16[256,2048]{1,0:T(8,128)(2,1)}) %all-reduce.11.cloned.1.call-update) | async-done | bytes 1048592 | tf_op jit(solution)/shard_map/psum | solution.py:806
  266.2 4.6 fusion.329
  280.5 4.2 collective-permute-start.20
  284.6 3.4 collective-permute-start.19
  290.0 5.8 fusion.309
  301.6 3.9 shard_map.357
  321.7 3.5 shard_map.356
  325.2 3.7 collective-permute-done.22
  346.3 10.2 %copy.89 = bf16[256,8,2,1024]{3,1,2,0:T(8,128)(2,1)} copy(bf16[256,8,2,1024]{3,2,1,0:T(2,128)(2,1)} %bitcast.238) | data formatting | bytes 16777216
  358.3 31.3 %all-reduce.13.cloned.1.call-done = bf16[256,2048]{1,0:T(8,128)(2,1)} async-done(((bf16[256,2048]{1,0:T(8,128)(2,1)}), bf16[256,2048]{1,0:T(8,128)(2,1)}) %all-reduce.13.cloned.1.call-update) | async-done | bytes 1048592 | tf_op jit(solution)/shard_map/psum | solution.py:538
  393.6 5.9 fusion.334
  426.1 3.3 collective-permute-done.26
  440.4 29.3 %all-reduce.15.cloned.1.call-done = bf16[256,2048]{1,0:T(8,128)(2,1)} async-done(((bf16[256,2048]{1,0:T(8,128)(2,1)}), bf16[256,2048]{1,0:T(8,128)(2,1)}) %all-reduce.15.cloned.1.call-update) | async-done | bytes 1048592 | tf_op jit(solution)/shard_map/psum | solution.py:572
  472.2 3.8 multiply_convert_fusion.1
  498.9 3.8 shard_map.359
  503.6 3.9 collective-permute-done.30
  516.5 8.3 shard_map.360
  524.8 6.1 fusion.81
  538.4 4.0 fusion.307
  553.9 48.6 %all-reduce.19.cloned.1.call-done = bf16[256,2048]{1,0:T(8,128)(2,1)} async-done(((bf16[256,2048]{1,0:T(8,128)(2,1)}), bf16[256,2048]{1,0:T(8,128)(2,1)}) %all-reduce.19.cloned.1.call-update) | async-done | bytes 1048592 | tf_op jit(solution)/shard_map/psum | solution.py:674
  617.0 5.8 fusion.74
  625.7 3.7 maximum_select_fusion
  631.0 5.1 collective-permute-done.36
  640.5 9.8 %collective-permute-done.52 = bf16[16,3120]{1,0:T(8,128)(2,1)S(1)} collective-permute-done((bf16[16,3120]{1,0:T(8,128)(2,1)S(1)}, bf16[16,3120]{1,0:T(8,128)(2,1)S(1)}, u32[]{:S(2)}, u32[]{:S(2)}) %collective-permute-start.52) | collective-permute-done | bytes 99872 | tf_op jit(solution)/shard_map/ppermute | solution.py:385
  673.9 6.3 all-reduce.21.cloned.1.call-done
  682.3 3.7 multiply_convert_fusion
  701.6 3.8 shard_map.362
  705.7 8.6 %collective-permute-done.40 = bf16[272,768]{1,0:T(8,128)(2,1)S(1)} collective-permute-done((bf16[272,768]{1,0:T(8,128)(2,1)S(1)}, bf16[272,768]{1,0:T(8,128)(2,1)S(1)}, u32[]{:S(2)}, u32[]{:S(2)}) %collective-permute-start.40) | collective-permute-done | bytes 417824 | tf_op jit(solution)/shard_map/ppermute | solution.py:378
  720.0 8.2 shard_map.363
  728.3 6.1 fusion.79
  741.3 3.9 collective-permute-done.47
  746.6 3.8 fusion.306
  755.0 4.9 collective-permute-done.49
  778.8 36.0 %all-reduce.23.cloned.1.call-done = bf16[256,2048]{1,0:T(8,128)(2,1)} async-done(((bf16[256,2048]{1,0:T(8,128)(2,1)}), bf16[256,2048]{1,0:T(8,128)(2,1)}) %all-reduce.23.cloned.1.call-update) | async-done | bytes 1048592 | tf_op jit(solution)/shard_map/psum | solution.py:674
  (825 shorter events, 351.0 us)
Async XLA Ops:
  7.2 186.9 %all-reduce.9.cloned.1.call-start = ((), (), s32[]{:S(2)}) async-start(), calls=%async_computation | async-start | bytes 2097152 | tf_op jit(solution)/shard_map/psum | solution.py:538
  9.4 25.4 %collective-permute-start = (f32[4132]{0:T(1024)S(1)}, f32[4132]{0:T(1024)S(1)}, u32[]{:S(2)}, u32[]{:S(2)}) collective-permute-start(f32[4132]{0:T(1024)S(1)} %concatenate.155), channel_id=1, source_target_pairs={{0,16},{16,0},{1,17},{17,1},{2,18},{18,2},{3,19},{19,3},{4,20},{20... | collective-permute-start | bytes 49592 | tf_op jit(solution)/shard_map/ppermute | solution.py:368
  19.8 17.1 %collective-permute-start.2 = (bf16[16,4912]{1,0:T(8,128)(2,1)S(1)}, bf16[16,4912]{1,0:T(8,128)(2,1)S(1)}, u32[]{:S(2)}, u32[]{:S(2)}) collective-permute-start(bf16[16,4912]{1,0:T(8,128)(2,1)S(1)} %pad_maximum_fusion.33), channel_id=1, source_target_pairs={{0,16},{16,0},{1,17},{17,1},{2,18},{18,2},{3,19},{19,3},{4,20},{20... | collective-permute-start | bytes 471560 | tf_op jit(solution)/shard_map/ppermute | solution.py:368
  19.8 18.8 %collective-permute-start.1 = (bf16[2048,256]{1,0:T(8,128)(2,1)}, bf16[2048,256]{1,0:T(8,128)(2,1)}, u32[]{:S(2)}, u32[]{:S(2)}) collective-permute-start(bf16[2048,256]{1,0:T(8,128)(2,1)} %bitcast.261), channel_id=1, source_target_pairs={{0,16},{16,0},{1,17},{17,1},{2,18},{18,2},{3,19},{19,3},{4,20},{20... | collective-permute-start | bytes 3145736 | tf_op jit(solution)/shard_map/ppermute | solution.py:368
  20.3 21.8 %collective-permute-start.3 = (bf16[2048,1072]{0,1:T(8,128)(2,1)}, bf16[2048,1072]{0,1:T(8,128)(2,1)}, u32[]{:S(2)}, u32[]{:S(2)}) collective-permute-start(bf16[2048,1072]{0,1:T(8,128)(2,1)} %bitcast.254), channel_id=1, source_target_pairs={{0,16},{16,0},{1,17},{17,1},{2,18},{18,2},{3,19},{19,3},{4,20},{20... | collective-permute-start | bytes 13172744 | tf_op jit(solution)/shard_map/ppermute | solution.py:368
  20.4 54.4 %collective-permute-start.7 = (bf16[2048,2,768]{2,1,0:T(2,128)(2,1)}, bf16[2048,2,768]{2,1,0:T(2,128)(2,1)}, u32[]{:S(2)}, u32[]{:S(2)}) collective-permute-start(bf16[2048,2,768]{2,1,0:T(2,128)(2,1)} %bitcast.253), channel_id=1, source_target_pairs={{0,16},{16,0},{1,17},{17,1},{2,18},{18,2},{3,19},{19,3},{4,20},{20... | collective-permute-start | bytes 18874376 | tf_op jit(solution)/shard_map/ppermute | solution.py:368
  51.1 17.4 %collective-permute-start.5 = (bf16[256,256]{1,0:T(8,128)(2,1)S(1)}, bf16[256,256]{1,0:T(8,128)(2,1)}, u32[]{:S(2)}, u32[]{:S(2)}) collective-permute-start(bf16[256,256]{1,0:T(8,128)(2,1)S(1)} %pad_maximum_fusion.34), channel_id=1, source_target_pairs={{0,8},{4,12},{1,9},{5,13},{2,10},{6,14},{3,11},{7,15},{16,24},{20,... | collective-permute-start | bytes 393224 | tf_op jit(solution)/shard_map/ppermute | solution.py:378
  56.3 11.2 %collective-permute-start.4 = (bf16[256,256]{1,0:T(8,128)(2,1)S(1)}, bf16[256,256]{1,0:T(8,128)(2,1)}, u32[]{:S(2)}, u32[]{:S(2)}) collective-permute-start(bf16[256,256]{1,0:T(8,128)(2,1)S(1)} %pad_maximum_fusion.34), channel_id=1, source_target_pairs={{0,12},{1,13},{2,14},{3,15},{16,28},{17,29},{18,30},{19,31}} | collective-permute-start | bytes 393224 | tf_op jit(solution)/shard_map/ppermute | solution.py:378
  74.8 32.3 %collective-permute-start.13 = (bf16[16,3072]{1,0:T(8,128)(2,1)S(1)}, bf16[16,3072]{1,0:T(8,128)(2,1)S(1)}, u32[]{:S(2)}, u32[]{:S(2)}) collective-permute-start(bf16[16,3072]{1,0:T(8,128)(2,1)S(1)} %copy-done.120), channel_id=1, source_target_pairs={{0,16},{16,0},{1,17},{17,1},{2,18},{18,2},{3,19},{19,3},{4,20},{20... | collective-permute-start | bytes 294920 | tf_op jit(solution)/shard_map/ppermute | solution.py:368
  74.9 56.4 %collective-permute-start.12 = (bf16[768,2048]{1,0:T(8,128)(2,1)}, bf16[768,2048]{1,0:T(8,128)(2,1)}, u32[]{:S(2)}, u32[]{:S(2)}) collective-permute-start(bf16[768,2048]{1,0:T(8,128)(2,1)} %bitcast.260), channel_id=1, source_target_pairs={{0,16},{16,0},{1,17},{17,1},{2,18},{18,2},{3,19},{19,3},{4,20},{20... | collective-permute-start | bytes 9437192 | tf_op jit(solution)/shard_map/ppermute | solution.py:368
  75.4 73.1 %collective-permute-start.14 = (bf16[2048,2,1024]{2,1,0:T(2,128)(2,1)}, bf16[2048,2,1024]{2,1,0:T(2,128)(2,1)}, u32[]{:S(2)}, u32[]{:S(2)}) collective-permute-start(bf16[2048,2,1024]{2,1,0:T(2,128)(2,1)} %bitcast.242), channel_id=1, source_target_pairs={{0,16},{16,0},{1,17},{17,1},{2,18},{18,2},{3,19},{19,3},{4,20},{20... | collective-permute-start | bytes 25165832 | tf_op jit(solution)/shard_map/ppermute | solution.py:368
  99.9 26.5 %collective-permute-start.11 = (bf16[272,768]{1,0:T(8,128)(2,1)S(1)}, bf16[272,768]{1,0:T(8,128)(2,1)S(1)}, u32[]{:S(2)}, u32[]{:S(2)}) collective-permute-start(bf16[272,768]{1,0:T(8,128)(2,1)S(1)} %fusion.72), channel_id=1, source_target_pairs={{0,12},{1,13},{2,14},{3,15},{16,28},{17,29},{18,30},{19,31}} | collective-permute-start | bytes 1253384 | tf_op jit(solution)/shard_map/ppermute | solution.py:378
  105.8 19.7 %collective-permute-start.10 = (bf16[272,768]{1,0:T(8,128)(2,1)S(1)}, bf16[272,768]{1,0:T(8,128)(2,1)S(1)}, u32[]{:S(2)}, u32[]{:S(2)}) collective-permute-start(bf16[272,768]{1,0:T(8,128)(2,1)S(1)} %fusion.72), channel_id=1, source_target_pairs={{0,8},{4,12},{1,9},{5,13},{2,10},{6,14},{3,11},{7,15},{16,24},{20,... | collective-permute-start | bytes 1253384 | tf_op jit(solution)/shard_map/ppermute | solution.py:378
  107.2 18.5 %collective-permute-start.9 = (bf16[272,768]{1,0:T(8,128)(2,1)S(1)}, bf16[272,768]{1,0:T(8,128)(2,1)S(1)}, u32[]{:S(2)}, u32[]{:S(2)}) collective-permute-start(bf16[272,768]{1,0:T(8,128)(2,1)S(1)} %fusion.72), channel_id=1, source_target_pairs={{0,4},{4,8},{8,12},{1,5},{5,9},{9,13},{2,6},{6,10},{10,14},{3,7},{... | collective-permute-start | bytes 1253384 | tf_op jit(solution)/shard_map/ppermute | solution.py:378
  125.7 16.9 %collective-permute-start.15 = (bf16[1024,2048]{1,0:T(8,128)(2,1)}, bf16[1024,2048]{1,0:T(8,128)(2,1)}, u32[]{:S(2)}, u32[]{:S(2)}) collective-permute-start(bf16[1024,2048]{1,0:T(8,128)(2,1)} %bitcast.32), channel_id=1, source_target_pairs={{0,16},{16,0},{1,17},{17,1},{2,18},{18,2},{3,19},{19,3},{4,20},{20... | collective-permute-start | bytes 12582920 | tf_op jit(solution)/shard_map/ppermute | solution.py:368
  140.7 120.8 %all-reduce.11.cloned.1.call-start = ((), (), s32[]{:S(2)}) async-start(), calls=%async_computation.1 | async-start | bytes 2097152 | tf_op jit(solution)/shard_map/psum | solution.py:806
  210.2 179.3 %all-reduce.13.cloned.1.call-start = ((), (), s32[]{:S(2)}) async-start(), calls=%async_computation.2 | async-start | bytes 2097152 | tf_op jit(solution)/shard_map/psum | solution.py:538
  280.5 38.5 %collective-permute-start.20 = (bf16[256,256]{1,0:T(8,128)(2,1)}, bf16[256,256]{1,0:T(8,128)(2,1)}, u32[]{:S(2)}, u32[]{:S(2)}) collective-permute-start(bf16[256,256]{1,0:T(8,128)(2,1)} %pad_maximum_fusion.35), channel_id=1, source_target_pairs={{0,4},{4,8},{8,12},{1,5},{5,9},{9,13},{2,6},{6,10},{10,14},{3,7},{... | collective-permute-start | bytes 393224 | tf_op jit(solution)/shard_map/ppermute | solution.py:378
  284.6 33.4 %collective-permute-start.19 = (bf16[256,256]{1,0:T(8,128)(2,1)}, bf16[256,256]{1,0:T(8,128)(2,1)}, u32[]{:S(2)}, u32[]{:S(2)}) collective-permute-start(bf16[256,256]{1,0:T(8,128)(2,1)} %pad_maximum_fusion.35), channel_id=1, source_target_pairs={{0,8},{4,12},{1,9},{5,13},{2,10},{6,14},{3,11},{7,15},{16,24},{20,... | collective-permute-start | bytes 393224 | tf_op jit(solution)/shard_map/ppermute | solution.py:378
  288.0 27.7 %collective-permute-start.18 = (bf16[256,256]{1,0:T(8,128)(2,1)}, bf16[256,256]{1,0:T(8,128)(2,1)}, u32[]{:S(2)}, u32[]{:S(2)}) collective-permute-start(bf16[256,256]{1,0:T(8,128)(2,1)} %pad_maximum_fusion.35), channel_id=1, source_target_pairs={{0,12},{1,13},{2,14},{3,15},{16,28},{17,29},{18,30},{19,31}} | collective-permute-start | bytes 393224 | tf_op jit(solution)/shard_map/ppermute | solution.py:378
  307.5 22.7 %collective-permute-start.23 = (bf16[272,768]{1,0:T(8,128)(2,1)}, bf16[272,768]{1,0:T(8,128)(2,1)}, u32[]{:S(2)}, u32[]{:S(2)}) collective-permute-start(bf16[272,768]{1,0:T(8,128)(2,1)} %fusion.70), channel_id=1, source_target_pairs={{0,12},{1,13},{2,14},{3,15},{16,28},{17,29},{18,30},{19,31}} | collective-permute-start | bytes 1253384 | tf_op jit(solution)/shard_map/ppermute | solution.py:378
  309.6 19.3 %collective-permute-start.22 = (bf16[272,768]{1,0:T(8,128)(2,1)}, bf16[272,768]{1,0:T(8,128)(2,1)}, u32[]{:S(2)}, u32[]{:S(2)}) collective-permute-start(bf16[272,768]{1,0:T(8,128)(2,1)} %fusion.70), channel_id=1, source_target_pairs={{0,8},{4,12},{1,9},{5,13},{2,10},{6,14},{3,11},{7,15},{16,24},{20,... | collective-permute-start | bytes 1253384 | tf_op jit(solution)/shard_map/ppermute | solution.py:378
  315.8 14.3 %collective-permute-start.21 = (bf16[272,768]{1,0:T(8,128)(2,1)}, bf16[272,768]{1,0:T(8,128)(2,1)S(1)}, u32[]{:S(2)}, u32[]{:S(2)}) collective-permute-start(bf16[272,768]{1,0:T(8,128)(2,1)} %fusion.70), channel_id=1, source_target_pairs={{0,4},{4,8},{8,12},{1,5},{5,9},{9,13},{2,6},{6,10},{10,14},{3,7},{... | collective-permute-start | bytes 1253384 | tf_op jit(solution)/shard_map/ppermute | solution.py:378
  338.1 131.6 %all-reduce.15.cloned.1.call-start = ((), (), s32[]{:S(2)}) async-start(), calls=%async_computation.3 | async-start | bytes 2097152 | tf_op jit(solution)/shard_map/psum | solution.py:572
  356.5 267.9 %collective-permute-start.17 = (bf16[256,2048]{1,0:T(8,128)(2,1)S(1)}, bf16[256,2048]{1,0:T(8,128)(2,1)}, u32[]{:S(2)}, u32[]{:S(2)}) collective-permute-start(bf16[256,2048]{1,0:T(8,128)(2,1)S(1)} %get-tuple-element.131), channel_id=1, source_target_pairs={{16,0},{17,1},{18,2},{19,3},{20,4},{21,5},{22,6},{23,7},{24,8},{25... | collective-permute-start | bytes 3145736 | tf_op jit(solution)/shard_map/ppermute | solution.py:815
  418.0 125.9 %all-reduce.17.cloned.1.call-start = ((), (), s32[]{:S(2)}) async-start(), calls=%async_computation.4 | async-start | bytes 2097152 | tf_op jit(solution)/shard_map/psum | solution.py:458
  438.3 226.6 %collective-permute-start.58 = (bf16[16,7168]{1,0:T(8,128)(2,1)}, bf16[16,7168]{1,0:T(8,128)(2,1)}, u32[]{:S(2)}, u32[]{:S(2)}) collective-permute-start(bf16[16,7168]{1,0:T(8,128)(2,1)} %add_convert_fusion.8), channel_id=1, source_target_pairs={{0,16},{1,17},{2,18},{3,19},{4,20},{5,21},{6,22},{7,23},{8,24},{9,... | collective-permute-start | bytes 688136 | tf_op jit(solution)/shard_map/ppermute | solution.py:812
  483.9 25.8 %collective-permute-start.31 = (bf16[272,768]{1,0:T(8,128)(2,1)}, bf16[272,768]{1,0:T(8,128)(2,1)}, u32[]{:S(2)}, u32[]{:S(2)}) collective-permute-start(bf16[272,768]{1,0:T(8,128)(2,1)} %fusion.71), channel_id=1, source_target_pairs={{12,0},{13,1},{14,2},{15,3},{28,16},{29,17},{30,18},{31,19}} | collective-permute-start | bytes 1253384 | tf_op jit(solution)/shard_map/ppermute | solution.py:378
  485.2 22.3 %collective-permute-start.30 = (bf16[272,768]{1,0:T(8,128)(2,1)}, bf16[272,768]{1,0:T(8,128)(2,1)}, u32[]{:S(2)}, u32[]{:S(2)}) collective-permute-start(bf16[272,768]{1,0:T(8,128)(2,1)} %fusion.71), channel_id=1, source_target_pairs={{8,0},{12,4},{9,1},{13,5},{10,2},{14,6},{11,3},{15,7},{24,16},{28,... | collective-permute-start | bytes 1253384 | tf_op jit(solution)/shard_map/ppermute | solution.py:378
  486.5 22.0 %collective-permute-start.29 = (bf16[272,768]{1,0:T(8,128)(2,1)}, bf16[272,768]{1,0:T(8,128)(2,1)}, u32[]{:S(2)}, u32[]{:S(2)}) collective-permute-start(bf16[272,768]{1,0:T(8,128)(2,1)} %fusion.71), channel_id=1, source_target_pairs={{4,0},{8,4},{12,8},{5,1},{9,5},{13,9},{6,2},{10,6},{14,10},{7,3},{... | collective-permute-start | bytes 1253384 | tf_op jit(solution)/shard_map/ppermute | solution.py:378
  487.8 114.7 %all-reduce.19.cloned.1.call-start = ((), (), s32[]{:S(2)}) async-start(), calls=%async_computation.5 | async-start | bytes 2097152 | tf_op jit(solution)/shard_map/psum | solution.py:674
  512.4 22.2 %collective-permute-start.32 = (bf16[256,256]{1,0:T(8,128)(2,1)}, bf16[256,256]{1,0:T(8,128)(2,1)}, u32[]{:S(2)}, u32[]{:S(2)}) collective-permute-start(bf16[256,256]{1,0:T(8,128)(2,1)} %get-tuple-element.168), channel_id=1, source_target_pairs={{4,0},{8,4},{12,8},{5,1},{9,5},{13,9},{6,2},{10,6},{14,10},{7,3},{... | collective-permute-start | bytes 393224 | tf_op jit(solution)/shard_map/ppermute | solution.py:378
  513.7 21.0 %collective-permute-start.34 = (bf16[256,256]{1,0:T(8,128)(2,1)}, bf16[256,256]{1,0:T(8,128)(2,1)}, u32[]{:S(2)}, u32[]{:S(2)}) collective-permute-start(bf16[256,256]{1,0:T(8,128)(2,1)} %get-tuple-element.169), channel_id=1, source_target_pairs={{12,0},{13,1},{14,2},{15,3},{28,16},{29,17},{30,18},{31,19}} | collective-permute-start | bytes 393224 | tf_op jit(solution)/shard_map/ppermute | solution.py:378
  515.0 19.7 %collective-permute-start.33 = (bf16[256,256]{1,0:T(8,128)(2,1)}, bf16[256,256]{1,0:T(8,128)(2,1)}, u32[]{:S(2)}, u32[]{:S(2)}) collective-permute-start(bf16[256,256]{1,0:T(8,128)(2,1)} %get-tuple-element.170), channel_id=1, source_target_pairs={{8,0},{12,4},{9,1},{13,5},{10,2},{14,6},{11,3},{15,7},{24,16},{28,... | collective-permute-start | bytes 393224 | tf_op jit(solution)/shard_map/ppermute | solution.py:378
  547.2 133.1 %all-reduce.21.cloned.1.call-start = ((), (), s32[]{:S(2)}) async-start(), calls=%async_computation.6 | async-start | bytes 2097152 | tf_op jit(solution)/shard_map/psum | solution.py:572
  551.0 74.7 %collective-permute-start.28 = (bf16[256,2048]{1,0:T(8,128)(2,1)}, bf16[256,2048]{1,0:T(8,128)(2,1)}, u32[]{:S(2)}, u32[]{:S(2)}) collective-permute-start(bf16[256,2048]{1,0:T(8,128)(2,1)} %add_convert_fusion), channel_id=1, source_target_pairs={{0,16},{1,17},{2,18},{3,19},{4,20},{5,21},{6,22},{7,23},{8,24},{9,... | collective-permute-start | bytes 3145736 | tf_op jit(solution)/shard_map/ppermute | solution.py:812
  609.2 214.1 %collective-permute-start.46 = (bf16[256,2048]{1,0:T(8,128)(2,1)}, bf16[256,2048]{1,0:T(8,128)(2,1)}, u32[]{:S(2)}, u32[]{:S(2)}) collective-permute-start(bf16[256,2048]{1,0:T(8,128)(2,1)} %fusion.24), channel_id=1, source_target_pairs={{0,16},{1,17},{2,18},{3,19},{4,20},{5,21},{6,22},{7,23},{8,24},{9,... | collective-permute-start | bytes 3145736 | tf_op jit(solution)/shard_map/ppermute | solution.py:812
  612.5 25.5 %collective-permute-start.51 = (bf16[16,3120]{1,0:T(8,128)(2,1)S(1)}, bf16[16,3120]{1,0:T(8,128)(2,1)}, u32[]{:S(2)}, u32[]{:S(2)}) collective-permute-start(bf16[16,3120]{1,0:T(8,128)(2,1)S(1)} %pad_maximum_fusion.39), channel_id=1, source_target_pairs={{0,1},{1,0},{2,3},{3,2},{4,5},{5,4},{6,7},{7,6},{8,9},{9,8},{10,11... | collective-permute-start | bytes 299528 | tf_op jit(solution)/shard_map/ppermute | solution.py:385
  624.3 190.5 %all-reduce.23.cloned.1.call-start = ((), (), s32[]{:S(2)}) async-start(), calls=%async_computation.7 | async-start | bytes 2097152 | tf_op jit(solution)/shard_map/psum | solution.py:674
  638.9 11.5 %collective-permute-start.52 = (bf16[16,3120]{1,0:T(8,128)(2,1)S(1)}, bf16[16,3120]{1,0:T(8,128)(2,1)S(1)}, u32[]{:S(2)}, u32[]{:S(2)}) collective-permute-start(bf16[16,3120]{1,0:T(8,128)(2,1)S(1)} %add_convert_fusion.11), channel_id=1, source_target_pairs={{0,2},{1,3},{2,0},{3,1},{4,6},{5,7},{6,4},{7,5},{8,10},{9,11},{10,... | collective-permute-start | bytes 299528 | tf_op jit(solution)/shard_map/ppermute | solution.py:385
  639.0 13.0 %collective-permute-start.37 = (bf16[16,7168]{1,0:T(8,128)(2,1)S(1)}, bf16[16,7168]{1,0:T(8,128)(2,1)S(1)}, u32[]{:S(2)}, u32[]{:S(2)}) collective-permute-start(bf16[16,7168]{1,0:T(8,128)(2,1)S(1)} %pad_maximum_fusion.25), channel_id=1, source_target_pairs={{0,4},{4,0},{8,12},{12,8},{1,5},{5,1},{9,13},{13,9},{2,6},{6,2},{1... | collective-permute-start | bytes 688136 | tf_op jit(solution)/shard_map/ppermute | solution.py:385
  657.6 106.9 %collective-permute-start.54 = (bf16[16,7984]{1,0:T(8,128)(2,1)}, bf16[16,7984]{1,0:T(8,128)(2,1)}, u32[]{:S(2)}, u32[]{:S(2)}) collective-permute-start(bf16[16,7984]{1,0:T(8,128)(2,1)} %add_convert_fusion.3), channel_id=1, source_target_pairs={{0,8},{4,12},{8,0},{12,4},{1,9},{5,13},{9,1},{13,5},{2,10},{6,14},... | collective-permute-start | bytes 766472 | tf_op jit(solution)/shard_map/ppermute | solution.py:385
  691.0 23.4 %collective-permute-start.41 = (bf16[272,768]{1,0:T(8,128)(2,1)S(1)}, bf16[272,768]{1,0:T(8,128)(2,1)S(1)}, u32[]{:S(2)}, u32[]{:S(2)}) collective-permute-start(bf16[272,768]{1,0:T(8,128)(2,1)S(1)} %fusion.73), channel_id=1, source_target_pairs={{12,0},{13,1},{14,2},{15,3},{28,16},{29,17},{30,18},{31,19}} | collective-permute-start | bytes 1253384 | tf_op jit(solution)/shard_map/ppermute | solution.py:378
  692.3 21.9 %collective-permute-start.40 = (bf16[272,768]{1,0:T(8,128)(2,1)S(1)}, bf16[272,768]{1,0:T(8,128)(2,1)S(1)}, u32[]{:S(2)}, u32[]{:S(2)}) collective-permute-start(bf16[272,768]{1,0:T(8,128)(2,1)S(1)} %fusion.73), channel_id=1, source_target_pairs={{8,0},{12,4},{9,1},{13,5},{10,2},{14,6},{11,3},{15,7},{24,16},{28,... | collective-permute-start | bytes 1253384 | tf_op jit(solution)/shard_map/ppermute | solution.py:378
  693.6 20.7 %collective-permute-start.39 = (bf16[272,768]{1,0:T(8,128)(2,1)S(1)}, bf16[272,768]{1,0:T(8,128)(2,1)S(1)}, u32[]{:S(2)}, u32[]{:S(2)}) collective-permute-start(bf16[272,768]{1,0:T(8,128)(2,1)S(1)} %fusion.73), channel_id=1, source_target_pairs={{4,0},{8,4},{12,8},{5,1},{9,5},{13,9},{6,2},{10,6},{14,10},{7,3},{... | collective-permute-start | bytes 1253384 | tf_op jit(solution)/shard_map/ppermute | solution.py:378
  716.1 20.0 %collective-permute-start.42 = (bf16[256,256]{1,0:T(8,128)(2,1)}, bf16[256,256]{1,0:T(8,128)(2,1)}, u32[]{:S(2)}, u32[]{:S(2)}) collective-permute-start(bf16[256,256]{1,0:T(8,128)(2,1)} %get-tuple-element.165), channel_id=1, source_target_pairs={{4,0},{8,4},{12,8},{5,1},{9,5},{13,9},{6,2},{10,6},{14,10},{7,3},{... | collective-permute-start | bytes 393224 | tf_op jit(solution)/shard_map/ppermute | solution.py:378
  717.4 18.7 %collective-permute-start.44 = (bf16[256,256]{1,0:T(8,128)(2,1)}, bf16[256,256]{1,0:T(8,128)(2,1)}, u32[]{:S(2)}, u32[]{:S(2)}) collective-permute-start(bf16[256,256]{1,0:T(8,128)(2,1)} %get-tuple-element.166), channel_id=1, source_target_pairs={{12,0},{13,1},{14,2},{15,3},{28,16},{29,17},{30,18},{31,19}} | collective-permute-start | bytes 393224 | tf_op jit(solution)/shard_map/ppermute | solution.py:378
  718.7 17.4 %collective-permute-start.43 = (bf16[256,256]{1,0:T(8,128)(2,1)S(1)}, bf16[256,256]{1,0:T(8,128)(2,1)}, u32[]{:S(2)}, u32[]{:S(2)}) collective-permute-start(bf16[256,256]{1,0:T(8,128)(2,1)S(1)} %get-tuple-element.167), channel_id=1, source_target_pairs={{8,0},{12,4},{9,1},{13,5},{10,2},{14,6},{11,3},{15,7},{24,16},{28,... | collective-permute-start | bytes 393224 | tf_op jit(solution)/shard_map/ppermute | solution.py:378
  (226 other events, 2005.0 us)
Sparse Core Ops, SparseCore 0:
  140.9 53.1 all-reduce.8
  210.3 51.1 all-reduce.10
  338.2 51.3 all-reduce.12
  418.2 51.4 all-reduce.14
  487.9 55.0 all-reduce.16
  547.3 55.1 all-reduce.18
  624.4 55.7 all-reduce.20
  764.7 50.1 all-reduce.22

commit v4 on v3

--- a/solution.py
+++ b/solution.py
@@ -65,9 +65,50 @@
     return jnp.where(lane < MHEAD, left, right)
 
 
+def moved_sum(moved_refs, states, lanes):
+    total, between = 0.0, 1.0
+    for moved_ref in moved_refs:
+        total = total + between * moved_ref[:states, lanes].astype(F32)
+        ends = moved_ref[states : states + 16, lanes].astype(F32)
+        between = between * (ends[0:1, :] + ends[1:2, :])
+    return total
+
+
+def scan_finish_kernel(y_ref, proj_ref, c_ref, cum_ref, skip_ref, *refs):
+    moved_refs, (out_ref, gated_ref, state_ref) = refs[:-3], refs[-3:]
+    rows, width = y_ref.shape
+    states = c_ref.shape[1]
+    heads = cum_ref.shape[1]
+    grown = jnp.exp(cum_ref[...])
+    for pair in range(heads // 2):
+        one, two = 2 * pair, 2 * pair + 1
+        lanes = slice(PAIR * pair, PAIR * (pair + 1))
+        state = moved_sum(moved_refs, states, lanes).astype(BF)
+        state_ref[:, lanes] = state
+        grown_pair = pair_lanes(rows, grown[:, one : one + 1], grown[:, two : two + 1])
+        scanned = y_ref[:, lanes] + grown_pair * mm(c_ref[...], state)
+        out_ref[:, lanes] = scanned
+        gate = proj_ref[:, lanes]
+        joined = scanned + skip_ref[:, lanes] * proj_ref[:, width + PAIR * pair : width + PAIR * (pair + 1)]
+        gated_ref[:, lanes] = (joined * (gate / (1.0 + jnp.exp(-gate)))).astype(BF)
+
+
+def scan_finish(y, proj, c_low, cum, skip, moved):
+    rows, width = y.shape
+    return vmem_call(
+        scan_finish_kernel,
+        (
+            jax.ShapeDtypeStruct((rows, width), F32),
+            jax.ShapeDtypeStruct((rows, width), BF),
+            jax.ShapeDtypeStruct((c_low.shape[1], width), BF),
+        ),
+    )(y, proj, c_low, cum, skip, *moved)
+
+
 def scan_forward_kernel(x_ref, b_ref, c_ref, dt_ref, cum_ref, cumt_ref, y_ref, state_ref, tail_scr):
     rows = x_ref.shape[0]
     heads = dt_ref.shape[1]
+    width = heads * MHEAD
     gram = mm_t(c_ref[...], b_ref[...])
     row = lax.broadcasted_iota(jnp.int32, (rows, rows), 0)
     col = lax.broadcasted_iota(jnp.int32, (rows, rows), 1)
@@ -79,7 +120,7 @@
     for pair in range(heads // 2):
         one, two = 2 * pair, 2 * pair + 1
         lanes = slice(PAIR * pair, PAIR * (pair + 1))
-        scaled = x_ref[:, lanes] * pair_lanes(rows, dt[:, one : one + 1], dt[:, two : two + 1])
+        scaled = x_ref[:, width + PAIR * pair : width + PAIR * (pair + 1)] * pair_lanes(rows, dt[:, one : one + 1], dt[:, two : two + 1])
         scaled_low = scaled.astype(BF)
         tail_scr[:, lanes] = (
             scaled * pair_lanes(rows, tail[:, one : one + 1], tail[:, two : two + 1])
@@ -93,7 +134,7 @@
 
 
 def scan_forward(x, b_low, c_low, dt, cum, cumt):
-    rows, width = x.shape
+    rows, width = x.shape[0], dt.shape[1] * MHEAD
     return vmem_call(
         scan_forward_kernel,
         (
@@ -158,7 +199,6 @@
     z_ref,
     y_ref,
     b_ref,
-    grad_state_ref,
     state_ref,
     db_ref,
     dc_ref,
@@ -168,16 +208,11 @@
     live_ref,
     rate_ref,
     skip_ref,
-    dx_ref,
-    db_out_ref,
-    dc_out_ref,
-    dstep_ref,
-    through_scr,
-    step_scr,
-    edge_scr,
-    tail_scr,
-    grown_scr,
+    *refs,
 ):
+    moved_refs = refs[:-10]
+    dx_ref, db_out_ref, dc_out_ref, dstep_ref = refs[-10:-6]
+    through_scr, step_scr, edge_scr, tail_scr, grown_scr, grad_state_scr = refs[-6:]
     rows, width = x_ref.shape
     heads = dt_ref.shape[1]
     cum = cum_ref[...]
@@ -195,7 +230,8 @@
         whole_pair = pair_lanes(1, whole[:, one : one + 1], whole[:, two : two + 1])
         x = x_ref[:, lanes]
         dy = dy_ref[:, lanes].astype(F32)
-        grad_state = grad_state_ref[:, lanes]
+        grad_state = moved_sum(moved_refs, b_ref.shape[1], lanes).astype(BF)
+        grad_state_scr[:, lanes] = grad_state
         z_tail = tail_pair * mm(b_ref[...], grad_state)
         z_all = z_ref[:, lanes] + z_tail
         dx_ref[:, lanes] = (dt_pair * z_all + skip_ref[:, lanes] * dy).astype(dx_ref.dtype)
@@ -209,7 +245,7 @@
         )
         edge = jnp.sum(scaled * z_tail, axis=0, keepdims=True) + kept * whole_pair
         edge_scr[:, lanes] = jnp.broadcast_to(edge, (edge_scr.shape[0], PAIR))
-    db_out_ref[...] = (db_ref[...] + mm_t(tail_scr[...], grad_state_ref[...])).astype(BF)
+    db_out_ref[...] = (db_ref[...] + mm_t(tail_scr[...], grad_state_scr[...])).astype(BF)
     dc_out_ref[...] = (dc_ref[...] + mm_t(grown_scr[...], state_ref[...])).astype(BF)
     lane = lax.broadcasted_iota(jnp.int32, (width, heads), 0)
     head = lax.broadcasted_iota(jnp.int32, (width, heads), 1)
@@ -227,7 +263,7 @@
     dstep_ref[...] = grad_steps * live_ref[...] / (1.0 + jnp.exp(-step_ref[...]))
 
 
-def scan_close(x, dy_low, z, y, b_low, grad_state, state, db, dc, dt, cum, step, live, rate, skip):
+def scan_close(x, dy_low, z, y, b_low, state, db, dc, dt, cum, step, live, rate, skip, moved):
     rows, width = x.shape
     states, heads = b_low.shape[1], dt.shape[1]
     return vmem_call(
@@ -244,8 +280,9 @@
             pltpu.VMEM((8, width), F32),
             pltpu.VMEM((rows, width), BF),
             pltpu.VMEM((rows, width), BF),
+            pltpu.VMEM((states, width), BF),
         ],
-    )(x, dy_low, z, y, b_low, grad_state, state, db, dc, dt, cum, step, live, rate, skip)
+    )(x, dy_low, z, y, b_low, state, db, dc, dt, cum, step, live, rate, skip, *moved)
 
 
 def block_mask(scores_shape, span, block, ctx_index, length):
@@ -427,15 +464,9 @@
     return total
 
 
-def carried_states(payload, states, reverse):
+def moved_states(payload, reverse):
     count = lax.axis_size("ctx")
-    summed = jnp.zeros((states, payload.shape[1]), F32)
-    between = jnp.ones((1, payload.shape[1]), F32)
-    for steps in range(1, count):
-        moved = shifted(payload, -steps if reverse else steps).astype(F32)
-        summed = summed + between * moved[:states]
-        between = between * (moved[states : states + 1] + moved[states + 1 : states + 2])
-    return summed
+    return [shifted(payload, -steps if reverse else steps) for steps in range(1, count)]
 
 
 def state_payload(state, total):
@@ -470,19 +501,14 @@
     normed = (entry * rms_scale(entry) * w.mixer_gain).astype(BF)
     small_in = mm_t(normed, w.mixin_down).astype(BF)
     shared = mm(normed, w.shared) + mm(small_in, w.shared_up)
-    query_proj = mm(normed, w.query) + mm(small_in, w.query_up)
     mamba_proj = mm(normed, w.mamba) + mm(small_in, w.mamba_up)
     span = entry.shape[0]
-    local_heads = query_proj.shape[1] // HEAD
+    local_heads = w.query.shape[1] // HEAD
     key_head = place.wt * local_heads // (QHEADS // KVHEADS)
     key_part = lax.dynamic_slice_in_dim(shared, key_head * HEAD, HEAD, 1)
     value_part = lax.dynamic_slice_in_dim(shared, (KVHEADS + key_head) * HEAD, HEAD, 1)
     key_value = jnp.concatenate([rotate(key_part, place.tables, 1.0), value_part], axis=1)
     key_all = gathered_rows(key_value.astype(BF), place.ctx)
-    rotated = rotate(query_proj, place.tables, 1.0).astype(BF)
-    query_rows = jnp.concatenate(
-        [rotated[:, head * HEAD : (head + 1) * HEAD] for head in range(local_heads)], axis=0
-    )
 
     half = mamba_proj.shape[1] // 2
     heads = half // MHEAD
@@ -497,14 +523,21 @@
     step_sizes = jax.nn.softplus(step_in) * place.live[:, None]
     cum = jnp.dot(place.lower, -w.decay_rate * step_sizes, precision=HIGH)
     local_y, local_state = scan_forward(
-        inputs, input_map, output_map, step_sizes, cum, cum.T
-    )
-    state_sum = carried_states(state_payload(local_state, cum[-1]), NSTATE, False)
+        mamba_proj, input_map, output_map, step_sizes, cum, cum.T
+    )
+    payload = after(state_payload(local_state, cum[-1]), key_all)
+    moved = moved_states(payload, False)
+    normed_now, small_now = lax.optimization_barrier((normed, small_in, payload))[:2]
+    query_proj = mm(normed_now, w.query) + mm(small_now, w.query_up)
+    rotated = rotate(query_proj, place.tables, 1.0).astype(BF)
+    query_rows = jnp.concatenate(
+        [rotated[:, head * HEAD : (head + 1) * HEAD] for head in range(local_heads)], axis=0
+    )
     attended, lse = attend_forward(place.scalars, query_rows, key_all, span)
-    state_in = state_sum.astype(BF)
-    scanned = local_y + wide(jnp.exp(cum)) * mm(output_map, state_in)
-    joined = scanned + jnp.repeat(w.skip_gain, MHEAD)[None, :] * inputs
-    gated_low = (joined * jax.nn.silu(gate_raw)).astype(BF)
+    skip = jnp.repeat(w.skip_gain, MHEAD)[None, :]
+    scanned, gated_low, state_in = scan_finish(
+        local_y, mamba_proj, output_map, cum, skip, moved
+    )
     attended_low = attended.astype(BF)
     small_mid = mm_t(attended_low, w.attnout_down) + mm_t(gated_low, w.mambaout_down)
     part = (
@@ -518,6 +551,7 @@
         key_head=key_head,
         gate_raw=gate_raw,
         inputs=inputs,
+        proj=mamba_proj,
         input_map=input_map,
         output_map=output_map,
         step_in=step_in,
@@ -587,7 +621,7 @@
     return grad_out + norm_back(s.hidden, summed, w.feed_gain), found
 
 
-def mixer_backward(grad_hidden, w, place, s, finish, before=()):
+def mixer_backward(grad_hidden, w, place, s, finish, before, late):
     grads = Weights()
     span = grad_hidden.shape[0]
     grad_mixed = (grad_hidden * place.live[:, None]).astype(BF)
@@ -607,7 +641,7 @@
     grown_dy = (grown * dy).astype(BF)
     local_grad = t_mm(s.output_map, grown_dy)
     payload = state_payload(local_grad, cum[-1])
-    grad_state = carried_states(payload, NSTATE, True).astype(BF)
+    moved = moved_states(payload, True)
     dy_now, grad_mid, small_now = lax.optimization_barrier(
         (dy_low, grad_mixed, grad_small_mid, payload)
     )[:3]
@@ -618,7 +652,7 @@
     grad_query, grad_keyval = attend_backward(
         place.scalars, s.query_rows, s.key_all, s.lse, s.attended, grad_attended
     )
-    own = returned_rows(after(grad_keyval, grad_state), span, place.ctx)
+    own = returned_rows(after(grad_keyval, *moved), span, place.ctx)
 
     z_local, db_local, dc_local = scan_backward(
         inputs, dy_now, s.input_map, s.output_map, step_sizes, cum, cum.T
@@ -629,7 +663,6 @@
         z_local,
         scanned,
         s.input_map,
-        grad_state,
         s.state_in,
         db_local,
         dc_local,
@@ -639,6 +672,7 @@
         place.live[:, None],
         w.decay_rate[None, :],
         skip,
+        moved,
     )
 
     heads = cum.shape[1]
@@ -679,7 +713,7 @@
     grads.mamba_up = t_mm(s.small_in, grad_mamba)
     grads.shared_up = t_mm(s.small_in, grad_shared)
     grads.mixin_down = t_mm(grad_small_in, s.normed)
-    found = finish(grads, *((summed,) if before else ()))
+    found = finish(grads, *((summed,) if late else ()))
     grad_entry = grad_hidden + norm_back(
         s.entry.astype(F32), summed.astype(F32), w.mixer_gain
     )
@@ -756,17 +790,6 @@
         items[name] = item[0]
     layers = (Weights(), Weights())
 
-    def packed_items(names, which):
-        return jnp.concatenate(
-            [
-                lax.dynamic_index_in_dim(items[name], which, 0, keepdims=False).reshape(
-                    items[name].shape[1], -1
-                )
-                for name in names
-            ],
-            axis=1,
-        )
-
     def place_pack(names, widths, kept, moved):
         for index, w in enumerate(layers):
             value = jnp.where(section == index, kept, moved)
@@ -778,8 +801,13 @@
     def exchange_pack(number, *gates):
         names = PACKS[number]
         widths = [items[name][0, 0].size for name in names]
-        moved = swap(after(packed_items(names, theirs), *gates))
-        place_pack(names, widths, packed_items(names, mine), moved)
+        packed = jnp.concatenate(
+            [items[name].reshape(items[name].shape[:2] + (-1,)) for name in names], axis=2
+        )
+        packed = lax.optimization_barrier((packed,) + gates)[0]
+        moved = swap(lax.dynamic_index_in_dim(packed, theirs, 0, keepdims=False))
+        kept = lax.dynamic_index_in_dim(packed, mine, 0, keepdims=False)
+        place_pack(names, widths, kept, moved)
 
     vectors = FIXED[:5]
     joined = jnp.concatenate([own[name].astype(F32) for name in vectors])
@@ -840,7 +868,7 @@
     last_part = after(last_part, grad_hidden)
     second_out = (saved_second.hidden + low_sum(last_part)).astype(BF)
     grad, found = mixer_backward(
-        grad_hidden, second, place, saved_second, summed_grads, (second_out,)
+        grad_hidden, second, place, saved_second, summed_grads, (second_out,), True
     )
     second_grad = grad.astype(BF)
     second_sets.append(found)
@@ -848,7 +876,9 @@
         second_grad.astype(F32), first, place, saved_first, summed_grads
     )
     first_sets = [found]
-    grad, found = mixer_backward(grad_hidden, first, place, saved_first, summed_grads)
+    grad, found = mixer_backward(
+        grad_hidden, first, place, saved_first, summed_grads, (), False
+    )
     first_grad = grad.astype(BF)
     first_sets.append(found)
 

time: 844 us -> 837 us (level)
  waiting for transfers between devices: 288 us -> 279 us
  Pallas kernels: 45.1 us -> 53.9 us
    dot_general x38 -> x36, matrix products: 59.6 us -> 55.5 us  [mm(): return jnp.dot(a.astype(BF), b.astype(BF), preferred_element_type=F32)]
    unnamed x422 -> x408, local copies, waits for them, and re-layouts: 44.8 us -> 41.9 us
  transfers between devices with their start and end apart: 67 -> 67, of which waited for: 25 -> 29; matrix products, arithmetic and copies ran while one was open for 39% -> 38% of each run, Pallas kernels for 5% -> 6%
where the time goes in v4:
time: 837 us; the launch traced here: 828 us
  waiting for transfers between devices  279 us (33%)
  other arithmetic  161 us (19%)
  matrix products  137 us (16%)
  starting transfers between devices  90.9 us (11%)
  local copies, waits for them, and re-layouts  83.8 us (10%)
  Pallas kernels  53.9 us (6%)
  between operations  21.9 us (3%)
    psum x2, waiting for transfers between devices, mixer_backward(): summed = lax.psum(norm_part, 'wt')  80.4 us
    dot_general x36, matrix products, mm_t(): lax.dot_general(a.astype(BF), b.astype(BF), (((1,), (1,)), ((), ())), pre...  56.8 us
    dot_general x36, matrix products, mm(): return jnp.dot(a.astype(BF), b.astype(BF), preferred_element_type=F32)  55.5 us
    select_n x7, other arithmetic, shards(): value = jnp.where(section == index, own[name], moved[name])  50 us
    ppermute x24, starting transfers between devices, shifted(): lax.ppermute(value, 'ctx', [(source, source + steps) for source in range(...  49.3 us
    psum x1, waiting for transfers between devices, shards(): fed = after(lax.psum(feed_part, 'wt'), *following)  43.3 us
    psum x2, waiting for transfers between devices, feed_forward(): mixed = after(lax.psum(part, 'wt'), w.gateup, w.down)  42 us
    unnamed x408, local copies, waits for them, and re-layouts  41.9 us
  transfers between devices with their start and end apart: 67, of which 29 were waited for; matrix products, arithmetic and copies ran while one was open for 38% of the time, Pallas kernels for 6%

profile of v4, /device:TPU:0, one launch (start us, length us, event | category | flops | bytes accessed | tf_op | source)
XLA Modules:
  0.0 827.9 jit_solution(13202713554817833837)
XLA Ops:
  40.9 6.2 broadcast_select_fusion.4
  50.9 5.1 collective-permute-start.5
  72.8 13.1 %broadcast_select_fusion.2 = (bf16[2048,2,768]{2,1,0:T(2,128)(2,1)}, bf16[2048,2,768]{2,1,0:T(2,128)(2,1)S(1)}) fusion(bf16[2048,2,768]{2,1,0:T(2,128)(2,1)} %collective-permute-done.2, pred[]{:T(512)S(6)} %eq.23, bf16[1,2048,2,768]{3,2,1,0:T(2,128)(2,1)} %param.37, pred[]{:T(512)S(6)} %eq.22), kind=kLoop, calls=%fused_computation.2 | loop fusion | flops 6291456 | bytes 25165826 | tf_op jit(solution)/shard_map/jit(_where)/select_n | solution.py:822
  91.5 4.3 shard_map.354
  97.7 3.5 collective-permute-start.11
  116.0 7.3 collective-permute-done.9.refs_0_
  124.1 3.9 shard_map.356
  131.1 4.4 broadcast_select_fusion.8
  142.9 5.8 broadcast_select_fusion.6
  148.8 16.7 %broadcast_select_fusion = (bf16[2048,2,1024]{2,1,0:T(2,128)(2,1)}, bf16[2048,2,1024]{2,1,0:T(2,128)(2,1)}) fusion(bf16[2048,2,1024]{2,1,0:T(2,128)(2,1)} %collective-permute-done.14, pred[]{:T(512)S(6)} %eq.23, bf16[1,2048,2,1024]{3,2,1,0:T(2,128)(2,1)} %param.41, pred[]{:T(512)S(6)} %eq.22), kind=kLoop, calls=%fused_computation | loop fusion | flops 8388608 | bytes 33554432 | tf_op jit(solution)/shard_map/jit(_where)/select_n | solution.py:822
  165.4 10.3 %copy.85 = bf16[256,8,2,1024]{3,1,2,0:T(8,128)(2,1)} copy(bf16[256,8,2,1024]{3,2,1,0:T(2,128)(2,1)} %bitcast.216) | data formatting | bytes 16777216
  175.7 18.5 %all-reduce.9.cloned.1.call-done = bf16[256,2048]{1,0:T(8,128)(2,1)} async-done(((bf16[256,2048]{1,0:T(8,128)(2,1)}), bf16[256,2048]{1,0:T(8,128)(2,1)}) %all-reduce.9.cloned.1.call-update) | async-done | bytes 1048592 | tf_op jit(solution)/shard_map/psum | solution.py:572
  197.2 6.1 fusion.287
  211.6 6.8 copy.86
  218.3 43.3 %all-reduce.11.cloned.1.call-done = bf16[256,2048]{1,0:T(8,128)(2,1)} async-done(((bf16[256,2048]{1,0:T(8,128)(2,1)}), bf16[256,2048]{1,0:T(8,128)(2,1)}) %all-reduce.11.cloned.1.call-update) | async-done | bytes 1048592 | tf_op jit(solution)/shard_map/psum | solution.py:834
  266.2 4.6 fusion.282
  277.6 4.2 collective-permute-start.20
  287.1 6.0 fusion.288
  299.4 4.3 shard_map.357
  315.4 3.5 shard_map.358
  319.2 9.0 %collective-permute-done.22.refs_1_ = bf16[272,768]{1,0:T(8,128)(2,1)S(1)} collective-permute-done((bf16[272,768]{1,0:T(8,128)(2,1)S(1)}, bf16[272,768]{1,0:T(8,128)(2,1)S(1)}, u32[]{:S(2)}, u32[]{:S(2)}) %collective-permute-start.22) | collective-permute-done | bytes 417824 | tf_op jit(solution)/shard_map/ppermute | solution.py:415
  329.0 3.9 shard_map.359
  350.4 10.2 %copy.87 = bf16[256,8,2,1024]{3,1,2,0:T(8,128)(2,1)} copy(bf16[256,8,2,1024]{3,2,1,0:T(2,128)(2,1)} %bitcast.215) | data formatting | bytes 16777216
  365.5 23.5 %all-reduce.13.cloned.1.call-done = bf16[256,2048]{1,0:T(8,128)(2,1)} async-done(((bf16[256,2048]{1,0:T(8,128)(2,1)}), bf16[256,2048]{1,0:T(8,128)(2,1)}) %all-reduce.13.cloned.1.call-update) | async-done | bytes 1048592 | tf_op jit(solution)/shard_map/psum | solution.py:572
  393.1 5.9 fusion.290
  440.1 29.1 %all-reduce.15.cloned.1.call-done = bf16[256,2048]{1,0:T(8,128)(2,1)} async-done(((bf16[256,2048]{1,0:T(8,128)(2,1)}), bf16[256,2048]{1,0:T(8,128)(2,1)}) %all-reduce.15.cloned.1.call-update) | async-done | bytes 1048592 | tf_op jit(solution)/shard_map/psum | solution.py:606
  471.7 3.8 multiply_convert_fusion.1
  497.0 3.8 shard_map.361
  502.5 4.6 collective-permute-done.30.refs_1_
  511.9 8.6 %shard_map.362 = (bf16[256,768]{1,0:T(8,128)(2,1)}, bf16[256,256]{1,0:T(8,128)(2,1)}, bf16[256,256]{1,0:T(8,128)(2,1)}, f32[256,12]{1,0:T(8,128)}) custom-call(f32[256,768]{1,0:T(8,128)} %get-tuple-element.176.x_ref, bf16[256,768]{1,0:T(8,128)(2,1)} %copy-done.46, f32[256,768]{1,0:T(8,128)} %get-tuple-element.105.z_ref, ...), custom_call_target="tpu_custom_call" | custom-call | tf_op jit(solution)/shard_map/pallas_call | solution.py:269
  520.6 6.2 fusion.65
  533.7 4.0 fusion.273
  539.2 3.4 all-reduce.17.cloned.1.call-done
  552.5 44.9 %all-reduce.19.cloned.1.call-done = bf16[256,2048]{1,0:T(8,128)(2,1)} async-done(((bf16[256,2048]{1,0:T(8,128)(2,1)}), bf16[256,2048]{1,0:T(8,128)(2,1)}) %all-reduce.19.cloned.1.call-update) | async-done | bytes 1048592 | tf_op jit(solution)/shard_map/psum | solution.py:708
  611.9 5.8 fusion.58
  620.6 3.7 maximum_select_fusion
  625.9 5.1 collective-permute-done.36
  635.4 9.8 %collective-permute-done.52 = bf16[16,3120]{1,0:T(8,128)(2,1)S(1)} collective-permute-done((bf16[16,3120]{1,0:T(8,128)(2,1)S(1)}, bf16[16,3120]{1,0:T(8,128)(2,1)S(1)}, u32[]{:S(2)}, u32[]{:S(2)}) %collective-permute-start.52) | collective-permute-done | bytes 99872 | tf_op jit(solution)/shard_map/ppermute | solution.py:422
  668.7 6.3 all-reduce.21.cloned.1.call-done
  677.1 3.7 multiply_convert_fusion
  697.1 3.8 shard_map.364
  701.9 7.9 collective-permute-done.40.refs_1_
  714.5 8.5 %shard_map.365 = (bf16[256,768]{1,0:T(8,128)(2,1)}, bf16[256,256]{1,0:T(8,128)(2,1)}, bf16[256,256]{1,0:T(8,128)(2,1)}, f32[256,12]{1,0:T(8,128)}) custom-call(f32[256,768]{1,0:T(8,128)} %get-tuple-element.175.x_ref, bf16[256,768]{1,0:T(8,128)(2,1)} %copy-done.47, f32[256,768]{1,0:T(8,128)} %get-tuple-element.123.z_ref, ...), custom_call_target="tpu_custom_call" | custom-call | tf_op jit(solution)/shard_map/pallas_call | solution.py:269
  723.1 6.1 fusion.63
  735.4 3.9 collective-permute-done.47
  740.8 3.8 fusion.272
  749.1 5.0 collective-permute-done.49
  773.4 35.6 %all-reduce.23.cloned.1.call-done = bf16[256,2048]{1,0:T(8,128)(2,1)} async-done(((bf16[256,2048]{1,0:T(8,128)(2,1)}), bf16[256,2048]{1,0:T(8,128)(2,1)}) %all-reduce.23.cloned.1.call-update) | async-done | bytes 1048592 | tf_op jit(solution)/shard_map/psum | solution.py:708
  (794 shorter events, 358.2 us)
Async XLA Ops:
  7.2 187.0 %all-reduce.9.cloned.1.call-start = ((), (), s32[]{:S(2)}) async-start(), calls=%async_computation | async-start | bytes 2097152 | tf_op jit(solution)/shard_map/psum | solution.py:572
  9.6 23.0 %collective-permute-start = (f32[4132]{0:T(1024)S(1)}, f32[4132]{0:T(1024)S(1)}, u32[]{:S(2)}, u32[]{:S(2)}) collective-permute-start(f32[4132]{0:T(1024)S(1)} %concatenate.146), channel_id=1, source_target_pairs={{0,16},{16,0},{1,17},{17,1},{2,18},{18,2},{3,19},{19,3},{4,20},{20... | collective-permute-start | bytes 49592 | tf_op jit(solution)/shard_map/ppermute | solution.py:405
  18.8 16.8 %collective-permute-start.1 = (bf16[16,4912]{1,0:T(8,128)(2,1)}, bf16[16,4912]{1,0:T(8,128)(2,1)}, u32[]{:S(2)}, u32[]{:S(2)}) collective-permute-start(bf16[16,4912]{1,0:T(8,128)(2,1)} %dynamic-slice_bitcast_fusion.1), channel_id=1, source_target_pairs={{0,16},{16,0},{1,17},{17,1},{2,18},{18,2},{3,19},{19,3},{4,20},{20... | collective-permute-start | bytes 471560 | tf_op jit(solution)/shard_map/ppermute | solution.py:405
  18.8 19.3 %collective-permute-start.7 = (bf16[2048,256]{1,0:T(8,128)(2,1)}, bf16[2048,256]{1,0:T(8,128)(2,1)}, u32[]{:S(2)}, u32[]{:S(2)}) collective-permute-start(bf16[2048,256]{1,0:T(8,128)(2,1)} %bitcast.236), channel_id=1, source_target_pairs={{0,16},{16,0},{1,17},{17,1},{2,18},{18,2},{3,19},{19,3},{4,20},{20... | collective-permute-start | bytes 3145736 | tf_op jit(solution)/shard_map/ppermute | solution.py:405
  19.3 21.6 %collective-permute-start.3 = (bf16[2048,1072]{0,1:T(8,128)(2,1)}, bf16[2048,1072]{0,1:T(8,128)(2,1)}, u32[]{:S(2)}, u32[]{:S(2)}) collective-permute-start(bf16[2048,1072]{0,1:T(8,128)(2,1)} %bitcast.230), channel_id=1, source_target_pairs={{0,16},{16,0},{1,17},{17,1},{2,18},{18,2},{3,19},{19,3},{4,20},{20... | collective-permute-start | bytes 13172744 | tf_op jit(solution)/shard_map/ppermute | solution.py:405
  19.4 53.5 %collective-permute-start.2 = (bf16[2048,2,768]{2,1,0:T(2,128)(2,1)}, bf16[2048,2,768]{2,1,0:T(2,128)(2,1)}, u32[]{:S(2)}, u32[]{:S(2)}) collective-permute-start(bf16[2048,2,768]{2,1,0:T(2,128)(2,1)} %bitcast.229), channel_id=1, source_target_pairs={{0,16},{16,0},{1,17},{17,1},{2,18},{18,2},{3,19},{19,3},{4,20},{20... | collective-permute-start | bytes 18874376 | tf_op jit(solution)/shard_map/ppermute | solution.py:405
  50.9 18.6 %collective-permute-start.5 = (bf16[256,256]{1,0:T(8,128)(2,1)}, bf16[256,256]{1,0:T(8,128)(2,1)}, u32[]{:S(2)}, u32[]{:S(2)}) collective-permute-start(bf16[256,256]{1,0:T(8,128)(2,1)} %pad_maximum_fusion.33), channel_id=1, source_target_pairs={{0,8},{4,12},{1,9},{5,13},{2,10},{6,14},{3,11},{7,15},{16,24},{20,... | collective-permute-start | bytes 393224 | tf_op jit(solution)/shard_map/ppermute | solution.py:415
  56.0 12.5 %collective-permute-start.4 = (bf16[256,256]{1,0:T(8,128)(2,1)}, bf16[256,256]{1,0:T(8,128)(2,1)}, u32[]{:S(2)}, u32[]{:S(2)}) collective-permute-start(bf16[256,256]{1,0:T(8,128)(2,1)} %pad_maximum_fusion.33), channel_id=1, source_target_pairs={{0,12},{1,13},{2,14},{3,15},{16,28},{17,29},{18,30},{19,31}} | collective-permute-start | bytes 393224 | tf_op jit(solution)/shard_map/ppermute | solution.py:415
  91.5 57.2 %collective-permute-start.14 = (bf16[2048,2,1024]{2,1,0:T(2,128)(2,1)}, bf16[2048,2,1024]{2,1,0:T(2,128)(2,1)}, u32[]{:S(2)}, u32[]{:S(2)}) collective-permute-start(bf16[2048,2,1024]{2,1,0:T(2,128)(2,1)} %bitcast.28), channel_id=1, source_target_pairs={{0,16},{16,0},{1,17},{17,1},{2,18},{18,2},{3,19},{19,3},{4,20},{20... | collective-permute-start | bytes 25165832 | tf_op jit(solution)/shard_map/ppermute | solution.py:405
  97.7 16.2 %collective-permute-start.11 = (bf16[272,768]{1,0:T(8,128)(2,1)}, bf16[272,768]{1,0:T(8,128)(2,1)}, u32[]{:S(2)}, u32[]{:S(2)}) collective-permute-start(bf16[272,768]{1,0:T(8,128)(2,1)} %fusion.56), channel_id=1, source_target_pairs={{0,12},{1,13},{2,14},{3,15},{16,28},{17,29},{18,30},{19,31}} | collective-permute-start | bytes 1253384 | tf_op jit(solution)/shard_map/ppermute | solution.py:415
  101.2 14.3 %collective-permute-start.10 = (bf16[272,768]{1,0:T(8,128)(2,1)}, bf16[272,768]{1,0:T(8,128)(2,1)}, u32[]{:S(2)}, u32[]{:S(2)}) collective-permute-start(bf16[272,768]{1,0:T(8,128)(2,1)} %fusion.56), channel_id=1, source_target_pairs={{0,8},{4,12},{1,9},{5,13},{2,10},{6,14},{3,11},{7,15},{16,24},{20,... | collective-permute-start | bytes 1253384 | tf_op jit(solution)/shard_map/ppermute | solution.py:415
  103.9 27.2 %collective-permute-start.12 = (bf16[768,2048]{1,0:T(8,128)(2,1)S(1)}, bf16[768,2048]{1,0:T(8,128)(2,1)}, u32[]{:S(2)}, u32[]{:S(2)}) collective-permute-start(bf16[768,2048]{1,0:T(8,128)(2,1)S(1)} %bitcast.235), channel_id=1, source_target_pairs={{0,16},{16,0},{1,17},{17,1},{2,18},{18,2},{3,19},{19,3},{4,20},{20... | collective-permute-start | bytes 9437192 | tf_op jit(solution)/shard_map/ppermute | solution.py:405
  110.7 12.6 %collective-permute-start.9 = (bf16[272,768]{1,0:T(8,128)(2,1)}, bf16[272,768]{1,0:T(8,128)(2,1)S(1)}, u32[]{:S(2)}, u32[]{:S(2)}) collective-permute-start(bf16[272,768]{1,0:T(8,128)(2,1)} %fusion.56), channel_id=1, source_target_pairs={{0,4},{4,8},{8,12},{1,5},{5,9},{9,13},{2,6},{6,10},{10,14},{3,7},{... | collective-permute-start | bytes 1253384 | tf_op jit(solution)/shard_map/ppermute | solution.py:415
  113.8 16.1 %collective-permute-start.8 = (bf16[256,2048]{1,0:T(8,128)(2,1)}, bf16[256,2048]{1,0:T(8,128)(2,1)S(1)}, u32[]{:S(2)}, u32[]{:S(2)}) collective-permute-start(bf16[256,2048]{1,0:T(8,128)(2,1)} %bitcast.237), channel_id=1, source_target_pairs={{0,16},{16,0},{1,17},{17,1},{2,18},{18,2},{3,19},{19,3},{4,20},{20... | collective-permute-start | bytes 3145736 | tf_op jit(solution)/shard_map/ppermute | solution.py:405
  115.5 27.4 %collective-permute-start.15 = (bf16[1024,2048]{1,0:T(8,128)(2,1)}, bf16[1024,2048]{1,0:T(8,128)(2,1)}, u32[]{:S(2)}, u32[]{:S(2)}) collective-permute-start(bf16[1024,2048]{1,0:T(8,128)(2,1)} %bitcast.232), channel_id=1, source_target_pairs={{0,16},{16,0},{1,17},{17,1},{2,18},{18,2},{3,19},{19,3},{4,20},{20... | collective-permute-start | bytes 12582920 | tf_op jit(solution)/shard_map/ppermute | solution.py:405
  139.7 122.0 %all-reduce.11.cloned.1.call-start = ((), (), s32[]{:S(2)}) async-start(), calls=%async_computation.1 | async-start | bytes 2097152 | tf_op jit(solution)/shard_map/psum | solution.py:834
  210.4 178.6 %all-reduce.13.cloned.1.call-start = ((), (), s32[]{:S(2)}) async-start(), calls=%async_computation.2 | async-start | bytes 2097152 | tf_op jit(solution)/shard_map/psum | solution.py:572
  277.6 29.2 %collective-permute-start.20 = (bf16[256,256]{1,0:T(8,128)(2,1)}, bf16[256,256]{1,0:T(8,128)(2,1)}, u32[]{:S(2)}, u32[]{:S(2)}) collective-permute-start(bf16[256,256]{1,0:T(8,128)(2,1)} %pad_maximum_fusion.34), channel_id=1, source_target_pairs={{0,4},{4,8},{8,12},{1,5},{5,9},{9,13},{2,6},{6,10},{10,14},{3,7},{... | collective-permute-start | bytes 393224 | tf_op jit(solution)/shard_map/ppermute | solution.py:415
  281.7 24.1 %collective-permute-start.19 = (bf16[256,256]{1,0:T(8,128)(2,1)}, bf16[256,256]{1,0:T(8,128)(2,1)}, u32[]{:S(2)}, u32[]{:S(2)}) collective-permute-start(bf16[256,256]{1,0:T(8,128)(2,1)} %pad_maximum_fusion.34), channel_id=1, source_target_pairs={{0,8},{4,12},{1,9},{5,13},{2,10},{6,14},{3,11},{7,15},{16,24},{20,... | collective-permute-start | bytes 393224 | tf_op jit(solution)/shard_map/ppermute | solution.py:415
  285.1 19.8 %collective-permute-start.18 = (bf16[256,256]{1,0:T(8,128)(2,1)}, bf16[256,256]{1,0:T(8,128)(2,1)}, u32[]{:S(2)}, u32[]{:S(2)}) collective-permute-start(bf16[256,256]{1,0:T(8,128)(2,1)} %pad_maximum_fusion.34), channel_id=1, source_target_pairs={{0,12},{1,13},{2,14},{3,15},{16,28},{17,29},{18,30},{19,31}} | collective-permute-start | bytes 393224 | tf_op jit(solution)/shard_map/ppermute | solution.py:415
  307.9 11.3 %collective-permute-start.23 = (bf16[272,768]{1,0:T(8,128)(2,1)S(1)}, bf16[272,768]{1,0:T(8,128)(2,1)S(1)}, u32[]{:S(2)}, u32[]{:S(2)}) collective-permute-start(bf16[272,768]{1,0:T(8,128)(2,1)S(1)} %fusion.54), channel_id=1, source_target_pairs={{0,12},{1,13},{2,14},{3,15},{16,28},{17,29},{18,30},{19,31}} | collective-permute-start | bytes 1253384 | tf_op jit(solution)/shard_map/ppermute | solution.py:415
  309.2 19.0 %collective-permute-start.22 = (bf16[272,768]{1,0:T(8,128)(2,1)S(1)}, bf16[272,768]{1,0:T(8,128)(2,1)S(1)}, u32[]{:S(2)}, u32[]{:S(2)}) collective-permute-start(bf16[272,768]{1,0:T(8,128)(2,1)S(1)} %fusion.54), channel_id=1, source_target_pairs={{0,8},{4,12},{1,9},{5,13},{2,10},{6,14},{3,11},{7,15},{16,24},{20,... | collective-permute-start | bytes 1253384 | tf_op jit(solution)/shard_map/ppermute | solution.py:415
  310.6 17.6 %collective-permute-start.21 = (bf16[272,768]{1,0:T(8,128)(2,1)S(1)}, bf16[272,768]{1,0:T(8,128)(2,1)}, u32[]{:S(2)}, u32[]{:S(2)}) collective-permute-start(bf16[272,768]{1,0:T(8,128)(2,1)S(1)} %fusion.54), channel_id=1, source_target_pairs={{0,4},{4,8},{8,12},{1,5},{5,9},{9,13},{2,6},{6,10},{10,14},{3,7},{... | collective-permute-start | bytes 1253384 | tf_op jit(solution)/shard_map/ppermute | solution.py:415
  337.6 131.6 %all-reduce.15.cloned.1.call-start = ((), (), s32[]{:S(2)}) async-start(), calls=%async_computation.3 | async-start | bytes 2097152 | tf_op jit(solution)/shard_map/psum | solution.py:606
  360.6 258.6 %collective-permute-start.17 = (bf16[256,2048]{1,0:T(8,128)(2,1)S(1)}, bf16[256,2048]{1,0:T(8,128)(2,1)}, u32[]{:S(2)}, u32[]{:S(2)}) collective-permute-start(bf16[256,2048]{1,0:T(8,128)(2,1)S(1)} %get-tuple-element.147), channel_id=1, source_target_pairs={{16,0},{17,1},{18,2},{19,3},{20,4},{21,5},{22,6},{23,7},{24,8},{25... | collective-permute-start | bytes 3145736 | tf_op jit(solution)/shard_map/ppermute | solution.py:843
  417.5 125.2 %all-reduce.17.cloned.1.call-start = ((), (), s32[]{:S(2)}) async-start(), calls=%async_computation.4 | async-start | bytes 2097152 | tf_op jit(solution)/shard_map/psum | solution.py:489
  437.7 222.0 %collective-permute-start.58 = (bf16[16,7168]{1,0:T(8,128)(2,1)}, bf16[16,7168]{1,0:T(8,128)(2,1)}, u32[]{:S(2)}, u32[]{:S(2)}) collective-permute-start(bf16[16,7168]{1,0:T(8,128)(2,1)} %add_convert_fusion.8), channel_id=1, source_target_pairs={{0,16},{1,17},{2,18},{3,19},{4,20},{5,21},{6,22},{7,23},{8,24},{9,... | collective-permute-start | bytes 688136 | tf_op jit(solution)/shard_map/ppermute | solution.py:840
  483.6 18.9 %collective-permute-start.31 = (bf16[272,768]{1,0:T(8,128)(2,1)}, bf16[272,768]{1,0:T(8,128)(2,1)}, u32[]{:S(2)}, u32[]{:S(2)}) collective-permute-start(bf16[272,768]{1,0:T(8,128)(2,1)} %fusion.55), channel_id=1, source_target_pairs={{12,0},{13,1},{14,2},{15,3},{28,16},{29,17},{30,18},{31,19}} | collective-permute-start | bytes 1253384 | tf_op jit(solution)/shard_map/ppermute | solution.py:415
  484.9 22.2 %collective-permute-start.30 = (bf16[272,768]{1,0:T(8,128)(2,1)}, bf16[272,768]{1,0:T(8,128)(2,1)}, u32[]{:S(2)}, u32[]{:S(2)}) collective-permute-start(bf16[272,768]{1,0:T(8,128)(2,1)} %fusion.55), channel_id=1, source_target_pairs={{8,0},{12,4},{9,1},{13,5},{10,2},{14,6},{11,3},{15,7},{24,16},{28,... | collective-permute-start | bytes 1253384 | tf_op jit(solution)/shard_map/ppermute | solution.py:415
  486.2 20.9 %collective-permute-start.29 = (bf16[272,768]{1,0:T(8,128)(2,1)}, bf16[272,768]{1,0:T(8,128)(2,1)}, u32[]{:S(2)}, u32[]{:S(2)}) collective-permute-start(bf16[272,768]{1,0:T(8,128)(2,1)} %fusion.55), channel_id=1, source_target_pairs={{4,0},{8,4},{12,8},{5,1},{9,5},{13,9},{6,2},{10,6},{14,10},{7,3},{... | collective-permute-start | bytes 1253384 | tf_op jit(solution)/shard_map/ppermute | solution.py:415
  487.5 109.9 %all-reduce.19.cloned.1.call-start = ((), (), s32[]{:S(2)}) async-start(), calls=%async_computation.5 | async-start | bytes 2097152 | tf_op jit(solution)/shard_map/psum | solution.py:708
  507.9 22.7 %collective-permute-start.32 = (bf16[256,256]{1,0:T(8,128)(2,1)}, bf16[256,256]{1,0:T(8,128)(2,1)}, u32[]{:S(2)}, u32[]{:S(2)}) collective-permute-start(bf16[256,256]{1,0:T(8,128)(2,1)} %get-tuple-element.192), channel_id=1, source_target_pairs={{4,0},{8,4},{12,8},{5,1},{9,5},{13,9},{6,2},{10,6},{14,10},{7,3},{... | collective-permute-start | bytes 393224 | tf_op jit(solution)/shard_map/ppermute | solution.py:415
  509.2 21.4 %collective-permute-start.34 = (bf16[256,256]{1,0:T(8,128)(2,1)}, bf16[256,256]{1,0:T(8,128)(2,1)}, u32[]{:S(2)}, u32[]{:S(2)}) collective-permute-start(bf16[256,256]{1,0:T(8,128)(2,1)} %get-tuple-element.193), channel_id=1, source_target_pairs={{12,0},{13,1},{14,2},{15,3},{28,16},{29,17},{30,18},{31,19}} | collective-permute-start | bytes 393224 | tf_op jit(solution)/shard_map/ppermute | solution.py:415
  510.5 20.1 %collective-permute-start.33 = (bf16[256,256]{1,0:T(8,128)(2,1)}, bf16[256,256]{1,0:T(8,128)(2,1)}, u32[]{:S(2)}, u32[]{:S(2)}) collective-permute-start(bf16[256,256]{1,0:T(8,128)(2,1)} %get-tuple-element.194), channel_id=1, source_target_pairs={{8,0},{12,4},{9,1},{13,5},{10,2},{14,6},{11,3},{15,7},{24,16},{28,... | collective-permute-start | bytes 393224 | tf_op jit(solution)/shard_map/ppermute | solution.py:415
  546.0 129.1 %all-reduce.21.cloned.1.call-start = ((), (), s32[]{:S(2)}) async-start(), calls=%async_computation.6 | async-start | bytes 2097152 | tf_op jit(solution)/shard_map/psum | solution.py:606
  549.7 70.8 %collective-permute-start.28 = (bf16[256,2048]{1,0:T(8,128)(2,1)}, bf16[256,2048]{1,0:T(8,128)(2,1)}, u32[]{:S(2)}, u32[]{:S(2)}) collective-permute-start(bf16[256,2048]{1,0:T(8,128)(2,1)} %add_convert_fusion), channel_id=1, source_target_pairs={{0,16},{1,17},{2,18},{3,19},{4,20},{5,21},{6,22},{7,23},{8,24},{9,... | collective-permute-start | bytes 3145736 | tf_op jit(solution)/shard_map/ppermute | solution.py:840
  604.1 213.5 %collective-permute-start.46 = (bf16[256,2048]{1,0:T(8,128)(2,1)}, bf16[256,2048]{1,0:T(8,128)(2,1)}, u32[]{:S(2)}, u32[]{:S(2)}) collective-permute-start(bf16[256,2048]{1,0:T(8,128)(2,1)} %fusion.24), channel_id=1, source_target_pairs={{0,16},{1,17},{2,18},{3,19},{4,20},{5,21},{6,22},{7,23},{8,24},{9,... | collective-permute-start | bytes 3145736 | tf_op jit(solution)/shard_map/ppermute | solution.py:840
  607.3 25.5 %collective-permute-start.51 = (bf16[16,3120]{1,0:T(8,128)(2,1)S(1)}, bf16[16,3120]{1,0:T(8,128)(2,1)}, u32[]{:S(2)}, u32[]{:S(2)}) collective-permute-start(bf16[16,3120]{1,0:T(8,128)(2,1)S(1)} %pad_maximum_fusion.38), channel_id=1, source_target_pairs={{0,1},{1,0},{2,3},{3,2},{4,5},{5,4},{6,7},{7,6},{8,9},{9,8},{10,11... | collective-permute-start | bytes 299528 | tf_op jit(solution)/shard_map/ppermute | solution.py:422
  619.1 189.8 %all-reduce.23.cloned.1.call-start = ((), (), s32[]{:S(2)}) async-start(), calls=%async_computation.7 | async-start | bytes 2097152 | tf_op jit(solution)/shard_map/psum | solution.py:708
  633.7 11.5 %collective-permute-start.52 = (bf16[16,3120]{1,0:T(8,128)(2,1)S(1)}, bf16[16,3120]{1,0:T(8,128)(2,1)S(1)}, u32[]{:S(2)}, u32[]{:S(2)}) collective-permute-start(bf16[16,3120]{1,0:T(8,128)(2,1)S(1)} %add_convert_fusion.11), channel_id=1, source_target_pairs={{0,2},{1,3},{2,0},{3,1},{4,6},{5,7},{6,4},{7,5},{8,10},{9,11},{10,... | collective-permute-start | bytes 299528 | tf_op jit(solution)/shard_map/ppermute | solution.py:422
  633.8 13.0 %collective-permute-start.37 = (bf16[16,7168]{1,0:T(8,128)(2,1)S(1)}, bf16[16,7168]{1,0:T(8,128)(2,1)S(1)}, u32[]{:S(2)}, u32[]{:S(2)}) collective-permute-start(bf16[16,7168]{1,0:T(8,128)(2,1)S(1)} %pad_maximum_fusion.26), channel_id=1, source_target_pairs={{0,4},{4,0},{8,12},{12,8},{1,5},{5,1},{9,13},{13,9},{2,6},{6,2},{1... | collective-permute-start | bytes 688136 | tf_op jit(solution)/shard_map/ppermute | solution.py:422
  652.4 106.2 %collective-permute-start.54 = (bf16[16,7984]{1,0:T(8,128)(2,1)}, bf16[16,7984]{1,0:T(8,128)(2,1)}, u32[]{:S(2)}, u32[]{:S(2)}) collective-permute-start(bf16[16,7984]{1,0:T(8,128)(2,1)} %add_convert_fusion.3), channel_id=1, source_target_pairs={{0,8},{4,12},{8,0},{12,4},{1,9},{5,13},{9,1},{13,5},{2,10},{6,14},... | collective-permute-start | bytes 766472 | tf_op jit(solution)/shard_map/ppermute | solution.py:422
  686.6 15.4 %collective-permute-start.41 = (bf16[272,768]{1,0:T(8,128)(2,1)S(1)}, bf16[272,768]{1,0:T(8,128)(2,1)S(1)}, u32[]{:S(2)}, u32[]{:S(2)}) collective-permute-start(bf16[272,768]{1,0:T(8,128)(2,1)S(1)} %fusion.57), channel_id=1, source_target_pairs={{12,0},{13,1},{14,2},{15,3},{28,16},{29,17},{30,18},{31,19}} | collective-permute-start | bytes 1253384 | tf_op jit(solution)/shard_map/ppermute | solution.py:415
  687.9 21.9 %collective-permute-start.40 = (bf16[272,768]{1,0:T(8,128)(2,1)S(1)}, bf16[272,768]{1,0:T(8,128)(2,1)S(1)}, u32[]{:S(2)}, u32[]{:S(2)}) collective-permute-start(bf16[272,768]{1,0:T(8,128)(2,1)S(1)} %fusion.57), channel_id=1, source_target_pairs={{8,0},{12,4},{9,1},{13,5},{10,2},{14,6},{11,3},{15,7},{24,16},{28,... | collective-permute-start | bytes 1253384 | tf_op jit(solution)/shard_map/ppermute | solution.py:415
  689.2 20.6 %collective-permute-start.39 = (bf16[272,768]{1,0:T(8,128)(2,1)S(1)}, bf16[272,768]{1,0:T(8,128)(2,1)S(1)}, u32[]{:S(2)}, u32[]{:S(2)}) collective-permute-start(bf16[272,768]{1,0:T(8,128)(2,1)S(1)} %fusion.57), channel_id=1, source_target_pairs={{4,0},{8,4},{12,8},{5,1},{9,5},{13,9},{6,2},{10,6},{14,10},{7,3},{... | collective-permute-start | bytes 1253384 | tf_op jit(solution)/shard_map/ppermute | solution.py:415
  710.6 20.4 %collective-permute-start.42 = (bf16[256,256]{1,0:T(8,128)(2,1)}, bf16[256,256]{1,0:T(8,128)(2,1)S(1)}, u32[]{:S(2)}, u32[]{:S(2)}) collective-permute-start(bf16[256,256]{1,0:T(8,128)(2,1)} %get-tuple-element.189), channel_id=1, source_target_pairs={{4,0},{8,4},{12,8},{5,1},{9,5},{13,9},{6,2},{10,6},{14,10},{7,3},{... | collective-permute-start | bytes 393224 | tf_op jit(solution)/shard_map/ppermute | solution.py:415
  711.9 19.1 %collective-permute-start.44 = (bf16[256,256]{1,0:T(8,128)(2,1)S(1)}, bf16[256,256]{1,0:T(8,128)(2,1)}, u32[]{:S(2)}, u32[]{:S(2)}) collective-permute-start(bf16[256,256]{1,0:T(8,128)(2,1)S(1)} %get-tuple-element.190), channel_id=1, source_target_pairs={{12,0},{13,1},{14,2},{15,3},{28,16},{29,17},{30,18},{31,19}} | collective-permute-start | bytes 393224 | tf_op jit(solution)/shard_map/ppermute | solution.py:415
  713.2 17.8 %collective-permute-start.43 = (bf16[256,256]{1,0:T(8,128)(2,1)S(1)}, bf16[256,256]{1,0:T(8,128)(2,1)}, u32[]{:S(2)}, u32[]{:S(2)}) collective-permute-start(bf16[256,256]{1,0:T(8,128)(2,1)S(1)} %get-tuple-element.191), channel_id=1, source_target_pairs={{8,0},{12,4},{9,1},{13,5},{10,2},{14,6},{11,3},{15,7},{24,16},{28,... | collective-permute-start | bytes 393224 | tf_op jit(solution)/shard_map/ppermute | solution.py:415
  (221 other events, 3014.7 us)
Sparse Core Ops, SparseCore 0:
  139.8 54.3 all-reduce.8
  210.5 51.1 all-reduce.10
  337.7 51.2 all-reduce.12
  417.6 51.5 all-reduce.14
  487.6 54.9 all-reduce.16
  546.1 51.2 all-reduce.18
  619.2 55.7 all-reduce.20
  758.8 50.1 all-reduce.22

commit v5 on v4

--- a/solution.py
+++ b/solution.py
@@ -417,6 +417,12 @@
 
 def exchange_sum(value, axis):
     count = lax.axis_size(axis)
+    if count == 4:
+        parts = [value.astype(F32)]
+        for step in range(1, count):
+            pairs = [(place, place ^ step) for place in range(count)]
+            parts.append(lax.ppermute(value, axis, pairs).astype(F32))
+        return ((parts[0] + parts[1]) + (parts[2] + parts[3])).astype(value.dtype)
     bit = 1
     while bit < count:
         moved = lax.ppermute(value, axis, [(place, place ^ bit) for place in range(count)])

time: 837 us -> 835 us (level)
  waiting for transfers between devices: 279 us -> 253 us
  starting transfers between devices: 90.9 us -> 107 us
    ppermute x16 -> x24, starting transfers between devices: 22.7 us -> 37.4 us  [exchange_sum(): parts.append(lax.ppermute(value, axis, pairs).astype(F32))]
    psum x2, waiting for transfers between devices: 80.4 us -> 66 us  [mixer_backward(): summed = lax.psum(norm_part, 'wt')]
    ppermute x16 -> x24, waiting for transfers between devices: 40.1 us -> 26.2 us  [exchange_sum(): parts.append(lax.ppermute(value, axis, pairs).astype(F32))]
    unnamed x408 -> x418, local copies, waits for them, and re-layouts: 41.9 us -> 42.2 us
  transfers between devices with their start and end apart: 67 -> 75, of which waited for: 29 -> 24; matrix products, arithmetic and copies ran while one was open for 38% -> 39% of each run, Pallas kernels for 6% -> 6%
where the time goes in v5:
time: 835 us; the launch traced here: 825 us
  waiting for transfers between devices  253 us (30%)
  other arithmetic  166 us (20%)
  matrix products  136 us (16%)
  starting transfers between devices  107 us (13%)
  local copies, waits for them, and re-layouts  87.9 us (11%)
  Pallas kernels  53.9 us (6%)
  between operations  21.8 us (3%)
    psum x2, waiting for transfers between devices, mixer_backward(): summed = lax.psum(norm_part, 'wt')  66 us
    dot_general x36, matrix products, mm(): return jnp.dot(a.astype(BF), b.astype(BF), preferred_element_type=F32)  58.2 us
    dot_general x36, matrix products, mm_t(): lax.dot_general(a.astype(BF), b.astype(BF), (((1,), (1,)), ((), ())), pre...  54.2 us
    select_n x7, other arithmetic, shards(): value = jnp.where(section == index, own[name], moved[name])  50.1 us
    ppermute x24, starting transfers between devices, shifted(): lax.ppermute(value, 'ctx', [(source, source + steps) for source in range(...  49.4 us
    psum x1, waiting for transfers between devices, shards(): fed = after(lax.psum(feed_part, 'wt'), *following)  43.7 us
    unnamed x418, local copies, waits for them, and re-layouts  42.2 us
    psum x2, waiting for transfers between devices, feed_forward(): mixed = after(lax.psum(part, 'wt'), w.gateup, w.down)  41.8 us
  transfers between devices with their start and end apart: 75, of which 24 were waited for; matrix products, arithmetic and copies ran while one was open for 39% of the time, Pallas kernels for 6%

profile of v5, /device:TPU:0, one launch (start us, length us, event | category | flops | bytes accessed | tf_op | source)
XLA Modules:
  0.0 825.1 jit_solution(7173769153182176346)
XLA Ops:
  39.4 6.3 broadcast_select_fusion.4
  49.6 5.1 collective-permute-start.5
  71.5 13.1 %broadcast_select_fusion.2 = (bf16[2048,2,768]{2,1,0:T(2,128)(2,1)}, bf16[2048,2,768]{2,1,0:T(2,128)(2,1)S(1)}) fusion(bf16[2048,2,768]{2,1,0:T(2,128)(2,1)} %collective-permute-done.2, pred[]{:T(512)S(6)} %eq.23, bf16[1,2048,2,768]{3,2,1,0:T(2,128)(2,1)} %param.37, pred[]{:T(512)S(6)} %eq.22), kind=kLoop, calls=%fused_computation.2 | loop fusion | flops 6291456 | bytes 25165826 | tf_op jit(solution)/shard_map/jit(_where)/select_n | solution.py:828
  90.1 4.3 shard_map.354
  96.2 3.5 collective-permute-start.11
  114.6 7.3 collective-permute-done.9.refs_0_
  122.6 3.9 shard_map.356
  129.7 4.4 broadcast_select_fusion.8
  141.4 5.9 broadcast_select_fusion.6
  147.3 16.7 %broadcast_select_fusion = (bf16[2048,2,1024]{2,1,0:T(2,128)(2,1)}, bf16[2048,2,1024]{2,1,0:T(2,128)(2,1)}) fusion(bf16[2048,2,1024]{2,1,0:T(2,128)(2,1)} %collective-permute-done.14, pred[]{:T(512)S(6)} %eq.23, bf16[1,2048,2,1024]{3,2,1,0:T(2,128)(2,1)} %param.41, pred[]{:T(512)S(6)} %eq.22), kind=kLoop, calls=%fused_computation | loop fusion | flops 8388608 | bytes 33554432 | tf_op jit(solution)/shard_map/jit(_where)/select_n | solution.py:828
  164.0 10.2 %copy.85 = bf16[256,8,2,1024]{3,1,2,0:T(8,128)(2,1)} copy(bf16[256,8,2,1024]{3,2,1,0:T(2,128)(2,1)} %bitcast.216) | data formatting | bytes 16777216
  174.2 18.6 %all-reduce.9.cloned.1.call-done = bf16[256,2048]{1,0:T(8,128)(2,1)} async-done(((bf16[256,2048]{1,0:T(8,128)(2,1)}), bf16[256,2048]{1,0:T(8,128)(2,1)}) %all-reduce.9.cloned.1.call-update) | async-done | bytes 1048592 | tf_op jit(solution)/shard_map/psum | solution.py:578
  195.9 6.1 fusion.287
  210.0 6.7 copy.86
  216.7 43.7 %all-reduce.11.cloned.1.call-done = bf16[256,2048]{1,0:T(8,128)(2,1)} async-done(((bf16[256,2048]{1,0:T(8,128)(2,1)}), bf16[256,2048]{1,0:T(8,128)(2,1)}) %all-reduce.11.cloned.1.call-update) | async-done | bytes 1048592 | tf_op jit(solution)/shard_map/psum | solution.py:840
  264.9 4.6 fusion.282
  276.2 4.1 collective-permute-start.20
  280.4 3.4 collective-permute-start.19
  285.7 6.0 fusion.288
  298.0 4.3 shard_map.357
  314.0 3.5 shard_map.358
  317.8 9.0 %collective-permute-done.22.refs_1_ = bf16[272,768]{1,0:T(8,128)(2,1)S(1)} collective-permute-done((bf16[272,768]{1,0:T(8,128)(2,1)S(1)}, bf16[272,768]{1,0:T(8,128)(2,1)S(1)}, u32[]{:S(2)}, u32[]{:S(2)}) %collective-permute-start.22) | collective-permute-done | bytes 417824 | tf_op jit(solution)/shard_map/ppermute | solution.py:415
  327.5 3.9 shard_map.359
  349.0 10.3 %copy.87 = bf16[256,8,2,1024]{3,1,2,0:T(8,128)(2,1)} copy(bf16[256,8,2,1024]{3,2,1,0:T(2,128)(2,1)} %bitcast.215) | data formatting | bytes 16777216
  364.4 23.2 %all-reduce.13.cloned.1.call-done = bf16[256,2048]{1,0:T(8,128)(2,1)} async-done(((bf16[256,2048]{1,0:T(8,128)(2,1)}), bf16[256,2048]{1,0:T(8,128)(2,1)}) %all-reduce.13.cloned.1.call-update) | async-done | bytes 1048592 | tf_op jit(solution)/shard_map/psum | solution.py:578
  391.6 5.9 fusion.290
  424.9 4.5 fusion.11
  438.9 28.2 %all-reduce.15.cloned.1.call-done = bf16[256,2048]{1,0:T(8,128)(2,1)} async-done(((bf16[256,2048]{1,0:T(8,128)(2,1)}), bf16[256,2048]{1,0:T(8,128)(2,1)}) %all-reduce.15.cloned.1.call-update) | async-done | bytes 1048592 | tf_op jit(solution)/shard_map/psum | solution.py:612
  469.7 3.8 multiply_convert_fusion.1
  494.9 3.8 shard_map.361
  500.4 4.6 collective-permute-done.32.refs_1_
  509.9 8.6 %shard_map.362 = (bf16[256,768]{1,0:T(8,128)(2,1)}, bf16[256,256]{1,0:T(8,128)(2,1)}, bf16[256,256]{1,0:T(8,128)(2,1)}, f32[256,12]{1,0:T(8,128)}) custom-call(f32[256,768]{1,0:T(8,128)} %get-tuple-element.176.x_ref, bf16[256,768]{1,0:T(8,128)(2,1)} %copy-done.48, f32[256,768]{1,0:T(8,128)} %get-tuple-element.105.z_ref, ...), custom_call_target="tpu_custom_call" | custom-call | tf_op jit(solution)/shard_map/pallas_call | solution.py:269
  518.5 6.3 fusion.65
  531.6 4.0 fusion.273
  537.2 3.4 all-reduce.17.cloned.1.call-done
  550.7 44.6 %all-reduce.19.cloned.1.call-done = bf16[256,2048]{1,0:T(8,128)(2,1)} async-done(((bf16[256,2048]{1,0:T(8,128)(2,1)}), bf16[256,2048]{1,0:T(8,128)(2,1)}) %all-reduce.19.cloned.1.call-update) | async-done | bytes 1048592 | tf_op jit(solution)/shard_map/psum | solution.py:714
  606.4 5.7 fusion.58
  618.7 3.7 maximum_select_fusion
  630.0 7.6 collective-permute-done.58
  641.9 3.9 collective-permute-done.40
  661.4 10.9 %all-reduce.21.cloned.1.call-done = bf16[256,2048]{1,0:T(8,128)(2,1)} async-done(((bf16[256,2048]{1,0:T(8,128)(2,1)}), bf16[256,2048]{1,0:T(8,128)(2,1)}) %all-reduce.21.cloned.1.call-update) | async-done | bytes 1048592 | tf_op jit(solution)/shard_map/psum | solution.py:612
  692.8 3.8 shard_map.364
  697.9 7.9 collective-permute-done.44.refs_1_
  710.7 8.5 %shard_map.365 = (bf16[256,768]{1,0:T(8,128)(2,1)}, bf16[256,256]{1,0:T(8,128)(2,1)}, bf16[256,256]{1,0:T(8,128)(2,1)}, f32[256,12]{1,0:T(8,128)}) custom-call(f32[256,768]{1,0:T(8,128)} %get-tuple-element.175.x_ref, bf16[256,768]{1,0:T(8,128)(2,1)} %copy-done.49, f32[256,768]{1,0:T(8,128)} %get-tuple-element.123.z_ref, ...), custom_call_target="tpu_custom_call" | custom-call | tf_op jit(solution)/shard_map/pallas_call | solution.py:269
  719.2 6.2 fusion.63
  729.3 3.8 fusion.272
  742.5 5.3 collective-permute-start.62
  785.2 21.4 %all-reduce.23.cloned.1.call-done = bf16[256,2048]{1,0:T(8,128)(2,1)} async-done(((bf16[256,2048]{1,0:T(8,128)(2,1)}), bf16[256,2048]{1,0:T(8,128)(2,1)}) %all-reduce.23.cloned.1.call-update) | async-done | bytes 1048592 | tf_op jit(solution)/shard_map/psum | solution.py:714
  (812 shorter events, 369.1 us)
Async XLA Ops:
  7.2 185.6 %all-reduce.9.cloned.1.call-start = ((), (), s32[]{:S(2)}) async-start(), calls=%async_computation | async-start | bytes 2097152 | tf_op jit(solution)/shard_map/psum | solution.py:578
  9.6 22.2 %collective-permute-start = (f32[4132]{0:T(1024)S(1)}, f32[4132]{0:T(1024)S(1)}, u32[]{:S(2)}, u32[]{:S(2)}) collective-permute-start(f32[4132]{0:T(1024)S(1)} %concatenate.146), channel_id=1, source_target_pairs={{0,16},{16,0},{1,17},{17,1},{2,18},{18,2},{3,19},{19,3},{4,20},{20... | collective-permute-start | bytes 49592 | tf_op jit(solution)/shard_map/ppermute | solution.py:405
  17.6 16.6 %collective-permute-start.1 = (bf16[16,4912]{1,0:T(8,128)(2,1)}, bf16[16,4912]{1,0:T(8,128)(2,1)}, u32[]{:S(2)}, u32[]{:S(2)}) collective-permute-start(bf16[16,4912]{1,0:T(8,128)(2,1)} %dynamic-slice_bitcast_fusion.1), channel_id=1, source_target_pairs={{0,16},{16,0},{1,17},{17,1},{2,18},{18,2},{3,19},{19,3},{4,20},{20... | collective-permute-start | bytes 471560 | tf_op jit(solution)/shard_map/ppermute | solution.py:405
  17.6 19.1 %collective-permute-start.7 = (bf16[2048,256]{1,0:T(8,128)(2,1)}, bf16[2048,256]{1,0:T(8,128)(2,1)}, u32[]{:S(2)}, u32[]{:S(2)}) collective-permute-start(bf16[2048,256]{1,0:T(8,128)(2,1)} %bitcast.237), channel_id=1, source_target_pairs={{0,16},{16,0},{1,17},{17,1},{2,18},{18,2},{3,19},{19,3},{4,20},{20... | collective-permute-start | bytes 3145736 | tf_op jit(solution)/shard_map/ppermute | solution.py:405
  18.1 21.4 %collective-permute-start.3 = (bf16[2048,1072]{0,1:T(8,128)(2,1)}, bf16[2048,1072]{0,1:T(8,128)(2,1)}, u32[]{:S(2)}, u32[]{:S(2)}) collective-permute-start(bf16[2048,1072]{0,1:T(8,128)(2,1)} %bitcast.231), channel_id=1, source_target_pairs={{0,16},{16,0},{1,17},{17,1},{2,18},{18,2},{3,19},{19,3},{4,20},{20... | collective-permute-start | bytes 13172744 | tf_op jit(solution)/shard_map/ppermute | solution.py:405
  18.1 53.3 %collective-permute-start.2 = (bf16[2048,2,768]{2,1,0:T(2,128)(2,1)}, bf16[2048,2,768]{2,1,0:T(2,128)(2,1)}, u32[]{:S(2)}, u32[]{:S(2)}) collective-permute-start(bf16[2048,2,768]{2,1,0:T(2,128)(2,1)} %bitcast.230), channel_id=1, source_target_pairs={{0,16},{16,0},{1,17},{17,1},{2,18},{18,2},{3,19},{19,3},{4,20},{20... | collective-permute-start | bytes 18874376 | tf_op jit(solution)/shard_map/ppermute | solution.py:405
  49.6 18.6 %collective-permute-start.5 = (bf16[256,256]{1,0:T(8,128)(2,1)}, bf16[256,256]{1,0:T(8,128)(2,1)}, u32[]{:S(2)}, u32[]{:S(2)}) collective-permute-start(bf16[256,256]{1,0:T(8,128)(2,1)} %pad_maximum_fusion.33), channel_id=1, source_target_pairs={{0,8},{4,12},{1,9},{5,13},{2,10},{6,14},{3,11},{7,15},{16,24},{20,... | collective-permute-start | bytes 393224 | tf_op jit(solution)/shard_map/ppermute | solution.py:415
  90.1 57.2 %collective-permute-start.14 = (bf16[2048,2,1024]{2,1,0:T(2,128)(2,1)}, bf16[2048,2,1024]{2,1,0:T(2,128)(2,1)}, u32[]{:S(2)}, u32[]{:S(2)}) collective-permute-start(bf16[2048,2,1024]{2,1,0:T(2,128)(2,1)} %bitcast.28), channel_id=1, source_target_pairs={{0,16},{16,0},{1,17},{17,1},{2,18},{18,2},{3,19},{19,3},{4,20},{20... | collective-permute-start | bytes 25165832 | tf_op jit(solution)/shard_map/ppermute | solution.py:405
  96.2 16.2 %collective-permute-start.11 = (bf16[272,768]{1,0:T(8,128)(2,1)}, bf16[272,768]{1,0:T(8,128)(2,1)}, u32[]{:S(2)}, u32[]{:S(2)}) collective-permute-start(bf16[272,768]{1,0:T(8,128)(2,1)} %fusion.56), channel_id=1, source_target_pairs={{0,12},{1,13},{2,14},{3,15},{16,28},{17,29},{18,30},{19,31}} | collective-permute-start | bytes 1253384 | tf_op jit(solution)/shard_map/ppermute | solution.py:415
  99.7 14.3 %collective-permute-start.10 = (bf16[272,768]{1,0:T(8,128)(2,1)}, bf16[272,768]{1,0:T(8,128)(2,1)}, u32[]{:S(2)}, u32[]{:S(2)}) collective-permute-start(bf16[272,768]{1,0:T(8,128)(2,1)} %fusion.56), channel_id=1, source_target_pairs={{0,8},{4,12},{1,9},{5,13},{2,10},{6,14},{3,11},{7,15},{16,24},{20,... | collective-permute-start | bytes 1253384 | tf_op jit(solution)/shard_map/ppermute | solution.py:415
  102.5 27.2 %collective-permute-start.12 = (bf16[768,2048]{1,0:T(8,128)(2,1)S(1)}, bf16[768,2048]{1,0:T(8,128)(2,1)}, u32[]{:S(2)}, u32[]{:S(2)}) collective-permute-start(bf16[768,2048]{1,0:T(8,128)(2,1)S(1)} %bitcast.236), channel_id=1, source_target_pairs={{0,16},{16,0},{1,17},{17,1},{2,18},{18,2},{3,19},{19,3},{4,20},{20... | collective-permute-start | bytes 9437192 | tf_op jit(solution)/shard_map/ppermute | solution.py:405
  112.4 16.1 %collective-permute-start.8 = (bf16[256,2048]{1,0:T(8,128)(2,1)}, bf16[256,2048]{1,0:T(8,128)(2,1)S(1)}, u32[]{:S(2)}, u32[]{:S(2)}) collective-permute-start(bf16[256,2048]{1,0:T(8,128)(2,1)} %bitcast.238), channel_id=1, source_target_pairs={{0,16},{16,0},{1,17},{17,1},{2,18},{18,2},{3,19},{19,3},{4,20},{20... | collective-permute-start | bytes 3145736 | tf_op jit(solution)/shard_map/ppermute | solution.py:405
  114.1 27.4 %collective-permute-start.15 = (bf16[1024,2048]{1,0:T(8,128)(2,1)}, bf16[1024,2048]{1,0:T(8,128)(2,1)}, u32[]{:S(2)}, u32[]{:S(2)}) collective-permute-start(bf16[1024,2048]{1,0:T(8,128)(2,1)} %bitcast.233), channel_id=1, source_target_pairs={{0,16},{16,0},{1,17},{17,1},{2,18},{18,2},{3,19},{19,3},{4,20},{20... | collective-permute-start | bytes 12582920 | tf_op jit(solution)/shard_map/ppermute | solution.py:405
  138.3 122.0 %all-reduce.11.cloned.1.call-start = ((), (), s32[]{:S(2)}) async-start(), calls=%async_computation.1 | async-start | bytes 2097152 | tf_op jit(solution)/shard_map/psum | solution.py:840
  209.0 178.6 %all-reduce.13.cloned.1.call-start = ((), (), s32[]{:S(2)}) async-start(), calls=%async_computation.2 | async-start | bytes 2097152 | tf_op jit(solution)/shard_map/psum | solution.py:578
  276.2 29.1 %collective-permute-start.20 = (bf16[256,256]{1,0:T(8,128)(2,1)}, bf16[256,256]{1,0:T(8,128)(2,1)}, u32[]{:S(2)}, u32[]{:S(2)}) collective-permute-start(bf16[256,256]{1,0:T(8,128)(2,1)} %pad_maximum_fusion.34), channel_id=1, source_target_pairs={{0,4},{4,8},{8,12},{1,5},{5,9},{9,13},{2,6},{6,10},{10,14},{3,7},{... | collective-permute-start | bytes 393224 | tf_op jit(solution)/shard_map/ppermute | solution.py:415
  280.4 24.1 %collective-permute-start.19 = (bf16[256,256]{1,0:T(8,128)(2,1)}, bf16[256,256]{1,0:T(8,128)(2,1)}, u32[]{:S(2)}, u32[]{:S(2)}) collective-permute-start(bf16[256,256]{1,0:T(8,128)(2,1)} %pad_maximum_fusion.34), channel_id=1, source_target_pairs={{0,8},{4,12},{1,9},{5,13},{2,10},{6,14},{3,11},{7,15},{16,24},{20,... | collective-permute-start | bytes 393224 | tf_op jit(solution)/shard_map/ppermute | solution.py:415
  283.8 19.7 %collective-permute-start.18 = (bf16[256,256]{1,0:T(8,128)(2,1)}, bf16[256,256]{1,0:T(8,128)(2,1)}, u32[]{:S(2)}, u32[]{:S(2)}) collective-permute-start(bf16[256,256]{1,0:T(8,128)(2,1)} %pad_maximum_fusion.34), channel_id=1, source_target_pairs={{0,12},{1,13},{2,14},{3,15},{16,28},{17,29},{18,30},{19,31}} | collective-permute-start | bytes 393224 | tf_op jit(solution)/shard_map/ppermute | solution.py:415
  307.8 19.0 %collective-permute-start.22 = (bf16[272,768]{1,0:T(8,128)(2,1)S(1)}, bf16[272,768]{1,0:T(8,128)(2,1)S(1)}, u32[]{:S(2)}, u32[]{:S(2)}) collective-permute-start(bf16[272,768]{1,0:T(8,128)(2,1)S(1)} %fusion.54), channel_id=1, source_target_pairs={{0,8},{4,12},{1,9},{5,13},{2,10},{6,14},{3,11},{7,15},{16,24},{20,... | collective-permute-start | bytes 1253384 | tf_op jit(solution)/shard_map/ppermute | solution.py:415
  309.1 17.6 %collective-permute-start.21 = (bf16[272,768]{1,0:T(8,128)(2,1)S(1)}, bf16[272,768]{1,0:T(8,128)(2,1)}, u32[]{:S(2)}, u32[]{:S(2)}) collective-permute-start(bf16[272,768]{1,0:T(8,128)(2,1)S(1)} %fusion.54), channel_id=1, source_target_pairs={{0,4},{4,8},{8,12},{1,5},{5,9},{9,13},{2,6},{6,10},{10,14},{3,7},{... | collective-permute-start | bytes 1253384 | tf_op jit(solution)/shard_map/ppermute | solution.py:415
  336.2 131.0 %all-reduce.15.cloned.1.call-start = ((), (), s32[]{:S(2)}) async-start(), calls=%async_computation.3 | async-start | bytes 2097152 | tf_op jit(solution)/shard_map/psum | solution.py:612
  359.3 255.5 %collective-permute-start.17 = (bf16[256,2048]{1,0:T(8,128)(2,1)S(1)}, bf16[256,2048]{1,0:T(8,128)(2,1)}, u32[]{:S(2)}, u32[]{:S(2)}) collective-permute-start(bf16[256,2048]{1,0:T(8,128)(2,1)S(1)} %get-tuple-element.147), channel_id=1, source_target_pairs={{16,0},{17,1},{18,2},{19,3},{20,4},{21,5},{22,6},{23,7},{24,8},{25... | collective-permute-start | bytes 3145736 | tf_op jit(solution)/shard_map/ppermute | solution.py:849
  415.8 124.7 %all-reduce.17.cloned.1.call-start = ((), (), s32[]{:S(2)}) async-start(), calls=%async_computation.4 | async-start | bytes 2097152 | tf_op jit(solution)/shard_map/psum | solution.py:495
  436.2 216.0 %collective-permute-start.66 = (bf16[16,7168]{1,0:T(8,128)(2,1)}, bf16[16,7168]{1,0:T(8,128)(2,1)}, u32[]{:S(2)}, u32[]{:S(2)}) collective-permute-start(bf16[16,7168]{1,0:T(8,128)(2,1)} %add_convert_fusion.5), channel_id=1, source_target_pairs={{0,16},{1,17},{2,18},{3,19},{4,20},{5,21},{6,22},{7,23},{8,24},{9,... | collective-permute-start | bytes 688136 | tf_op jit(solution)/shard_map/ppermute | solution.py:846
  481.5 18.9 %collective-permute-start.33 = (bf16[272,768]{1,0:T(8,128)(2,1)}, bf16[272,768]{1,0:T(8,128)(2,1)}, u32[]{:S(2)}, u32[]{:S(2)}) collective-permute-start(bf16[272,768]{1,0:T(8,128)(2,1)} %fusion.55), channel_id=1, source_target_pairs={{12,0},{13,1},{14,2},{15,3},{28,16},{29,17},{30,18},{31,19}} | collective-permute-start | bytes 1253384 | tf_op jit(solution)/shard_map/ppermute | solution.py:415
  482.8 22.2 %collective-permute-start.32 = (bf16[272,768]{1,0:T(8,128)(2,1)}, bf16[272,768]{1,0:T(8,128)(2,1)}, u32[]{:S(2)}, u32[]{:S(2)}) collective-permute-start(bf16[272,768]{1,0:T(8,128)(2,1)} %fusion.55), channel_id=1, source_target_pairs={{8,0},{12,4},{9,1},{13,5},{10,2},{14,6},{11,3},{15,7},{24,16},{28,... | collective-permute-start | bytes 1253384 | tf_op jit(solution)/shard_map/ppermute | solution.py:415
  484.1 20.9 %collective-permute-start.31 = (bf16[272,768]{1,0:T(8,128)(2,1)}, bf16[272,768]{1,0:T(8,128)(2,1)}, u32[]{:S(2)}, u32[]{:S(2)}) collective-permute-start(bf16[272,768]{1,0:T(8,128)(2,1)} %fusion.55), channel_id=1, source_target_pairs={{4,0},{8,4},{12,8},{5,1},{9,5},{13,9},{6,2},{10,6},{14,10},{7,3},{... | collective-permute-start | bytes 1253384 | tf_op jit(solution)/shard_map/ppermute | solution.py:415
  485.4 109.9 %all-reduce.19.cloned.1.call-start = ((), (), s32[]{:S(2)}) async-start(), calls=%async_computation.5 | async-start | bytes 2097152 | tf_op jit(solution)/shard_map/psum | solution.py:714
  505.8 22.7 %collective-permute-start.34 = (bf16[256,256]{1,0:T(8,128)(2,1)}, bf16[256,256]{1,0:T(8,128)(2,1)}, u32[]{:S(2)}, u32[]{:S(2)}) collective-permute-start(bf16[256,256]{1,0:T(8,128)(2,1)} %get-tuple-element.192), channel_id=1, source_target_pairs={{4,0},{8,4},{12,8},{5,1},{9,5},{13,9},{6,2},{10,6},{14,10},{7,3},{... | collective-permute-start | bytes 393224 | tf_op jit(solution)/shard_map/ppermute | solution.py:415
  507.1 21.5 %collective-permute-start.36 = (bf16[256,256]{1,0:T(8,128)(2,1)}, bf16[256,256]{1,0:T(8,128)(2,1)}, u32[]{:S(2)}, u32[]{:S(2)}) collective-permute-start(bf16[256,256]{1,0:T(8,128)(2,1)} %get-tuple-element.193), channel_id=1, source_target_pairs={{12,0},{13,1},{14,2},{15,3},{28,16},{29,17},{30,18},{31,19}} | collective-permute-start | bytes 393224 | tf_op jit(solution)/shard_map/ppermute | solution.py:415
  508.4 20.2 %collective-permute-start.35 = (bf16[256,256]{1,0:T(8,128)(2,1)}, bf16[256,256]{1,0:T(8,128)(2,1)}, u32[]{:S(2)}, u32[]{:S(2)}) collective-permute-start(bf16[256,256]{1,0:T(8,128)(2,1)} %get-tuple-element.194), channel_id=1, source_target_pairs={{8,0},{12,4},{9,1},{13,5},{10,2},{14,6},{11,3},{15,7},{24,16},{28,... | collective-permute-start | bytes 393224 | tf_op jit(solution)/shard_map/ppermute | solution.py:415
  543.8 128.4 %all-reduce.21.cloned.1.call-start = ((), (), s32[]{:S(2)}) async-start(), calls=%async_computation.6 | async-start | bytes 2097152 | tf_op jit(solution)/shard_map/psum | solution.py:612
  547.6 69.4 %collective-permute-start.30 = (bf16[256,2048]{1,0:T(8,128)(2,1)}, bf16[256,2048]{1,0:T(8,128)(2,1)}, u32[]{:S(2)}, u32[]{:S(2)}) collective-permute-start(bf16[256,2048]{1,0:T(8,128)(2,1)} %add_convert_fusion), channel_id=1, source_target_pairs={{0,16},{1,17},{2,18},{3,19},{4,20},{5,21},{6,22},{7,23},{8,24},{9,... | collective-permute-start | bytes 3145736 | tf_op jit(solution)/shard_map/ppermute | solution.py:846
  604.1 18.6 %collective-permute-start.38 = (bf16[256,48]{0,1:T(8,128)(2,1)}, bf16[256,48]{0,1:T(8,128)(2,1)}, u32[]{:S(2)}, u32[]{:S(2)}) collective-permute-start(bf16[256,48]{0,1:T(8,128)(2,1)} %pad_maximum_fusion.40), channel_id=1, source_target_pairs={{0,2},{1,3},{2,0},{3,1},{4,6},{5,7},{6,4},{7,5},{8,10},{9,11},{10,... | collective-permute-start | bytes 73736 | tf_op jit(solution)/shard_map/ppermute | solution.py:424
  605.8 17.2 %collective-permute-start.37 = (bf16[256,48]{0,1:T(8,128)(2,1)}, bf16[256,48]{0,1:T(8,128)(2,1)}, u32[]{:S(2)}, u32[]{:S(2)}) collective-permute-start(bf16[256,48]{0,1:T(8,128)(2,1)} %pad_maximum_fusion.40), channel_id=1, source_target_pairs={{0,1},{1,0},{2,3},{3,2},{4,5},{5,4},{6,7},{7,6},{8,9},{9,8},{10,11... | collective-permute-start | bytes 73736 | tf_op jit(solution)/shard_map/ppermute | solution.py:424
  613.6 192.9 %all-reduce.23.cloned.1.call-start = ((), (), s32[]{:S(2)}) async-start(), calls=%async_computation.7 | async-start | bytes 2097152 | tf_op jit(solution)/shard_map/psum | solution.py:714
  622.7 14.9 %collective-permute-start.58 = (bf16[16,3120]{1,0:T(8,128)(2,1)S(1)}, bf16[16,3120]{1,0:T(8,128)(2,1)S(1)}, u32[]{:S(2)}, u32[]{:S(2)}) collective-permute-start(bf16[16,3120]{1,0:T(8,128)(2,1)S(1)} %pad_maximum_fusion.38), channel_id=1, source_target_pairs={{0,2},{1,3},{2,0},{3,1},{4,6},{5,7},{6,4},{7,5},{8,10},{9,11},{10,... | collective-permute-start | bytes 299528 | tf_op jit(solution)/shard_map/ppermute | solution.py:424
  623.0 16.1 %collective-permute-start.57 = (bf16[16,3120]{1,0:T(8,128)(2,1)S(1)}, bf16[16,3120]{1,0:T(8,128)(2,1)S(1)}, u32[]{:S(2)}, u32[]{:S(2)}) collective-permute-start(bf16[16,3120]{1,0:T(8,128)(2,1)S(1)} %pad_maximum_fusion.38), channel_id=1, source_target_pairs={{0,1},{1,0},{2,3},{3,2},{4,5},{5,4},{6,7},{7,6},{8,9},{9,8},{10,11... | collective-permute-start | bytes 299528 | tf_op jit(solution)/shard_map/ppermute | solution.py:424
  627.0 14.3 %collective-permute-start.42 = (bf16[16,7168]{1,0:T(8,128)(2,1)S(1)}, bf16[16,7168]{1,0:T(8,128)(2,1)S(1)}, u32[]{:S(2)}, u32[]{:S(2)}) collective-permute-start(bf16[16,7168]{1,0:T(8,128)(2,1)S(1)} %pad_maximum_fusion.26), channel_id=1, source_target_pairs={{0,12},{4,8},{8,4},{12,0},{1,13},{5,9},{9,5},{13,1},{2,14},{6,10},... | collective-permute-start | bytes 688136 | tf_op jit(solution)/shard_map/ppermute | solution.py:424
  639.9 113.0 %collective-permute-start.61 = (bf16[16,7984]{1,0:T(8,128)(2,1)}, bf16[16,7984]{1,0:T(8,128)(2,1)}, u32[]{:S(2)}, u32[]{:S(2)}) collective-permute-start(bf16[16,7984]{1,0:T(8,128)(2,1)} %pad_maximum_fusion.24), channel_id=1, source_target_pairs={{0,8},{4,12},{8,0},{12,4},{1,9},{5,13},{9,1},{13,5},{2,10},{6,14},... | collective-permute-start | bytes 766472 | tf_op jit(solution)/shard_map/ppermute | solution.py:424
  641.3 113.1 %collective-permute-start.60 = (bf16[16,7984]{1,0:T(8,128)(2,1)}, bf16[16,7984]{1,0:T(8,128)(2,1)}, u32[]{:S(2)}, u32[]{:S(2)}) collective-permute-start(bf16[16,7984]{1,0:T(8,128)(2,1)} %pad_maximum_fusion.24), channel_id=1, source_target_pairs={{0,4},{4,0},{8,12},{12,8},{1,5},{5,1},{9,13},{13,9},{2,6},{6,2},{1... | collective-permute-start | bytes 766472 | tf_op jit(solution)/shard_map/ppermute | solution.py:424
  682.5 15.4 %collective-permute-start.45 = (bf16[272,768]{1,0:T(8,128)(2,1)S(1)}, bf16[272,768]{1,0:T(8,128)(2,1)S(1)}, u32[]{:S(2)}, u32[]{:S(2)}) collective-permute-start(bf16[272,768]{1,0:T(8,128)(2,1)S(1)} %fusion.57), channel_id=1, source_target_pairs={{12,0},{13,1},{14,2},{15,3},{28,16},{29,17},{30,18},{31,19}} | collective-permute-start | bytes 1253384 | tf_op jit(solution)/shard_map/ppermute | solution.py:415
  683.8 21.9 %collective-permute-start.44 = (bf16[272,768]{1,0:T(8,128)(2,1)S(1)}, bf16[272,768]{1,0:T(8,128)(2,1)S(1)}, u32[]{:S(2)}, u32[]{:S(2)}) collective-permute-start(bf16[272,768]{1,0:T(8,128)(2,1)S(1)} %fusion.57), channel_id=1, source_target_pairs={{8,0},{12,4},{9,1},{13,5},{10,2},{14,6},{11,3},{15,7},{24,16},{28,... | collective-permute-start | bytes 1253384 | tf_op jit(solution)/shard_map/ppermute | solution.py:415
  685.1 20.6 %collective-permute-start.43 = (bf16[272,768]{1,0:T(8,128)(2,1)S(1)}, bf16[272,768]{1,0:T(8,128)(2,1)S(1)}, u32[]{:S(2)}, u32[]{:S(2)}) collective-permute-start(bf16[272,768]{1,0:T(8,128)(2,1)S(1)} %fusion.57), channel_id=1, source_target_pairs={{4,0},{8,4},{12,8},{5,1},{9,5},{13,9},{6,2},{10,6},{14,10},{7,3},{... | collective-permute-start | bytes 1253384 | tf_op jit(solution)/shard_map/ppermute | solution.py:415
  706.6 20.8 %collective-permute-start.46 = (bf16[256,256]{1,0:T(8,128)(2,1)}, bf16[256,256]{1,0:T(8,128)(2,1)}, u32[]{:S(2)}, u32[]{:S(2)}) collective-permute-start(bf16[256,256]{1,0:T(8,128)(2,1)} %get-tuple-element.189), channel_id=1, source_target_pairs={{4,0},{8,4},{12,8},{5,1},{9,5},{13,9},{6,2},{10,6},{14,10},{7,3},{... | collective-permute-start | bytes 393224 | tf_op jit(solution)/shard_map/ppermute | solution.py:415
  707.8 19.6 %collective-permute-start.48 = (bf16[256,256]{1,0:T(8,128)(2,1)}, bf16[256,256]{1,0:T(8,128)(2,1)}, u32[]{:S(2)}, u32[]{:S(2)}) collective-permute-start(bf16[256,256]{1,0:T(8,128)(2,1)} %get-tuple-element.190), channel_id=1, source_target_pairs={{12,0},{13,1},{14,2},{15,3},{28,16},{29,17},{30,18},{31,19}} | collective-permute-start | bytes 393224 | tf_op jit(solution)/shard_map/ppermute | solution.py:415
  709.1 18.3 %collective-permute-start.47 = (bf16[256,256]{1,0:T(8,128)(2,1)S(1)}, bf16[256,256]{1,0:T(8,128)(2,1)}, u32[]{:S(2)}, u32[]{:S(2)}) collective-permute-start(bf16[256,256]{1,0:T(8,128)(2,1)S(1)} %get-tuple-element.191), channel_id=1, source_target_pairs={{8,0},{12,4},{9,1},{13,5},{10,2},{14,6},{11,3},{15,7},{24,16},{28,... | collective-permute-start | bytes 393224 | tf_op jit(solution)/shard_map/ppermute | solution.py:415
  754.5 60.7 %collective-permute-start.50 = (bf16[256,2048]{1,0:T(8,128)(2,1)S(1)}, bf16[256,2048]{1,0:T(8,128)(2,1)}, u32[]{:S(2)}, u32[]{:S(2)}) collective-permute-start(bf16[256,2048]{1,0:T(8,128)(2,1)S(1)} %copy-done.6), channel_id=1, source_target_pairs={{0,16},{1,17},{2,18},{3,19},{4,20},{5,21},{6,22},{7,23},{8,24},{9,... | collective-permute-start | bytes 3145736 | tf_op jit(solution)/shard_map/ppermute | solution.py:846
  (234 other events, 3356.6 us)
Sparse Core Ops, SparseCore 0:
  138.5 54.3 all-reduce.8
  209.1 51.1 all-reduce.10
  336.3 51.2 all-reduce.12
  415.9 51.1 all-reduce.14
  485.5 54.9 all-reduce.16
  543.9 51.2 all-reduce.18
  613.7 58.5 all-reduce.20
  754.6 51.9 all-reduce.22
